TPU v7x, 32 devices: a whole 2x2x4 slice. The times are simulated.
32 devices in a mesh: grp: 4 (over y, x), slab: 8 (over z, core).
Axes of the slice: x: 2, y: 2, z: 4, core: 2. Of those that a mesh axis runs over, the one named last changes fastest.
Arguments:
- grain_ids: int32 [2097152], P(('grp', 'slab')), may hold values from 0 to 16383, as said below
- orientation: float32 [4, 2097152], P(None, ('grp', 'slab')), may hold values from -2 to 2, as said below
- stress: float32 [9, 2097152], P(None, ('grp', 'slab')), may hold values from -8 to 8
- owner_blocks: int32 [256], replicated, may hold values from 0 to 255, each once
Outputs:
- grain_table: float32 [13, 16384], P(None, ('grp', 'slab'))
- fluctuation: bfloat16 [13, 2097152], P(None, ('grp', 'slab'))
Inputs may be any that keep to these rules, and one draw needn't show every extreme that they name: `grain_ids`: the grain of point x is floor(x / 128) - 1, floor(x / 128) or floor(x / 128) + 1, and both outer cases occur in every draw; ids never fall from one point to the next, and every grain has 16 points or more. `orientation`: the first component of every quaternion is 0.4 or more.
All inputs are finite; a program needn't handle non-finite values.
Results may differ from a plain program's by a relative error of at most 0.012.
The roundings to bfloat16 on the way count: a program that leaves them out, or rounds other values in their place, can miss the bound.
Values may be sent and summed in bfloat16 or wider, within the bound.
No kernel may reach another device: no remote copies, remote signals or barrier semaphores. Data moves between devices by JAX's collectives and lax.ppermute only.
A program may use at most 64 MiB of HBM per device.

v0:
```python
import jax
import jax.numpy as jnp
from jax import lax
from jax.sharding import PartitionSpec as P

BLK = 64
BLOCK_PTS = 8192
GD = 512
WIN = 640
BLK_DEV = 8


def from_behind(value, axis, steps):
    count = lax.axis_size(axis)
    first, last = (max(0, -steps), min(count, count - steps))
    return lax.ppermute(value, axis, [(source, source + steps) for source in range(first, last)])


def finish(totals):
    counts = totals[0:1]
    quat_sum = totals[1:5]
    stress_sum = totals[5:14]
    mean_quat = quat_sum / jnp.sqrt(jnp.sum(quat_sum * quat_sum, axis=0, keepdims=True))
    mean_stress = stress_sum / counts
    return jnp.concatenate([mean_quat, mean_stress], axis=0)


def local(grain_ids, orientation, stress, owner_blocks):
    device_index = lax.axis_index(("grp", "slab"))
    points = grain_ids.shape[0]
    block_total = owner_blocks.shape[0]
    values = jnp.concatenate(
        [
            jnp.ones((1, points), jnp.float32),
            orientation,
            stress,
            jnp.zeros((2, points), jnp.float32),
        ],
        axis=0,
    )
    unit_quat = orientation / jnp.sqrt(jnp.sum(orientation * orientation, axis=0, keepdims=True))
    point_local = jnp.concatenate([unit_quat, stress], axis=0)
    window_base = device_index * GD - BLK
    block_count = points // BLOCK_PTS
    window_width = WIN

    def indicator(block_ids):
        columns = window_base + lax.iota(jnp.int32, window_width)
        return block_ids[:, None] == columns[None, :]

    def add_block(block_step, totals):
        first_point = (block_step * BLOCK_PTS).astype(jnp.int32)
        block_ids = lax.dynamic_slice_in_dim(grain_ids, first_point, BLOCK_PTS)
        block_values = lax.dynamic_slice_in_dim(values, first_point, BLOCK_PTS, 1)
        selector = indicator(block_ids).astype(jnp.float32)
        block_sums = jnp.dot(
            block_values,
            selector,
            precision=lax.Precision.HIGHEST,
            preferred_element_type=jnp.float32,
        )
        return totals + block_sums

    totals = lax.fori_loop(0, block_count, add_block, jnp.zeros((16, WIN), jnp.float32))
    lower_rim = totals[:, :BLK]
    upper_rim = totals[:, BLK + GD :]
    from_above = from_behind(lower_rim, ("grp", "slab"), -1)
    from_below = from_behind(upper_rim, ("grp", "slab"), 1)
    owned_sums = totals[:, BLK : BLK + GD]
    owned_sums = owned_sums.at[:, :BLK].add(from_below)
    owned_sums = owned_sums.at[:, GD - BLK :].add(from_above)
    finished = finish(owned_sums)
    rounded = finished.astype(jnp.bfloat16)
    left_edge = from_behind(rounded[:, GD - BLK :], ("grp", "slab"), 1)
    right_edge = from_behind(rounded[:, :BLK], ("grp", "slab"), -1)
    lookup_table = jnp.concatenate([left_edge, rounded, right_edge], axis=1)
    gathered = lax.all_gather(finished, ("grp", "slab"), axis=1, tiled=True)
    my_blocks = lax.dynamic_slice_in_dim(owner_blocks, device_index * BLK_DEV, BLK_DEV)
    grain_table = jnp.take(gathered.reshape(13, block_total, BLK), my_blocks, axis=1).reshape(
        13, GD
    )

    def look_block(block_step, fluctuation):
        first_point = (block_step * BLOCK_PTS).astype(jnp.int32)
        block_ids = lax.dynamic_slice_in_dim(grain_ids, first_point, BLOCK_PTS)
        selector = indicator(block_ids).astype(jnp.bfloat16)
        grain_means = jnp.einsum(
            "cw,pw->cp", lookup_table, selector, preferred_element_type=jnp.float32
        )
        point_part = lax.dynamic_slice_in_dim(point_local, first_point, BLOCK_PTS, 1)
        return lax.dynamic_update_slice_in_dim(
            fluctuation, (point_part - grain_means).astype(jnp.bfloat16), first_point, 1
        )

    fluctuation = lax.fori_loop(0, block_count, look_block, jnp.zeros((13, points), jnp.bfloat16))
    return (grain_table, fluctuation)


def solution(mesh):
    placed = (P(("grp", "slab")), P(None, ("grp", "slab")), P(None, ("grp", "slab")), P())
    return jax.shard_map(
        local,
        mesh=mesh,
        in_specs=placed,
        out_specs=(P(None, ("grp", "slab")), P(None, ("grp", "slab"))),
        check_vma=False,
    )
```

profile of v0, /device:TPU:4, one launch (start us, length us, event | category | flops | bytes accessed | tf_op | source)
XLA Modules:
  0.0 192.0 jit_solution(18427413634858542837)
XLA Ops:
  0.7 5.5 %maximum_maximum_fusion = f32[16,65536]{1,0:T(8,128)} fusion(f32[9,65536]{1,0:T(8,128)} %param.14, f32[4,65536]{1,0:T(4,128)} %param.13, f32[16]{0:T(128)S(1)} %pad.14.clone, f32[16]{0:T(128)S(1)} %pad.11.clone), kind=kLoop, calls=%fused_computation.18 | loop fusion | flops 3145728 | bytes 7602304 | tf_op jit(solution)/shard_map/concatenate | solution.py:32
  6.3 62.9 %while.30 = (s32[]{:T(128)}, f32[16,640]{1,0:T(8,128)S(1)}, f32[16,65536]{1,0:T(8,128)}, s32[65536]{0:T(1024)}, s32[]{:T(128)}, /*index=5*/s32[]{:T(128)}, s32[]{:T(128)}, s32[]{:T(128)}, s32[]{:T(128)}) while((s32[]{:T(128)}, f32[16,640]{1,0:T(8,128)S(1)}, f32[16,65536]{1,0:T(8,128)}, s32[65536]{0:T(1024)}, s32[]{:T(128)}, ...), condition=%wide.region_1.0_spmd.clone, body=%wide.region_0.0_spmd.clone.sunk | while | flops 1011896960 | bytes 709801 | solution.py:64
  7.1 7.1 %fusion.40 = f32[16,640]{1,0:T(8,128)S(1)} fusion(s32[640]{0:T(1024)S(1)} %iota_add_fusion.5, s32[8192]{0:T(1024)S(1)} %dynamic_slice.46, f32[16,65536]{1,0:T(8,128)} %get-tuple-element.367, s32[]{:T(128)S(6)} %select_n.40, f32[16,640]{1,0:T(8,128)S(1)} %get-tuple-element.357, pred[]{:T(512)S(6)} %compare.17), kind=kOutput, calls=%fused_computation.14.clone.1 | convolution fusion | flops 1011896320 | bytes 641541 | tf_op jit(solution)/shard_map/while/body/eval_jaxpr/dot_general | solution.py:56
  15.0 7.1 %fusion.40 = f32[16,640]{1,0:T(8,128)S(1)} fusion(s32[640]{0:T(1024)S(1)} %iota_add_fusion.5, s32[8192]{0:T(1024)S(1)} %dynamic_slice.46, f32[16,65536]{1,0:T(8,128)} %get-tuple-element.367, s32[]{:T(128)S(6)} %select_n.40, f32[16,640]{1,0:T(8,128)S(1)} %get-tuple-element.357, pred[]{:T(512)S(6)} %compare.17), kind=kOutput, calls=%fused_computation.14.clone.1 | convolution fusion | flops 1011896320 | bytes 641541 | tf_op jit(solution)/shard_map/while/body/eval_jaxpr/dot_general | solution.py:56
  22.8 7.1 %fusion.40 = f32[16,640]{1,0:T(8,128)S(1)} fusion(s32[640]{0:T(1024)S(1)} %iota_add_fusion.5, s32[8192]{0:T(1024)S(1)} %dynamic_slice.46, f32[16,65536]{1,0:T(8,128)} %get-tuple-element.367, s32[]{:T(128)S(6)} %select_n.40, f32[16,640]{1,0:T(8,128)S(1)} %get-tuple-element.357, pred[]{:T(512)S(6)} %compare.17), kind=kOutput, calls=%fused_computation.14.clone.1 | convolution fusion | flops 1011896320 | bytes 641541 | tf_op jit(solution)/shard_map/while/body/eval_jaxpr/dot_general | solution.py:56
  30.7 7.1 %fusion.40 = f32[16,640]{1,0:T(8,128)S(1)} fusion(s32[640]{0:T(1024)S(1)} %iota_add_fusion.5, s32[8192]{0:T(1024)S(1)} %dynamic_slice.46, f32[16,65536]{1,0:T(8,128)} %get-tuple-element.367, s32[]{:T(128)S(6)} %select_n.40, f32[16,640]{1,0:T(8,128)S(1)} %get-tuple-element.357, pred[]{:T(512)S(6)} %compare.17), kind=kOutput, calls=%fused_computation.14.clone.1 | convolution fusion | flops 1011896320 | bytes 641541 | tf_op jit(solution)/shard_map/while/body/eval_jaxpr/dot_general | solution.py:56
  38.5 7.1 %fusion.40 = f32[16,640]{1,0:T(8,128)S(1)} fusion(s32[640]{0:T(1024)S(1)} %iota_add_fusion.5, s32[8192]{0:T(1024)S(1)} %dynamic_slice.46, f32[16,65536]{1,0:T(8,128)} %get-tuple-element.367, s32[]{:T(128)S(6)} %select_n.40, f32[16,640]{1,0:T(8,128)S(1)} %get-tuple-element.357, pred[]{:T(512)S(6)} %compare.17), kind=kOutput, calls=%fused_computation.14.clone.1 | convolution fusion | flops 1011896320 | bytes 641541 | tf_op jit(solution)/shard_map/while/body/eval_jaxpr/dot_general | solution.py:56
  46.4 7.1 %fusion.40 = f32[16,640]{1,0:T(8,128)S(1)} fusion(s32[640]{0:T(1024)S(1)} %iota_add_fusion.5, s32[8192]{0:T(1024)S(1)} %dynamic_slice.46, f32[16,65536]{1,0:T(8,128)} %get-tuple-element.367, s32[]{:T(128)S(6)} %select_n.40, f32[16,640]{1,0:T(8,128)S(1)} %get-tuple-element.357, pred[]{:T(512)S(6)} %compare.17), kind=kOutput, calls=%fused_computation.14.clone.1 | convolution fusion | flops 1011896320 | bytes 641541 | tf_op jit(solution)/shard_map/while/body/eval_jaxpr/dot_general | solution.py:56
  54.2 7.1 %fusion.40 = f32[16,640]{1,0:T(8,128)S(1)} fusion(s32[640]{0:T(1024)S(1)} %iota_add_fusion.5, s32[8192]{0:T(1024)S(1)} %dynamic_slice.46, f32[16,65536]{1,0:T(8,128)} %get-tuple-element.367, s32[]{:T(128)S(6)} %select_n.40, f32[16,640]{1,0:T(8,128)S(1)} %get-tuple-element.357, pred[]{:T(512)S(6)} %compare.17), kind=kOutput, calls=%fused_computation.14.clone.1 | convolution fusion | flops 1011896320 | bytes 641541 | tf_op jit(solution)/shard_map/while/body/eval_jaxpr/dot_general | solution.py:56
  62.1 7.1 %fusion.40 = f32[16,640]{1,0:T(8,128)S(1)} fusion(s32[640]{0:T(1024)S(1)} %iota_add_fusion.5, s32[8192]{0:T(1024)S(1)} %dynamic_slice.46, f32[16,65536]{1,0:T(8,128)} %get-tuple-element.367, s32[]{:T(128)S(6)} %select_n.40, f32[16,640]{1,0:T(8,128)S(1)} %get-tuple-element.357, pred[]{:T(512)S(6)} %compare.17), kind=kOutput, calls=%fused_computation.14.clone.1 | convolution fusion | flops 1011896320 | bytes 641541 | tf_op jit(solution)/shard_map/while/body/eval_jaxpr/dot_general | solution.py:56
  72.3 4.7 %pad_maximum_fusion = f32[13,65536]{1,0:T(8,128)} fusion(f32[9,65536]{1,0:T(8,128)} %param.14, f32[4,65536]{1,0:T(4,128)S(1)} %broadcast_divide_fusion), kind=kLoop, calls=%fused_computation.19 | loop fusion | flops 851968 | bytes 6815744 | tf_op jit(solution)/shard_map/concatenate | solution.py:42
  78.5 7.2 %collective-permute-start.1 = (f32[16,64]{1,0:T(8,128)S(1)}, f32[16,64]{1,0:T(8,128)S(1)}, u32[]{:S(2)}, u32[]{:S(2)}) collective-permute-start(f32[16,64]{1,0:T(8,128)S(1)} %get-tuple-element.275), channel_id=1, source_target_pairs={{1,0},{2,1},{3,2},{4,3},{5,4},{6,5},{7,6},{8,7},{9,8},{10,9},{11,1... | collective-permute-start | bytes 12296 | tf_op jit(solution)/shard_map/ppermute | solution.py:16
  87.4 42.4 %all_gather.3 = f32[13,16384]{1,0:T(8,128)S(1)} all-gather(f32[13,512]{1,0:T(8,128)S(1)} %get-tuple-element.272), channel_id=1, replica_groups=mesh['grp'=4,'slab'=8] {'grp','slab'}, dimensions={1}, use_global_device_ids=true | all-gather | bytes 878592 | tf_op jit(solution)/shard_map/all_gather | solution.py:77
  135.2 2.4 %collective-permute-start.3 = (bf16[13,64]{1,0:T(8,128)(2,1)S(1)}, bf16[13,64]{1,0:T(8,128)(2,1)S(1)}, u32[]{:S(2)}, u32[]{:S(2)}) collective-permute-start(bf16[13,64]{1,0:T(8,128)(2,1)S(1)} %get-tuple-element.278), channel_id=1, source_target_pairs={{1,0},{2,1},{3,2},{4,3},{5,4},{6,5},{7,6},{8,7},{9,8},{10,9},{11,1... | collective-permute-start | bytes 5000 | tf_op jit(solution)/shard_map/ppermute | solution.py:16
  140.1 6.0 %collective-permute-done.2 = bf16[13,64]{1,0:T(8,128)(2,1)S(1)} collective-permute-done((bf16[13,64]{1,0:T(8,128)(2,1)S(1)}, bf16[13,64]{1,0:T(8,128)(2,1)S(1)}, u32[]{:S(2)}, u32[]{:S(2)}) %collective-permute-start.2) | collective-permute-done | bytes 1696 | tf_op jit(solution)/shard_map/ppermute | solution.py:16
  146.3 44.4 %while.29 = (s32[]{:T(128)}, bf16[13,65536]{1,0:T(8,128)(2,1)S(1)}, f32[13,65536]{1,0:T(8,128)}, s32[65536]{0:T(1024)}, s32[]{:T(128)}, /*index=5*/bf16[13,640]{...) while((s32[]{:T(128)}, bf16[13,65536]{1,0:T(8,128)(2,1)S(1)}, f32[13,65536]{1,0:T(8,128)}, ...), condition=%wide.region_6.7_spmd, body=%wide.region_5.0_spmd.sunk | while | flops 141771392 | bytes 813735 | solution.py:95
  147.1 4.8 %fusion.37 = bf16[13,65536]{1,0:T(8,128)(2,1)S(1)} fusion(bf16[13,65536]{1,0:T(8,128)(2,1)S(1)} %get-tuple-element.385, s32[]{:T(128)S(6)} %select_n.39, bf16[13,640]{1,0:T(8,128)(2,1)S(1)} %get-tuple-element.399, s32[640]{0:T(1024)S(1)} %iota_add_fusion.4, s32[8192]{0:T(1024)S(1)} %dynamic_slice.44, f32[13,65536]{1,0:T(8,128)} %get-tuple-element.396), kind=kOutput, calls=%fused_computation.8.clone.1 | convolution fusion | flops 141770752 | bytes 745476 | tf_op jit(solution)/shard_map/while/body/eval_jaxpr/cw,pw->cp/dot_general | solution.py:87
  152.7 4.8 %fusion.37 = bf16[13,65536]{1,0:T(8,128)(2,1)S(1)} fusion(bf16[13,65536]{1,0:T(8,128)(2,1)S(1)} %get-tuple-element.385, s32[]{:T(128)S(6)} %select_n.39, bf16[13,640]{1,0:T(8,128)(2,1)S(1)} %get-tuple-element.399, s32[640]{0:T(1024)S(1)} %iota_add_fusion.4, s32[8192]{0:T(1024)S(1)} %dynamic_slice.44, f32[13,65536]{1,0:T(8,128)} %get-tuple-element.396), kind=kOutput, calls=%fused_computation.8.clone.1 | convolution fusion | flops 141770752 | bytes 745476 | tf_op jit(solution)/shard_map/while/body/eval_jaxpr/cw,pw->cp/dot_general | solution.py:87
  158.2 4.8 %fusion.37 = bf16[13,65536]{1,0:T(8,128)(2,1)S(1)} fusion(bf16[13,65536]{1,0:T(8,128)(2,1)S(1)} %get-tuple-element.385, s32[]{:T(128)S(6)} %select_n.39, bf16[13,640]{1,0:T(8,128)(2,1)S(1)} %get-tuple-element.399, s32[640]{0:T(1024)S(1)} %iota_add_fusion.4, s32[8192]{0:T(1024)S(1)} %dynamic_slice.44, f32[13,65536]{1,0:T(8,128)} %get-tuple-element.396), kind=kOutput, calls=%fused_computation.8.clone.1 | convolution fusion | flops 141770752 | bytes 745476 | tf_op jit(solution)/shard_map/while/body/eval_jaxpr/cw,pw->cp/dot_general | solution.py:87
  163.7 4.8 %fusion.37 = bf16[13,65536]{1,0:T(8,128)(2,1)S(1)} fusion(bf16[13,65536]{1,0:T(8,128)(2,1)S(1)} %get-tuple-element.385, s32[]{:T(128)S(6)} %select_n.39, bf16[13,640]{1,0:T(8,128)(2,1)S(1)} %get-tuple-element.399, s32[640]{0:T(1024)S(1)} %iota_add_fusion.4, s32[8192]{0:T(1024)S(1)} %dynamic_slice.44, f32[13,65536]{1,0:T(8,128)} %get-tuple-element.396), kind=kOutput, calls=%fused_computation.8.clone.1 | convolution fusion | flops 141770752 | bytes 745476 | tf_op jit(solution)/shard_map/while/body/eval_jaxpr/cw,pw->cp/dot_general | solution.py:87
  169.3 4.8 %fusion.37 = bf16[13,65536]{1,0:T(8,128)(2,1)S(1)} fusion(bf16[13,65536]{1,0:T(8,128)(2,1)S(1)} %get-tuple-element.385, s32[]{:T(128)S(6)} %select_n.39, bf16[13,640]{1,0:T(8,128)(2,1)S(1)} %get-tuple-element.399, s32[640]{0:T(1024)S(1)} %iota_add_fusion.4, s32[8192]{0:T(1024)S(1)} %dynamic_slice.44, f32[13,65536]{1,0:T(8,128)} %get-tuple-element.396), kind=kOutput, calls=%fused_computation.8.clone.1 | convolution fusion | flops 141770752 | bytes 745476 | tf_op jit(solution)/shard_map/while/body/eval_jaxpr/cw,pw->cp/dot_general | solution.py:87
  174.8 4.8 %fusion.37 = bf16[13,65536]{1,0:T(8,128)(2,1)S(1)} fusion(bf16[13,65536]{1,0:T(8,128)(2,1)S(1)} %get-tuple-element.385, s32[]{:T(128)S(6)} %select_n.39, bf16[13,640]{1,0:T(8,128)(2,1)S(1)} %get-tuple-element.399, s32[640]{0:T(1024)S(1)} %iota_add_fusion.4, s32[8192]{0:T(1024)S(1)} %dynamic_slice.44, f32[13,65536]{1,0:T(8,128)} %get-tuple-element.396), kind=kOutput, calls=%fused_computation.8.clone.1 | convolution fusion | flops 141770752 | bytes 745476 | tf_op jit(solution)/shard_map/while/body/eval_jaxpr/cw,pw->cp/dot_general | solution.py:87
  180.4 4.8 %fusion.37 = bf16[13,65536]{1,0:T(8,128)(2,1)S(1)} fusion(bf16[13,65536]{1,0:T(8,128)(2,1)S(1)} %get-tuple-element.385, s32[]{:T(128)S(6)} %select_n.39, bf16[13,640]{1,0:T(8,128)(2,1)S(1)} %get-tuple-element.399, s32[640]{0:T(1024)S(1)} %iota_add_fusion.4, s32[8192]{0:T(1024)S(1)} %dynamic_slice.44, f32[13,65536]{1,0:T(8,128)} %get-tuple-element.396), kind=kOutput, calls=%fused_computation.8.clone.1 | convolution fusion | flops 141770752 | bytes 745476 | tf_op jit(solution)/shard_map/while/body/eval_jaxpr/cw,pw->cp/dot_general | solution.py:87
  185.9 4.8 %fusion.37 = bf16[13,65536]{1,0:T(8,128)(2,1)S(1)} fusion(bf16[13,65536]{1,0:T(8,128)(2,1)S(1)} %get-tuple-element.385, s32[]{:T(128)S(6)} %select_n.39, bf16[13,640]{1,0:T(8,128)(2,1)S(1)} %get-tuple-element.399, s32[640]{0:T(1024)S(1)} %iota_add_fusion.4, s32[8192]{0:T(1024)S(1)} %dynamic_slice.44, f32[13,65536]{1,0:T(8,128)} %get-tuple-element.396), kind=kOutput, calls=%fused_computation.8.clone.1 | convolution fusion | flops 141770752 | bytes 745476 | tf_op jit(solution)/shard_map/while/body/eval_jaxpr/cw,pw->cp/dot_general | solution.py:87
  (76 shorter events, 28.1 us)
Async XLA Ops:
  6.3 64.9 %copy-start = (f32[4,65536]{1,0:T(4,128)S(1)}, f32[4,65536]{1,0:T(4,128)}, u32[]{:S(2)}) copy-start(f32[4,65536]{1,0:T(4,128)} %param.13) | copy-start | bytes 3145732
  69.2 8.6 %collective-permute-start = (f32[16,64]{1,0:T(8,128)S(1)}, f32[16,64]{1,0:T(8,128)S(1)}, u32[]{:S(2)}, u32[]{:S(2)}) collective-permute-start(f32[16,64]{1,0:T(8,128)S(1)} %slice.65), channel_id=1, source_target_pairs={{0,1},{1,2},{2,3},{3,4},{4,5},{5,6},{6,7},{7,8},{8,9},{9,10},{10,1... | collective-permute-start | bytes 12296 | tf_op jit(solution)/shard_map/ppermute | solution.py:16
  72.3 4.7 %copy-start.2 = (s32[256]{0:T(256)S(1)}, s32[256]{0:T(256)}, u32[]{:S(2)}) copy-start(s32[256]{0:T(256)} %param.15) | copy-start | bytes 3076
  78.5 8.5 %collective-permute-start.1 = (f32[16,64]{1,0:T(8,128)S(1)}, f32[16,64]{1,0:T(8,128)S(1)}, u32[]{:S(2)}, u32[]{:S(2)}) collective-permute-start(f32[16,64]{1,0:T(8,128)S(1)} %get-tuple-element.275), channel_id=1, source_target_pairs={{1,0},{2,1},{3,2},{4,3},{5,4},{6,5},{7,6},{8,7},{9,8},{10,9},{11,1... | collective-permute-start | bytes 12296 | tf_op jit(solution)/shard_map/ppermute | solution.py:16
  135.2 5.0 %collective-permute-start.3 = (bf16[13,64]{1,0:T(8,128)(2,1)S(1)}, bf16[13,64]{1,0:T(8,128)(2,1)S(1)}, u32[]{:S(2)}, u32[]{:S(2)}) collective-permute-start(bf16[13,64]{1,0:T(8,128)(2,1)S(1)} %get-tuple-element.278), channel_id=1, source_target_pairs={{1,0},{2,1},{3,2},{4,3},{5,4},{6,5},{7,6},{8,7},{9,8},{10,9},{11,1... | collective-permute-start | bytes 5000 | tf_op jit(solution)/shard_map/ppermute | solution.py:16
  137.6 8.5 %collective-permute-start.2 = (bf16[13,64]{1,0:T(8,128)(2,1)S(1)}, bf16[13,64]{1,0:T(8,128)(2,1)S(1)}, u32[]{:S(2)}, u32[]{:S(2)}) collective-permute-start(bf16[13,64]{1,0:T(8,128)(2,1)S(1)} %get-tuple-element.277), channel_id=1, source_target_pairs={{0,1},{1,2},{2,3},{3,4},{4,5},{5,6},{6,7},{7,8},{8,9},{9,10},{10,1... | collective-permute-start | bytes 5000 | tf_op jit(solution)/shard_map/ppermute | solution.py:16
  190.7 1.3 copy-start.1
where the time goes:
time: 194 us; the launch traced here: 192 us
  matrix products  94.5 us (49%)
  blocking collectives  42.4 us (22%)
  local copies, waits for them, and re-layouts  20 us (10%)
  other arithmetic  13.6 us (7%)
  starting transfers between devices  13.4 us (7%)
  waiting for transfers between devices  6.9 us (4%)
    dot_general x8, matrix products, add_block(): jnp.dot(block_values, selector, precision=lax.Precision.HIGHEST, preferre...  56.4 us
    all_gather x1, blocking collectives, local(): gathered = lax.all_gather(finished, ('grp', 'slab'), axis=1, tiled=True)  42.4 us
    dot_general x8, matrix products, look_block(): jnp.einsum('cw,pw->cp', lookup_table, selector, preferred_element_type=jn...  38.1 us
    ppermute x4, starting transfers between devices, from_behind(): lax.ppermute(value, axis, [(source, source + steps) for source in range(f...  13.4 us
    ppermute x4, waiting for transfers between devices, from_behind(): lax.ppermute(value, axis, [(source, source + steps) for source in range(f...  6.9 us
    dynamic_slice x8, local copies, waits for them, and re-layouts, add_block(): block_ids = lax.dynamic_slice_in_dim(grain_ids, first_point, BLOCK_PTS)  6.2 us
    dynamic_slice x8, local copies, waits for them, and re-layouts, look_block(): block_ids = lax.dynamic_slice_in_dim(grain_ids, first_point, BLOCK_PTS)  6.13 us
    concatenate x1, other arithmetic, local(): jnp.concatenate([jnp.ones((1, points), jnp.float32), orientation, stress,...  5.53 us
  transfers between devices with their start and end apart: 4, of which 3 were waited for; matrix products, arithmetic and copies ran while one was open for 4% of the time, Pallas kernels for 0%

commit v1 on v0

v1 whole, which is shorter than its diff:
```python
import functools

import jax
import jax.numpy as jnp
from jax import lax
from jax.experimental import pallas as pl
from jax.experimental.pallas import tpu as pltpu
from jax.sharding import PartitionSpec as P

AVG = 128
AXES = ("grp", "slab")
SUB = 8
WINDOW = 16
ROWS = 16
COUNT = 13
F32 = jnp.float32
BF16 = jnp.bfloat16


def window_sums(ids_ref, orientation, stress, first_tile, first_grain):
    grain_row = lax.broadcasted_iota(jnp.int32, (WINDOW, AVG), 0) + first_grain
    tiles = stress.shape[1] // AVG
    picks = []
    for tile in range(tiles):
        ids = jnp.broadcast_to(ids_ref[pl.ds(first_tile + tile, 1), :], (WINDOW, AVG))
        picks.append((ids == grain_row).astype(F32).astype(BF16))
    selector = jnp.concatenate(picks, axis=1)
    ones = jnp.ones((ROWS - COUNT, stress.shape[1]), F32)
    values = jnp.concatenate([orientation, stress, ones], axis=0)
    high = values.astype(BF16)
    low = (values - high.astype(F32)).astype(BF16)
    dims = (((1,), (1,)), ((), ()))
    return lax.dot_general(
        selector, high, dims, preferred_element_type=F32
    ) + lax.dot_general(selector, low, dims, preferred_element_type=F32)


def rim_kernel(tile_base, ids_lo, ids_hi, q_lo, q_hi, s_lo, s_hi, lower_ref, upper_ref, *, tiles):
    base = tile_base[0]
    low = window_sums(ids_lo, q_lo[...], s_lo[...], 0, base - 1)
    high = window_sums(ids_hi, q_hi[...], s_hi[...], ids_hi.shape[0] - 2, base + tiles - 1)
    square = ((0, AVG - WINDOW), (0, AVG - ROWS))
    lower_ref[...] = jnp.pad(low, square).T[:ROWS]
    upper_ref[...] = jnp.pad(high, square).T[:ROWS]


def sum_kernel(tile_base, ids_ref, q_ref, s_ref, out_ref, acc_ref, carry_ref):
    step = pl.program_id(0)
    tiles = ids_ref.shape[0]

    @pl.when(step == 0)
    def _():
        carry_ref[...] = jnp.zeros_like(carry_ref)

    carry = carry_ref[...]
    for sub in range(tiles // SUB):
        points = slice(sub * SUB * AVG, (sub + 1) * SUB * AVG)
        first = tile_base[0] + step * tiles + sub * SUB - 1
        sums = window_sums(ids_ref, q_ref[:, points], s_ref[:, points], sub * SUB, first)
        row = pl.multiple_of(step * tiles + sub * SUB, SUB)
        acc_ref[pl.ds(row, SUB), :ROWS] = carry + sums[:SUB]
        carry = sums[SUB:]
    carry_ref[...] = carry

    @pl.when(step == pl.num_programs(0) - 1)
    def _():
        total = pl.num_programs(0) * tiles
        acc_ref[pl.ds(pl.multiple_of(total, SUB), SUB), :ROWS] = carry
        for part in range(out_ref.shape[1] // AVG):
            block = acc_ref[part * AVG : (part + 1) * AVG, :]
            out_ref[:, part * AVG : (part + 1) * AVG] = block.T[:ROWS]


def finish_kernel(edge, part_ref, below_ref, above_ref, table_ref, window_ref, *, grains, blk):
    part = part_ref[...]
    lane = lax.broadcasted_iota(jnp.int32, (ROWS, AVG), 1)
    below = jnp.where((lane < 2) & (edge[0] > 0), below_ref[...], 0.0)
    above = jnp.where((lane < 2) & (edge[1] > 0), above_ref[...], 0.0)
    gap = jnp.zeros((ROWS, grains), F32)
    part = part + jnp.concatenate([below, gap], axis=1) + jnp.concatenate([gap, above], axis=1)
    row = lax.broadcasted_iota(jnp.int32, part.shape, 0)
    squares = jnp.sum(jnp.where(row < 4, part * part, 0.0), axis=0, keepdims=True)
    done = jnp.where(row < 4, part / jnp.sqrt(squares), part / part[COUNT : COUNT + 1])
    rounded = done.astype(BF16).astype(F32)
    for index in range(window_ref.shape[0]):
        window_ref[index] = rounded[:, index * blk : index * blk + AVG]
    own = rounded[:, 1 : 1 + grains]
    half = lax.broadcasted_iota(jnp.int32, (8, AVG), 1) < blk
    for pair in range(grains // AVG):
        top = own[:8, pair * AVG : (pair + 1) * AVG]
        low = own[8:, pair * AVG : (pair + 1) * AVG]
        first = jnp.where(half, top, pltpu.roll(low, blk, 1))
        second = jnp.where(half, pltpu.roll(top, blk, 1), low)
        table_ref[2 * pair] = first.astype(BF16)
        table_ref[2 * pair + 1] = second.astype(BF16)


def fluctuation_kernel(tile_base, ids_ref, q_ref, s_ref, window_ref, out_ref, *, blk):
    step = pl.program_id(0)
    tiles = ids_ref.shape[0]
    for tile in range(tiles):
        points = slice(tile * AVG, (tile + 1) * AVG)
        index = tile // blk
        base = tile_base[0] + step * tiles + index * blk - 1
        ids = jnp.broadcast_to(ids_ref[tile : tile + 1, :] - base, (8, AVG))
        means = jnp.concatenate(
            [
                jnp.take_along_axis(window_ref[index, :8], ids, axis=1),
                jnp.take_along_axis(window_ref[index, 8:], ids, axis=1),
            ],
            axis=0,
        )
        q = q_ref[:, points]
        unit = q / jnp.sqrt(jnp.sum(q * q, axis=0, keepdims=True))
        point_part = jnp.concatenate([unit, s_ref[:, points]], axis=0)
        out_ref[:, points] = (point_part - means[:COUNT]).astype(BF16)


def route_kernel(blocks_ref, place, held_ref, out_ref):
    slabs, per_device = out_ref.shape[:2]
    for slab in range(slabs):
        for slot in range(per_device):
            block = blocks_ref[(place[0] * slabs + slab) * per_device + slot]
            group = block // (slabs * per_device)
            out_ref[slab, slot] = held_ref[group, block % per_device]


def place_kernel(blocks_ref, place, got_ref, out_ref, *, blk):
    slabs, per_device = got_ref.shape[:2]
    half = lax.broadcasted_iota(jnp.int32, (8, AVG), 1) < blk

    def pick(slot):
        block = blocks_ref[place[0] * per_device + slot]
        slab = lax.rem(block // per_device, slabs)
        return got_ref[slab, slot].astype(F32)

    for pair in range(per_device // 2):
        first, second = pick(2 * pair), pick(2 * pair + 1)
        lanes = slice(pair * AVG, (pair + 1) * AVG)
        out_ref[:8, lanes] = jnp.where(half, first, pltpu.roll(second, blk, 1))
        low = jnp.where(half, pltpu.roll(first, blk, 1), second)
        out_ref[8:, lanes] = low[: COUNT - 8]


def local(grain_ids, orientation, stress, owner_blocks):
    groups, slabs = lax.axis_size("grp"), lax.axis_size("slab")
    devices = groups * slabs
    group, slab = lax.axis_index("grp"), lax.axis_index("slab")
    device = group * slabs + slab
    points = grain_ids.shape[0]
    tiles = points // AVG
    grains = tiles
    per_device = owner_blocks.shape[0] // devices
    blk = grains // per_device
    step_tiles = min(tiles, blk)
    steps = tiles // step_tiles
    step_points = step_tiles * AVG
    width = grains + AVG

    ids = grain_ids.reshape(tiles, AVG)
    tile_base = (device * tiles).astype(jnp.int32).reshape(1)
    smem = pl.BlockSpec(memory_space=pltpu.SMEM)
    vmem = pl.BlockSpec(memory_space=pltpu.VMEM)

    edge_tiles = 8
    edge_points = 2 * AVG
    last = tiles // edge_tiles - 1
    last_points = points // edge_points - 1
    lower, upper = pl.pallas_call(
        functools.partial(rim_kernel, tiles=tiles),
        out_shape=[jax.ShapeDtypeStruct((ROWS, AVG), F32)] * 2,
        grid=(1,),
        in_specs=[
            smem,
            pl.BlockSpec((edge_tiles, AVG), lambda i: (0, 0)),
            pl.BlockSpec((edge_tiles, AVG), lambda i: (last, 0)),
            pl.BlockSpec((4, edge_points), lambda i: (0, 0)),
            pl.BlockSpec((4, edge_points), lambda i: (0, last_points)),
            pl.BlockSpec((9, edge_points), lambda i: (0, 0)),
            pl.BlockSpec((9, edge_points), lambda i: (0, last_points)),
        ],
        out_specs=[pl.BlockSpec((ROWS, AVG), lambda i: (0, 0))] * 2,
        name="rims",
    )(tile_base, ids, ids, orientation, orientation, stress, stress)

    above = lax.ppermute(lower, AXES, [(d, (d - 1) % devices) for d in range(devices)])
    below = lax.ppermute(upper, AXES, [(d, (d + 1) % devices) for d in range(devices)])

    stream = [
        smem,
        pl.BlockSpec((step_tiles, AVG), lambda i: (i, 0)),
        pl.BlockSpec((4, step_points), lambda i: (0, i)),
        pl.BlockSpec((9, step_points), lambda i: (0, i)),
    ]
    part = pl.pallas_call(
        sum_kernel,
        out_shape=jax.ShapeDtypeStruct((ROWS, width), F32),
        grid=(steps,),
        in_specs=stream,
        out_specs=pl.BlockSpec((ROWS, width), lambda i: (0, 0)),
        scratch_shapes=[pltpu.VMEM((width, AVG), F32), pltpu.VMEM((SUB, ROWS), F32)],
        cost_estimate=pl.CostEstimate(
            flops=64 * points * ROWS, bytes_accessed=4 * points * ROWS, transcendentals=0
        ),
        name="sums",
    )(tile_base, ids, orientation, stress)

    edge = jnp.stack([device, devices - 1 - device]).astype(jnp.int32)
    table, windows = pl.pallas_call(
        functools.partial(finish_kernel, grains=grains, blk=blk),
        out_shape=[
            jax.ShapeDtypeStruct((per_device, 8, AVG), BF16),
            jax.ShapeDtypeStruct((tiles // blk, ROWS, AVG), F32),
        ],
        in_specs=[smem, vmem, vmem, vmem],
        out_specs=[vmem, vmem],
        name="finish",
    )(edge, part, below, above)

    fluctuation = pl.pallas_call(
        functools.partial(fluctuation_kernel, blk=blk),
        out_shape=jax.ShapeDtypeStruct((COUNT, points), BF16),
        grid=(steps,),
        in_specs=stream
        + [pl.BlockSpec((step_tiles // blk, ROWS, AVG), lambda i: (i, 0, 0))],
        out_specs=pl.BlockSpec((COUNT, step_points), lambda i: (0, i)),
        cost_estimate=pl.CostEstimate(
            flops=64 * points * ROWS, bytes_accessed=6 * points * ROWS, transcendentals=0
        ),
        name="fluctuation",
    )(tile_base, ids, orientation, stress, windows)

    held = lax.all_gather(table, "grp", axis=0)
    sent = pl.pallas_call(
        route_kernel,
        out_shape=jax.ShapeDtypeStruct((slabs, per_device, 8, AVG), BF16),
        in_specs=[smem, smem, vmem],
        out_specs=vmem,
        name="route",
    )(owner_blocks, group.astype(jnp.int32).reshape(1), held)
    got = lax.all_to_all(sent, "slab", 0, 0, tiled=True)
    grain_table = pl.pallas_call(
        functools.partial(place_kernel, blk=blk),
        out_shape=jax.ShapeDtypeStruct((COUNT, grains), F32),
        in_specs=[smem, smem, vmem],
        out_specs=vmem,
        name="place",
    )(owner_blocks, device.astype(jnp.int32).reshape(1), got)
    return (grain_table, fluctuation)


def solution(mesh):
    placed = (P(AXES), P(None, AXES), P(None, AXES), P())
    return jax.shard_map(
        local,
        mesh=mesh,
        in_specs=placed,
        out_specs=(P(None, AXES), P(None, AXES)),
        check_vma=False,
    )
```

time: 194 us -> 44.7 us (0.23)
  the two profiles are of different devices: /device:TPU:4 before, /device:TPU:0 now
where the time goes in v1:
time: 44.7 us; the launch traced here: 44 us
  Pallas kernels  21.9 us (49%)
  starting transfers between devices  9.77 us (22%)
  blocking collectives  9.28 us (21%)
  local copies, waits for them, and re-layouts  1.83 us (4%)
  between operations  0.66 us (1%)
  other arithmetic  0.58 us (1%)
    all_gather x1, blocking collectives, local(): held = lax.all_gather(table, 'grp', axis=0)  9.28 us
    pallas_call x1, Pallas kernels, local(): pl.pallas_call(functools.partial(fluctuation_kernel, blk=blk), out_shape=...  7.8 us
    pallas_call x1, Pallas kernels, local(): pl.pallas_call(sum_kernel, out_shape=jax.ShapeDtypeStruct((ROWS, width),...  7.2 us
    ppermute x1, starting transfers between devices, local(): lax.ppermute(lower, AXES, [(d, (d - 1) % devices) for d in range(devices)])  5.91 us
    all_to_all x1, starting transfers between devices, local(): got = lax.all_to_all(sent, 'slab', 0, 0, tiled=True)  3.37 us
    pallas_call x1, Pallas kernels, local(): pl.pallas_call(route_kernel, out_shape=jax.ShapeDtypeStruct((slabs, per_d...  1.97 us
    unnamed x6, local copies, waits for them, and re-layouts  1.83 us
    pallas_call x1, Pallas kernels, local(): pl.pallas_call(functools.partial(place_kernel, blk=blk), out_shape=jax.Sh...  1.66 us
  transfers between devices with their start and end apart: 3, of which 0 were waited for; matrix products, arithmetic and copies ran while one was open for 1% of the time, Pallas kernels for 34%

profile of v1, /device:TPU:0, one launch (start us, length us, event | category | flops | bytes accessed | tf_op | source)
XLA Modules:
  0.0 44.0 jit_solution(16566013072364116334)
XLA Ops:
  0.6 1.6 %rims.1 = (f32[16,128]{1,0:T(8,128)}, f32[16,128]{1,0:T(8,128)}) custom-call(s32[1]{0:T(128)} %bitcast.3.tile_base, s32[512,128]{1,0:T(8,128)} %bitcast.6, s32[512,128]{1,0:T(8,128)} %bitcast.7, f32[4,65536]{1,0:T(4,128)} %q_ref.3, f32[4,65536]{1,0:T(4,128)} %q_ref.3, f32[9,65536]{1,0:T(8,128)} %s_ref.3, f32[9,65536]{1,0:T(8,128)} %s_ref.3), custom_call_target="tpu_custom_call" | custom-call | tf_op jit(solution)/shard_map/rims/pallas_call | solution.py:169
  2.3 0.5 %collective-permute-start = (f32[16,128]{1,0:T(8,128)}, f32[16,128]{1,0:T(8,128)S(1)}, u32[]{:S(2)}, u32[]{:S(2)}) collective-permute-start(f32[16,128]{1,0:T(8,128)} %get-tuple-element.6), channel_id=1, source_target_pairs={{0,1},{1,2},{2,3},{3,4},{4,5},{5,6},{6,7},{7,8},{8,9},{9,10},{10,1... | collective-permute-start | bytes 24584 | tf_op jit(solution)/shard_map/ppermute | solution.py:187
  2.7 5.9 %collective-permute-start.1 = (f32[16,128]{1,0:T(8,128)}, f32[16,128]{1,0:T(8,128)S(1)}, u32[]{:S(2)}, u32[]{:S(2)}) collective-permute-start(f32[16,128]{1,0:T(8,128)} %get-tuple-element.7), channel_id=1, source_target_pairs={{0,31},{1,0},{2,1},{3,2},{4,3},{5,4},{6,5},{7,6},{8,7},{9,8},{10,9... | collective-permute-start | bytes 24584 | tf_op jit(solution)/shard_map/ppermute | solution.py:186
  8.7 0.6 %pad_add_fusion.edge = s32[2]{0:T(128)} fusion(s32[1]{0:T(128)} %bitcast.2, s32[1]{0:T(128)} %bitcast.place), kind=kLoop, calls=%fused_computation | loop fusion | flops 2 | bytes 16 | tf_op jit(solution)/shard_map/stack | solution.py:208
  9.2 7.2 %sums.1.part_ref = f32[16,640]{1,0:T(8,128)} custom-call(s32[1]{0:T(128)} %bitcast.3.tile_base, s32[512,128]{1,0:T(8,128)} %bitcast.8, f32[4,65536]{1,0:T(4,128)} %q_ref.3, f32[9,65536]{1,0:T(8,128)} %s_ref.3), custom_call_target="tpu_custom_call" | custom-call | flops 67108864 | bytes 4194304 | tf_op jit(solution)/shard_map/sums/pallas_call | solution.py:195
  16.4 0.0 collective-permute-done.below_ref
  16.4 0.0 copy-start.1
  16.4 0.0 collective-permute-done.1.above_ref
  16.4 0.6 %copy-done.1 = f32[16,128]{1,0:T(8,128)} copy-done((f32[16,128]{1,0:T(8,128)}, f32[16,128]{1,0:T(8,128)S(1)}, u32[]{:S(2)}) %copy-start.1) | copy-done | bytes 8216
  17.0 0.0 copy-start.2
  17.0 0.6 %copy-done.2 = f32[16,128]{1,0:T(8,128)} copy-done((f32[16,128]{1,0:T(8,128)}, f32[16,128]{1,0:T(8,128)S(1)}, u32[]{:S(2)}) %copy-start.2) | copy-done | bytes 8216
  17.6 1.6 %finish.1 = (bf16[8,8,128]{2,1,0:T(8,128)(2,1)}, f32[8,16,128]{2,1,0:T(8,128)}) custom-call(s32[2]{0:T(128)} %pad_add_fusion.edge, f32[16,640]{1,0:T(8,128)} %sums.1.part_ref, f32[16,128]{1,0:T(8,128)} %copy-done.1, f32[16,128]{1,0:T(8,128)} %copy-done.2), custom_call_target="tpu_custom_call" | custom-call | tf_op jit(solution)/shard_map/finish/pallas_call | solution.py:209
  19.2 9.3 %all-gather = bf16[32,8,128]{2,1,0:T(8,128)(2,1)} all-gather(bf16[8,8,128]{2,1,0:T(8,128)(2,1)} %get-tuple-element.8), channel_id=2, replica_groups=mesh['grp'=4,'slab'=8] {'grp'}, dimensions={0}, use_global_device_ids=true | all-gather | bytes 81920 | tf_op jit(solution)/shard_map/all_gather | solution.py:233
  28.5 2.0 %route.1 = bf16[8,8,8,128]{3,2,1,0:T(8,128)(2,1)} custom-call(s32[256]{0:T(256)} %blocks_ref.3, s32[1]{0:T(128)} %bitcast.1.place, bf16[4,8,8,128]{3,2,1,0:T(8,128)(2,1)} %bitcast.10), custom_call_target="tpu_custom_call" | custom-call | tf_op jit(solution)/shard_map/route/pallas_call | solution.py:234
  30.5 3.4 %all-to-all-start = ((bf16[8,8,8,128]{3,2,1,0:T(8,128)(2,1)}), bf16[8,8,8,128]{3,2,1,0:T(8,128)(2,1)S(1)}, u32[]{:S(2)}, u32[]{:S(2)}) async-start(bf16[8,8,8,128]{3,2,1,0:T(8,128)(2,1)} %route.1), calls=%async_computation | async-start | bytes 262144 | tf_op jit(solution)/shard_map/all_to_all | solution.py:241
  33.9 7.8 %fluctuation.1 = bf16[13,65536]{1,0:T(8,128)(2,1)} custom-call(s32[1]{0:T(128)} %bitcast.3.tile_base, s32[512,128]{1,0:T(8,128)} %bitcast.9, f32[4,65536]{1,0:T(4,128)} %q_ref.3, f32[9,65536]{1,0:T(8,128)} %s_ref.3, f32[8,16,128]{2,1,0:T(8,128)} %get-tuple-element.9.window_ref), custom_call_target="tpu_custom_call" | custom-call | flops 67108864 | bytes 6291456 | tf_op jit(solution)/shard_map/fluctuation/pallas_call | solution.py:220
  41.7 0.0 all-to-all-done.got_ref
  41.7 0.0 copy-start
  41.7 0.6 %copy-done = bf16[8,8,8,128]{3,2,1,0:T(8,128)(2,1)} copy-done((bf16[8,8,8,128]{3,2,1,0:T(8,128)(2,1)}, bf16[8,8,8,128]{3,2,1,0:T(8,128)(2,1)S(1)}, u32[]{:S(2)}) %copy-start) | copy-done | bytes 131096
  42.3 1.7 %place.1 = f32[13,512]{1,0:T(8,128)} custom-call(s32[256]{0:T(256)} %blocks_ref.3, s32[1]{0:T(128)} %bitcast.place, bf16[8,8,8,128]{3,2,1,0:T(8,128)(2,1)} %copy-done), custom_call_target="tpu_custom_call" | custom-call | tf_op jit(solution)/shard_map/place/pallas_call | solution.py:242
Async XLA Ops:
  2.3 14.2 %collective-permute-start = (f32[16,128]{1,0:T(8,128)}, f32[16,128]{1,0:T(8,128)S(1)}, u32[]{:S(2)}, u32[]{:S(2)}) collective-permute-start(f32[16,128]{1,0:T(8,128)} %get-tuple-element.6), channel_id=1, source_target_pairs={{0,1},{1,2},{2,3},{3,4},{4,5},{5,6},{6,7},{7,8},{8,9},{9,10},{10,1... | collective-permute-start | bytes 24584 | tf_op jit(solution)/shard_map/ppermute | solution.py:187
  2.7 13.7 %collective-permute-start.1 = (f32[16,128]{1,0:T(8,128)}, f32[16,128]{1,0:T(8,128)S(1)}, u32[]{:S(2)}, u32[]{:S(2)}) collective-permute-start(f32[16,128]{1,0:T(8,128)} %get-tuple-element.7), channel_id=1, source_target_pairs={{0,31},{1,0},{2,1},{3,2},{4,3},{5,4},{6,5},{7,6},{8,7},{9,8},{10,9... | collective-permute-start | bytes 24584 | tf_op jit(solution)/shard_map/ppermute | solution.py:186
  16.4 0.6 %copy-start.1 = (f32[16,128]{1,0:T(8,128)}, f32[16,128]{1,0:T(8,128)S(1)}, u32[]{:S(2)}) copy-start(f32[16,128]{1,0:T(8,128)S(1)} %collective-permute-done.below_ref) | copy-start | bytes 24580
  17.0 0.6 %copy-start.2 = (f32[16,128]{1,0:T(8,128)}, f32[16,128]{1,0:T(8,128)S(1)}, u32[]{:S(2)}) copy-start(f32[16,128]{1,0:T(8,128)S(1)} %collective-permute-done.1.above_ref) | copy-start | bytes 24580
  30.5 11.2 %all-to-all-start = ((bf16[8,8,8,128]{3,2,1,0:T(8,128)(2,1)}), bf16[8,8,8,128]{3,2,1,0:T(8,128)(2,1)S(1)}, u32[]{:S(2)}, u32[]{:S(2)}) async-start(bf16[8,8,8,128]{3,2,1,0:T(8,128)(2,1)} %route.1), calls=%async_computation | async-start | bytes 262144 | tf_op jit(solution)/shard_map/all_to_all | solution.py:241
  41.7 0.7 %copy-start = (bf16[8,8,8,128]{3,2,1,0:T(8,128)(2,1)}, bf16[8,8,8,128]{3,2,1,0:T(8,128)(2,1)S(1)}, u32[]{:S(2)}) copy-start(bf16[8,8,8,128]{3,2,1,0:T(8,128)(2,1)S(1)} %all-to-all-done.got_ref) | copy-start | bytes 393220

commit v2 on v0

v2 whole, which is shorter than its diff:
```python
import functools

import jax
import jax.numpy as jnp
from jax import lax
from jax.experimental import pallas as pl
from jax.experimental.pallas import tpu as pltpu
from jax.sharding import PartitionSpec as P

AVG = 128
AXES = ("grp", "slab")
SUB = 8
WINDOW = 16
ROWS = 16
COUNT = 13
EDGE = 2
F32 = jnp.float32
BF16 = jnp.bfloat16


def window_sums(ids_ref, values, first_tile, first_grain):
    grain_row = lax.broadcasted_iota(jnp.int32, (WINDOW, AVG), 0) + first_grain
    picks = []
    for tile in range(values.shape[1] // AVG):
        ids = jnp.broadcast_to(ids_ref[pl.ds(first_tile + tile, 1), :], (WINDOW, AVG))
        picks.append((ids == grain_row).astype(F32).astype(BF16))
    selector = jnp.concatenate(picks, axis=1)
    high = values.astype(BF16)
    low = (values - high.astype(F32)).astype(BF16)
    dims = (((1,), (1,)), ((), ()))
    return lax.dot_general(
        selector, high, dims, preferred_element_type=F32
    ) + lax.dot_general(selector, low, dims, preferred_element_type=F32)


def finish(total):
    row = lax.broadcasted_iota(jnp.int32, total.shape, 0)
    squares = jnp.sum(jnp.where(row < 4, total * total, 0.0), axis=0, keepdims=True)
    return total / jnp.where(row < 4, jnp.sqrt(squares), total[COUNT : COUNT + 1])


def look_up(top, low, ids):
    ids = jnp.broadcast_to(ids, (8, AVG))
    return jnp.concatenate([jnp.take_along_axis(half, ids, axis=1) for half in (top, low)], axis=0)


def sum_kernel(
    tile_base, ids_hbm, q_hbm, s_hbm, table_ref, window_ref, point_ref, ids_ref, q_ref, s_ref, acc_ref, sems,
    *, chunks, blk,
):
    tiles = ids_hbm.shape[0] // chunks
    points = tiles * AVG
    grains = chunks * tiles

    def copies(chunk):
        rows = pl.ds(pl.multiple_of(chunk * tiles, tiles), tiles)
        lanes = pl.ds(pl.multiple_of(chunk * points, points), points)
        return (
            pltpu.make_async_copy(ids_hbm.at[rows], ids_ref.at[rows], sems.at[0, chunk]),
            pltpu.make_async_copy(q_hbm.at[:, lanes], q_ref.at[:, lanes], sems.at[1, chunk]),
            pltpu.make_async_copy(s_hbm.at[:, lanes], s_ref.at[:, lanes], sems.at[2, chunk]),
        )

    for chunk in range(chunks):
        for copy in copies(chunk):
            copy.start()

    row = lax.broadcasted_iota(jnp.int32, (8, SUB * AVG), 0)
    ones = jnp.ones((ROWS - COUNT, SUB * AVG), F32)

    def step(chunk, carry):
        for copy in copies(chunk):
            copy.wait()
        for sub in range(tiles // SUB):
            tile = pl.multiple_of(chunk * tiles + sub * SUB, SUB)
            lanes = pl.ds(pl.multiple_of(tile * AVG, SUB * AVG), SUB * AVG)
            values = jnp.concatenate([q_ref[:, lanes], s_ref[:, lanes], ones], axis=0)
            sums = window_sums(ids_ref, values, tile, tile_base[0] + tile - 1)
            acc_ref[pl.ds(tile, SUB), :ROWS] = carry + sums[:SUB]
            carry = sums[SUB:]
            top = values[:8]
            squares = jnp.sum(jnp.where(row < 4, top * top, 0.0), axis=0, keepdims=True)
            point_ref[:8, lanes] = top * jnp.where(row < 4, lax.rsqrt(squares), 1.0)
            point_ref[8:, lanes] = values[8:]
        return carry

    carry = lax.fori_loop(0, chunks, step, jnp.zeros((SUB, ROWS), F32))
    acc_ref[grains : grains + SUB, :ROWS] = carry
    part = jnp.concatenate(
        [acc_ref[block * AVG : (block + 1) * AVG, :].T[:ROWS] for block in range(grains // AVG + 1)], axis=1
    )
    rounded = finish(part).astype(BF16).astype(F32)
    for index in range(window_ref.shape[0]):
        window_ref[index] = rounded[:, index * blk : index * blk + AVG]
    own = rounded[:, 1 : 1 + grains]
    half = lax.broadcasted_iota(jnp.int32, (8, AVG), 1) < blk
    for pair in range(grains // AVG):
        top = own[:8, pair * AVG : (pair + 1) * AVG]
        low = own[8:, pair * AVG : (pair + 1) * AVG]
        table_ref[2 * pair] = jnp.where(half, top, pltpu.roll(low, blk, 1)).astype(BF16)
        table_ref[2 * pair + 1] = jnp.where(half, pltpu.roll(top, blk, 1), low).astype(BF16)
    lane = lax.broadcasted_iota(jnp.int32, (ROWS, AVG), 1)
    ends = jnp.where(lane < 2, part[:, :AVG], pltpu.roll(part[:, grains:], 2, 1))
    high = ends.astype(BF16).astype(F32)
    mid = (ends - high).astype(BF16).astype(F32)
    rest = ends - high - mid
    pieces = jnp.where(lane < 4, high, jnp.where(lane < 8, pltpu.roll(mid, 4, 1), pltpu.roll(rest, 8, 1)))
    pieces = jnp.where(lane < 12, pieces, 0.0)
    table_ref[grains // blk] = jnp.where(half, pieces[:8], pltpu.roll(pieces[8:], blk, 1)).astype(BF16)


def fluctuation_kernel(
    tile_base, ids_ref, point_ref, window_ref, out_hbm, edge_ids_ref, edge_point_ref, edge_window_ref, out_ref, sems
):
    windows = window_ref.shape[0]
    total = ids_ref.shape[0]
    tiles = total // windows
    points = tiles * AVG

    def copy(window):
        lanes = pl.ds(pl.multiple_of(window * points, points), points)
        return pltpu.make_async_copy(out_ref.at[:, lanes], out_hbm.at[:, lanes], sems.at[window])

    def step(window, carry):
        base = tile_base[0] + window * tiles - 1
        top, low = window_ref[window, :8], window_ref[window, 8:]
        for index in range(tiles):
            tile = window * tiles + index
            lanes = pl.ds(pl.multiple_of(tile * AVG, AVG), AVG)
            value = point_ref[:, lanes] - look_up(top, low, ids_ref[pl.ds(tile, 1), :] - base)
            out_ref[:, lanes] = value[:COUNT].astype(BF16)
        copy(window).start()
        return carry

    lax.fori_loop(0, windows, step, 0)
    first, last = slice(0, EDGE), slice(total - EDGE, total)
    edge_ids_ref[:EDGE] = ids_ref[first] - (tile_base[0] - 1)
    edge_ids_ref[EDGE:] = ids_ref[last] - (tile_base[0] + total - tiles - 1)
    edge_point_ref[:, : EDGE * AVG] = point_ref[:, : EDGE * AVG]
    edge_point_ref[:, EDGE * AVG :] = point_ref[:, (total - EDGE) * AVG :]
    edge_window_ref[0] = window_ref[0]
    edge_window_ref[1] = window_ref[windows - 1]
    for window in range(windows):
        copy(window).wait()


def route_kernel(blocks_ref, place, *refs):
    *held_refs, out_ref, held_ref = refs
    groups = len(held_refs)
    slabs, slots = out_ref.shape[:2]
    per_device = slots - 1
    for offset, ref in enumerate(held_refs):
        held_ref[partner(place[0], offset, groups)] = ref[...]
    for slab in range(slabs):
        for slot in range(per_device):
            block = blocks_ref[(place[0] * slabs + slab) * per_device + slot]
            out_ref[slab, slot] = held_ref[block // (slabs * per_device), block % per_device]
    step = AVG // 2 // groups
    lane = lax.broadcasted_iota(jnp.int32, (8, AVG), 1) % (AVG // 2)
    ends = jnp.zeros((8, AVG), F32)
    for group in range(groups):
        rolled = pltpu.roll(held_ref[group, per_device].astype(F32), group * step, 1)
        ends = jnp.where((lane >= group * step) & (lane < group * step + 12), rolled, ends)
    for slab in range(slabs):
        out_ref[slab, per_device] = ends.astype(BF16)


def partner(group, offset, groups):
    if groups & (groups - 1) == 0:
        return group ^ offset
    return lax.rem(group + groups - offset, groups)


def place_kernel(
    blocks_ref, place, got_ref, edge_ids_ref, edge_point_ref, edge_window_ref, fluctuation_in, table_ref,
    fluctuation_hbm, edge_ref, sems, *, groups, blk,
):
    del fluctuation_in
    slabs, slots = got_ref.shape[:2]
    per_device = slots - 1
    devices = groups * slabs
    step = AVG // 2 // groups
    device = place[0]
    lane8 = lax.broadcasted_iota(jnp.int32, (8, AVG), 1)
    lane = lax.broadcasted_iota(jnp.int32, (ROWS, AVG), 1)
    half = lane8 < blk

    def ends(owner):
        inside = (owner >= 0) & (owner < devices)
        owner = jnp.clip(owner, 0, devices - 1)
        piece = got_ref[lax.rem(owner, slabs), per_device].astype(F32)
        piece = pltpu.roll(piece, lax.rem(AVG - step * (owner // slabs), AVG), 1)
        piece = piece + pltpu.roll(piece, AVG - 4, 1) + pltpu.roll(piece, AVG - 8, 1)
        piece = jnp.concatenate([piece, pltpu.roll(piece, blk, 1)], axis=0)
        return jnp.where(inside, piece, 0.0)

    def at(value, source, target):
        return pltpu.roll(value, (target - source) % AVG, 1)

    mine, below, above = ends(device), ends(device - 1), ends(device + 1)
    shared = jnp.where(lane < 2, mine + at(below, 2, 0), mine + at(above, 0, 2))
    shared = finish(shared).astype(BF16).astype(F32)
    first = jnp.where(lane < 2, shared, edge_window_ref[0])
    upper = edge_ref.shape[1] // AVG - 2 * EDGE
    last_lane = blk + upper
    last = jnp.where((lane >= last_lane) & (lane < last_lane + 2), at(shared, 2, last_lane), edge_window_ref[1])
    for tile in range(2 * EDGE):
        table = first if tile < EDGE else last
        lanes = slice(tile * AVG, (tile + 1) * AVG)
        value = edge_point_ref[:, lanes] - look_up(table[:8], table[8:], edge_ids_ref[tile : tile + 1, :])
        edge_ref[:, lanes] = value[:COUNT].astype(BF16)
    width = EDGE * AVG
    total = fluctuation_hbm.shape[1]
    copies = (
        pltpu.make_async_copy(edge_ref.at[:, :width], fluctuation_hbm.at[:, :width], sems.at[0]),
        pltpu.make_async_copy(edge_ref.at[:, width:], fluctuation_hbm.at[:, total - width :], sems.at[1]),
    )
    for copy in copies:
        copy.start()

    def pick(slot):
        block = blocks_ref[device * per_device + slot]
        owner, index = block // per_device, lax.rem(block, per_device)
        tile = got_ref[lax.rem(owner, slabs), slot].astype(F32)
        own = ends(owner)
        start = slot % 2 * blk
        low = at(own, 1, start) + at(ends(owner - 1), 3, start)
        high = at(own, 2, start + blk - 1) + at(ends(owner + 1), 0, start + blk - 1)
        is_low = (lane == start) & (index == 0)
        is_high = (lane == start + blk - 1) & (index == per_device - 1)
        return tile, jnp.where(is_low, low, high), is_low | is_high

    for pair in range(per_device // 2):
        (first, first_sums, first_mask), (second, second_sums, second_mask) = pick(2 * pair), pick(2 * pair + 1)
        lanes = slice(pair * AVG, (pair + 1) * AVG)
        top = jnp.where(half, first, pltpu.roll(second, blk, 1))
        low = jnp.where(half, pltpu.roll(first, blk, 1), second)
        repaired = finish(jnp.where(lane < blk, first_sums, second_sums))
        value = jnp.where(first_mask | second_mask, repaired, jnp.concatenate([top, low], axis=0))
        table_ref[:, lanes] = value[:COUNT]
    for copy in copies:
        copy.wait()


def local(grain_ids, orientation, stress, owner_blocks):
    groups, slabs = lax.axis_size("grp"), lax.axis_size("slab")
    group = lax.axis_index("grp")
    device = group * slabs + lax.axis_index("slab")
    points = grain_ids.shape[0]
    tiles = points // AVG
    grains = tiles
    per_device = owner_blocks.shape[0] // (groups * slabs)
    blk = grains // per_device
    slots = per_device + 1

    ids = grain_ids.reshape(tiles, AVG)
    in_hbm = [pltpu.with_memory_space_constraint(x, pltpu.HBM) for x in (ids, orientation, stress)]
    place = device.astype(jnp.int32).reshape(1)
    tile_base = place * tiles
    smem = pl.BlockSpec(memory_space=pltpu.SMEM)
    vmem = pl.BlockSpec(memory_space=pltpu.VMEM)
    hbm = pl.BlockSpec(memory_space=pltpu.HBM)
    params = pltpu.CompilerParams(vmem_limit_bytes=20 << 20)

    chunks = 8
    table, windows, point = pl.pallas_call(
        functools.partial(sum_kernel, chunks=chunks, blk=blk),
        out_shape=[
            jax.ShapeDtypeStruct((slots, 8, AVG), BF16),
            jax.ShapeDtypeStruct((tiles // blk, ROWS, AVG), F32),
            jax.ShapeDtypeStruct((ROWS, points), F32),
        ],
        in_specs=[smem, hbm, hbm, hbm],
        out_specs=[vmem, vmem, vmem],
        scratch_shapes=[
            pltpu.VMEM((tiles, AVG), jnp.int32),
            pltpu.VMEM((4, points), F32),
            pltpu.VMEM((9, points), F32),
            pltpu.VMEM((grains + AVG, AVG), F32),
            pltpu.SemaphoreType.DMA((3, chunks)),
        ],
        compiler_params=params,
        cost_estimate=pl.CostEstimate(
            flops=64 * points * ROWS, bytes_accessed=4 * points * ROWS, transcendentals=0
        ),
        name="sums",
    )(tile_base, *in_hbm)

    held = [table]
    for offset in range(1, groups):
        moves = [(int(partner(g, offset, groups)), g) for g in range(groups)]
        held.append(lax.ppermute(table, "grp", moves))

    fluctuation, edge_ids, edge_point, edge_windows = pl.pallas_call(
        fluctuation_kernel,
        out_shape=[
            jax.ShapeDtypeStruct((COUNT, points), BF16),
            jax.ShapeDtypeStruct((2 * EDGE, AVG), jnp.int32),
            jax.ShapeDtypeStruct((ROWS, 2 * EDGE * AVG), F32),
            jax.ShapeDtypeStruct((2, ROWS, AVG), F32),
        ],
        in_specs=[smem, vmem, vmem, vmem],
        out_specs=[hbm, vmem, vmem, vmem],
        scratch_shapes=[
            pltpu.VMEM((COUNT, points), BF16),
            pltpu.SemaphoreType.DMA((tiles // blk,)),
        ],
        compiler_params=params,
        cost_estimate=pl.CostEstimate(
            flops=64 * points * ROWS, bytes_accessed=6 * points * ROWS, transcendentals=0
        ),
        name="fluctuation",
    )(tile_base, ids, point, windows)

    held, edge_ids = lax.optimization_barrier((held, edge_ids))
    sent = pl.pallas_call(
        route_kernel,
        out_shape=jax.ShapeDtypeStruct((slabs, slots, 8, AVG), BF16),
        in_specs=[smem, smem] + [vmem] * groups,
        out_specs=vmem,
        scratch_shapes=[pltpu.VMEM((groups, slots, 8, AVG), BF16)],
        compiler_params=params,
        name="route",
    )(owner_blocks, group.astype(jnp.int32).reshape(1), *held)
    got = lax.all_to_all(sent, "slab", 0, 0, tiled=True)
    grain_table, fluctuation = pl.pallas_call(
        functools.partial(place_kernel, groups=groups, blk=blk),
        out_shape=[
            jax.ShapeDtypeStruct((COUNT, grains), F32),
            jax.ShapeDtypeStruct((COUNT, points), BF16),
        ],
        in_specs=[smem, smem, vmem, vmem, vmem, vmem, hbm],
        out_specs=[vmem, hbm],
        scratch_shapes=[pltpu.VMEM((COUNT, 2 * EDGE * AVG), BF16), pltpu.SemaphoreType.DMA((2,))],
        input_output_aliases={6: 1},
        compiler_params=params,
        name="place",
    )(owner_blocks, place, got, edge_ids, edge_point, edge_windows, fluctuation)
    return (grain_table, fluctuation)


def solution(mesh):
    placed = (P(AXES), P(None, AXES), P(None, AXES), P())
    return jax.shard_map(
        local,
        mesh=mesh,
        in_specs=placed,
        out_specs=(P(None, AXES), P(None, AXES)),
        check_vma=False,
    )
```

time: 194 us -> 29.7 us (0.15)
  the two profiles are of different devices: /device:TPU:4 before, /device:TPU:0 now
where the time goes in v2:
time: 29.7 us; the launch traced here: 29.5 us
  Pallas kernels  12.1 us (41%)
  blocking collectives  12 us (40%)
  starting transfers between devices  4.63 us (16%)
  between operations  0.71 us (2%)
    all_to_all x1, blocking collectives, local(): got = lax.all_to_all(sent, 'slab', 0, 0, tiled=True)  12 us
    pallas_call x1, Pallas kernels, local(): pl.pallas_call(functools.partial(sum_kernel, chunks=chunks, blk=blk), out...  4.83 us
    ppermute x3, starting transfers between devices, local(): held.append(lax.ppermute(table, 'grp', moves))  4.63 us
    pallas_call x1, Pallas kernels, local(): pl.pallas_call(fluctuation_kernel, out_shape=[jax.ShapeDtypeStruct((COUNT...  3.86 us
    pallas_call x1, Pallas kernels, local(): pl.pallas_call(functools.partial(place_kernel, groups=groups, blk=blk), o...  2.4 us
    pallas_call x1, Pallas kernels, local(): pl.pallas_call(route_kernel, out_shape=jax.ShapeDtypeStruct((slabs, slots...  1.03 us
  transfers between devices with their start and end apart: 3, of which 0 were waited for; matrix products, arithmetic and copies ran while one was open for 0% of the time, Pallas kernels for 13%

profile of v2, /device:TPU:0, one launch (start us, length us, event | category | flops | bytes accessed | tf_op | source)
XLA Modules:
  0.0 29.5 jit_solution(10464330934969750265)
XLA Ops:
  0.6 0.0 copy-start
  0.6 0.0 copy-start.1
  0.7 4.8 %sums.1 = (bf16[9,8,128]{2,1,0:T(8,128)(2,1)S(1)}, f32[8,16,128]{2,1,0:T(8,128)S(1)}, f32[16,65536]{1,0:T(8,128)S(1)}) custom-call(s32[1]{0:T(128)S(6)} %mul.7.tile_base, s32[512,128]{1,0:T(8,128)} %bitcast.3, f32[4,65536]{1,0:T(4,128)} %q_hbm.1, f32[9,65536]{1,0:T(8,128)} %s_hbm.1), custom_call_target="tpu_custom_call" | custom-call | flops 67108864 | bytes 4194304 | tf_op jit(solution)/shard_map/sums/pallas_call | solution.py:266
  5.5 4.0 %collective-permute-start.2 = (bf16[9,8,128]{2,1,0:T(8,128)(2,1)S(1)}, bf16[9,8,128]{2,1,0:T(8,128)(2,1)S(1)}, u32[]{:S(2)}, u32[]{:S(2)}) collective-permute-start(bf16[9,8,128]{2,1,0:T(8,128)(2,1)S(1)} %get-tuple-element.18.refs_0_), channel_id=1, source_target_pairs={{24,0},{16,8},{8,16},{0,24},{25,1},{17,9},{9,17},{1,25},{26,2},{18... | collective-permute-start | bytes 55304 | tf_op jit(solution)/shard_map/ppermute | solution.py:292
  9.5 0.5 %collective-permute-start.1 = (bf16[9,8,128]{2,1,0:T(8,128)(2,1)S(1)}, bf16[9,8,128]{2,1,0:T(8,128)(2,1)S(1)}, u32[]{:S(2)}, u32[]{:S(2)}) collective-permute-start(bf16[9,8,128]{2,1,0:T(8,128)(2,1)S(1)} %get-tuple-element.18.refs_0_), channel_id=1, source_target_pairs={{16,0},{24,8},{0,16},{8,24},{17,1},{25,9},{1,17},{9,25},{18,2},{26... | collective-permute-start | bytes 55304 | tf_op jit(solution)/shard_map/ppermute | solution.py:292
  10.0 0.1 collective-permute-start
  10.1 0.0 copy-done
  10.1 3.9 %fluctuation.1 = (bf16[13,65536]{1,0:T(8,128)(2,1)}, s32[4,128]{1,0:T(4,128)S(1)}, f32[16,512]{1,0:T(8,128)S(1)}, f32[2,16,128]{2,1,0:T(8,128)S(1)}) custom-call(s32[1]{0:T(128)S(6)} %mul.7.tile_base, s32[512,128]{1,0:T(8,128)S(1)} %bitcast.4, f32[16,65536]{1,0:T(8,128)S(1)} %get-tuple-element.15.point_ref, f32[8,16,128]{2,1,0:T(8,128)S(1)} %get-tuple-element.16.window_ref), custom_call_target="tpu_custom_call" | custom-call | flops 67108864 | bytes 6291456 | tf_op jit(solution)/shard_map/fluctuation/pallas_call | solution.py:294
  14.0 0.0 collective-permute-done.2.refs_3_
  14.0 0.0 collective-permute-done.1.refs_2_
  14.0 0.0 collective-permute-done.refs_1_
  14.0 0.0 copy-done.1
  14.0 1.0 %route.1 = bf16[8,9,8,128]{3,2,1,0:T(8,128)(2,1)S(1)} custom-call(s32[256]{0:T(256)S(1)} %copy-done.1, s32[1]{0:T(128)} %bitcast.1.place, bf16[9,8,128]{2,1,0:T(8,128)(2,1)S(1)} %get-tuple-element.18.refs_0_, bf16[9,8,128]{2,1,0:T(8,128)(2,1)S(1)} %collective-permute-done.refs_1_, bf16[9,8,128]{2,1,0:T(8,128)(2,1)S(1)} %collective-permute-done.1.refs_2_, ...), custom_call_target="tpu_custom_call" | custom-call | tf_op jit(solution)/shard_map/route/pallas_call | solution.py:316
  15.1 12.0 %all_to_all.5.got_ref = bf16[8,9,8,128]{3,2,1,0:T(8,128)(2,1)S(1)} all-to-all(bf16[8,9,8,128]{3,2,1,0:T(8,128)(2,1)S(1)} %route.1), channel_id=1, replica_groups=mesh['grp'=4,'slab'=8] {'slab'}, dimensions={0} | all-to-all | bytes 294912 | tf_op jit(solution)/shard_map/all_to_all | solution.py:325
  27.1 2.4 %place.1 = (f32[13,512]{1,0:T(8,128)}, bf16[13,65536]{1,0:T(8,128)(2,1)}) custom-call(s32[256]{0:T(256)S(1)} %copy-done.1, s32[1]{0:T(128)} %bitcast.place, bf16[8,9,8,128]{3,2,1,0:T(8,128)(2,1)S(1)} %all_to_all.5.got_ref, s32[4,128]{1,0:T(4,128)S(1)} %get-tuple-element.22.edge_ids_ref, ...), custom_call_target="tpu_custom_call", output_to_operand_aliasing={{1}: (6, {})} | custom-call | tf_op jit(solution)/shard_map/place/pallas_call | solution.py:326
Async XLA Ops:
  0.6 9.5 %copy-start = (s32[65536]{0:T(1024)S(1)}, s32[65536]{0:T(1024)}, u32[]{:S(2)}) copy-start(s32[65536]{0:T(1024)} %param.4) | copy-start | bytes 786436
  0.6 13.4 %copy-start.1 = (s32[256]{0:T(256)S(1)}, s32[256]{0:T(256)}, u32[]{:S(2)}) copy-start(s32[256]{0:T(256)} %blocks_ref.3) | copy-start | bytes 3076
  5.5 8.5 %collective-permute-start.2 = (bf16[9,8,128]{2,1,0:T(8,128)(2,1)S(1)}, bf16[9,8,128]{2,1,0:T(8,128)(2,1)S(1)}, u32[]{:S(2)}, u32[]{:S(2)}) collective-permute-start(bf16[9,8,128]{2,1,0:T(8,128)(2,1)S(1)} %get-tuple-element.18.refs_0_), channel_id=1, source_target_pairs={{24,0},{16,8},{8,16},{0,24},{25,1},{17,9},{9,17},{1,25},{26,2},{18... | collective-permute-start | bytes 55304 | tf_op jit(solution)/shard_map/ppermute | solution.py:292
  9.5 4.5 %collective-permute-start.1 = (bf16[9,8,128]{2,1,0:T(8,128)(2,1)S(1)}, bf16[9,8,128]{2,1,0:T(8,128)(2,1)S(1)}, u32[]{:S(2)}, u32[]{:S(2)}) collective-permute-start(bf16[9,8,128]{2,1,0:T(8,128)(2,1)S(1)} %get-tuple-element.18.refs_0_), channel_id=1, source_target_pairs={{16,0},{24,8},{0,16},{8,24},{17,1},{25,9},{1,17},{9,25},{18,2},{26... | collective-permute-start | bytes 55304 | tf_op jit(solution)/shard_map/ppermute | solution.py:292
  10.0 4.0 %collective-permute-start = (bf16[9,8,128]{2,1,0:T(8,128)(2,1)S(1)}, bf16[9,8,128]{2,1,0:T(8,128)(2,1)S(1)}, u32[]{:S(2)}, u32[]{:S(2)}) collective-permute-start(bf16[9,8,128]{2,1,0:T(8,128)(2,1)S(1)} %get-tuple-element.18.refs_0_), channel_id=1, source_target_pairs={{8,0},{0,8},{24,16},{16,24},{9,1},{1,9},{25,17},{17,25},{10,2},{2,... | collective-permute-start | bytes 55304 | tf_op jit(solution)/shard_map/ppermute | solution.py:292

commit v3 on v2

v3 whole, which is shorter than its diff:
```python
import functools

import jax
import jax.numpy as jnp
from jax import lax
from jax.experimental import pallas as pl
from jax.experimental.pallas import tpu as pltpu
from jax.sharding import PartitionSpec as P

AVG = 128
AXES = ("grp", "slab")
SUB = 8
WINDOW = 16
ROWS = 16
COUNT = 13
CORES = 2
EDGE = 2
F32 = jnp.float32
BF16 = jnp.bfloat16


def window_sums(selector, values):
    high = values.astype(BF16)
    low = (values - high.astype(F32)).astype(BF16)
    dims = (((1,), (1,)), ((), ()))
    return lax.dot_general(
        selector, high, dims, preferred_element_type=F32
    ) + lax.dot_general(selector, low, dims, preferred_element_type=F32)


def finish(total):
    row = lax.broadcasted_iota(jnp.int32, total.shape, 0)
    squares = jnp.sum(jnp.where(row < 4, total * total, 0.0), axis=0, keepdims=True)
    scale = jnp.where(row < 4, jnp.sqrt(squares), total[COUNT : COUNT + 1])
    return total / jnp.where(scale > 0.0, scale, 1.0)


def div_rem(x, n):
    if n & (n - 1) == 0:
        return x >> (n.bit_length() - 1), x & (n - 1)
    return lax.div(x, n), lax.rem(x, n)


def selection(ids_ref, first_tile, tiles, first_grain):
    grain_row = lax.broadcasted_iota(jnp.int32, (WINDOW, AVG), 0) + first_grain
    picks = []
    for tile in range(tiles):
        ids = jnp.broadcast_to(ids_ref[pl.ds(first_tile + tile, 1), :], (WINDOW, AVG))
        picks.append((ids == grain_row).astype(F32).astype(BF16))
    return jnp.concatenate(picks, axis=1)


def sum_kernel(
    tile_base, ids_hbm, q_hbm, s_hbm, table_ref, window_ref, point_ref, ids_ref, q_ref, s_ref, acc_ref, sems,
    *, chunks, blk,
):
    tiles = ids_hbm.shape[0] // chunks
    points = tiles * AVG
    grains = chunks * tiles

    def copies(chunk):
        rows = pl.ds(pl.multiple_of(chunk * tiles, tiles), tiles)
        quads = pl.ds(pl.multiple_of(chunk * tiles * 4, tiles * 4), tiles * 4)
        lanes = pl.ds(pl.multiple_of(chunk * points, points), points)
        return (
            pltpu.make_async_copy(ids_hbm.at[rows], ids_ref.at[rows], sems.at[0, chunk]),
            pltpu.make_async_copy(q_hbm.at[quads], q_ref.at[quads], sems.at[1, chunk]),
            pltpu.make_async_copy(s_hbm.at[:, lanes], s_ref.at[:, lanes], sems.at[2, chunk]),
        )

    for chunk in range(chunks):
        for copy in copies(chunk):
            copy.start()

    quaternion = lax.broadcasted_iota(jnp.int32, (8, AVG), 0) < 4
    ones = jnp.ones((ROWS - COUNT, SUB * AVG), F32)

    def step(chunk, carry):
        for copy in copies(chunk):
            copy.wait()
        for sub in range(tiles // SUB):
            tile = pl.multiple_of(chunk * tiles + sub * SUB, SUB)
            lanes = pl.ds(pl.multiple_of(tile * AVG, SUB * AVG), SUB * AVG)
            quad = pl.multiple_of(tile * 4, 4 * SUB)
            q = jnp.concatenate([q_ref[pl.ds(quad + 4 * t, 4), :] for t in range(SUB)], axis=1)
            values = jnp.concatenate([q, s_ref[:, lanes], ones], axis=0)
            sums = window_sums(selection(ids_ref, tile, SUB, tile_base[0] + tile - 1), values)
            acc_ref[pl.ds(tile, SUB), :ROWS] = carry + sums[:SUB]
            carry = sums[SUB:]
            parts = [q_ref[pl.ds(quad + c, SUB, stride=4), :] for c in range(4)]
            scale = lax.rsqrt(sum(part * part for part in parts))
            scales = [
                jnp.where(quaternion, jnp.broadcast_to(scale[t : t + 1], (8, AVG)), 1.0) for t in range(SUB)
            ]
            point_ref[:8, lanes] = values[:8] * jnp.concatenate(scales, axis=1)
            point_ref[8:, lanes] = values[8:]
        return carry

    carry = lax.fori_loop(0, chunks, step, jnp.zeros((SUB, ROWS), F32))
    acc_ref[grains : grains + SUB, :ROWS] = carry
    part = jnp.concatenate(
        [acc_ref[block * AVG : (block + 1) * AVG, :].T[:ROWS] for block in range(grains // AVG + 1)], axis=1
    )
    rounded = finish(part).astype(BF16).astype(F32)
    for index in range(window_ref.shape[0]):
        window_ref[index] = rounded[:, index * blk : index * blk + AVG]
    own = rounded[:, 1 : 1 + grains]
    half = lax.broadcasted_iota(jnp.int32, (8, AVG), 1) < blk
    for pair in range(grains // AVG):
        top = own[:8, pair * AVG : (pair + 1) * AVG]
        low = own[8:, pair * AVG : (pair + 1) * AVG]
        table_ref[2 * pair] = jnp.where(half, top, pltpu.roll(low, blk, 1)).astype(BF16)
        table_ref[2 * pair + 1] = jnp.where(half, pltpu.roll(top, blk, 1), low).astype(BF16)
    lane = lax.broadcasted_iota(jnp.int32, (ROWS, AVG), 1)
    ends = jnp.where(lane < 2, part[:, :AVG], pltpu.roll(part[:, grains:], 2, 1))
    high = ends.astype(BF16).astype(F32)
    mid = (ends - high).astype(BF16).astype(F32)
    rest = ends - high - mid
    pieces = jnp.where(lane < 4, high, jnp.where(lane < 8, pltpu.roll(mid, 4, 1), pltpu.roll(rest, 8, 1)))
    pieces = jnp.where(lane < 12, pieces, 0.0)
    table_ref[grains // blk] = jnp.where(half, pieces[:8], pltpu.roll(pieces[8:], blk, 1)).astype(BF16)


def fluctuation_kernel(
    tile_base, ids_ref, point_ref, window_ref, out_hbm, edge_ids_ref, edge_point_ref, edge_window_ref, out_ref, sems
):
    windows = window_ref.shape[0]
    total = ids_ref.shape[0]
    tiles = total // windows
    points = tiles * AVG

    def copy(window):
        lanes = pl.ds(pl.multiple_of(window * points, points), points)
        return pltpu.make_async_copy(out_ref.at[:, lanes], out_hbm.at[:, lanes], sems.at[window])

    def step(window, carry):
        table = window_ref[window]
        for sub in range(tiles // SUB):
            tile = pl.multiple_of(window * tiles + sub * SUB, SUB)
            lanes = pl.ds(pl.multiple_of(tile * AVG, SUB * AVG), SUB * AVG)
            near = pltpu.roll(table, (AVG - sub * SUB) % AVG, 1)[:, :WINDOW].astype(BF16)
            picks = selection(ids_ref, tile, SUB, tile_base[0] + tile - 1)
            means = jnp.dot(near, picks, preferred_element_type=F32)
            out_ref[:, lanes] = (point_ref[:, lanes] - means)[:COUNT].astype(BF16)
        copy(window).start()
        return carry

    lax.fori_loop(0, windows, step, 0)
    first, last = slice(0, EDGE), slice(total - EDGE, total)
    edge_ids_ref[:EDGE] = ids_ref[first]
    edge_ids_ref[EDGE:] = ids_ref[last]
    edge_point_ref[:, : EDGE * AVG] = point_ref[:, : EDGE * AVG]
    edge_point_ref[:, EDGE * AVG :] = point_ref[:, (total - EDGE) * AVG :]
    edge_window_ref[0] = window_ref[0]
    edge_window_ref[1] = pltpu.roll(window_ref[windows - 1], AVG - tiles + SUB, 1)
    for window in range(windows):
        copy(window).wait()


def source(me, offset, count):
    if count & (count - 1) == 0:
        return me ^ offset
    return (me + count - offset) % count


def target(me, offset, count):
    if count & (count - 1) == 0:
        return me ^ offset
    return (me + offset) % count


def stack_kernel(place, *refs):
    *held_refs, out_ref = refs
    for offset, ref in enumerate(held_refs):
        out_ref[source(place[0], offset, len(held_refs))] = ref[...]


def route_kernel(blocks_ref, place, mine_ref, other_ref, *refs):
    *out_refs, held_ref = refs
    chips = len(out_refs)
    groups, slots = mine_ref.shape[:2]
    per_device = slots - 1
    slabs = chips * CORES
    group, slab = div_rem(place[0], slabs)
    chip, core = div_rem(slab, CORES)
    held_ref[core] = mine_ref[...]
    held_ref[1 - core] = other_ref[...]
    step = AVG // 2 // groups
    lane = lax.broadcasted_iota(jnp.int32, (8, AVG), 1) & (AVG // 2 - 1)
    for owner_core in range(CORES):
        ends = held_ref[owner_core, 0, per_device].astype(F32)
        for owner_group in range(1, groups):
            rolled = pltpu.roll(held_ref[owner_core, owner_group, per_device].astype(F32), owner_group * step, 1)
            ends = jnp.where(lane >= owner_group * step, rolled, ends)
        for out_ref in out_refs:
            out_ref[per_device + owner_core] = ends.astype(BF16)
    for offset, out_ref in enumerate(out_refs):
        wanted = (group * slabs + target(chip, offset, chips) * CORES + core) * per_device
        for slot in range(per_device):
            owner, index = div_rem(blocks_ref[wanted + slot], per_device)
            owner_group, owner_slab = div_rem(owner, slabs)
            out_ref[slot] = held_ref[div_rem(owner_slab, CORES)[1], owner_group, index]


def place_kernel(blocks_ref, place, *refs, groups, chips, blk):
    (*got_refs, edge_ids_ref, edge_point_ref, edge_window_ref, _, table_ref, fluctuation_hbm, held_ref, ends_ref,
     edge_ref, sems) = refs
    slots = got_refs[0].shape[0]
    per_device = slots - CORES
    slabs = chips * CORES
    devices = groups * slabs
    grains = table_ref.shape[1]
    step = AVG // 2 // groups
    device = place[0]
    chip = div_rem(div_rem(device, slabs)[1], CORES)[0]
    lane = lax.broadcasted_iota(jnp.int32, (8, AVG), 1)
    half = lane < blk

    for offset, ref in enumerate(got_refs):
        owner_chip = source(chip, offset, chips)
        held_ref[owner_chip] = ref[...]
        for core in range(CORES):
            piece = ref[per_device + core].astype(F32)
            piece = piece + pltpu.roll(piece, AVG - 4, 1) + pltpu.roll(piece, AVG - 8, 1)
            ends_ref[owner_chip * CORES + core] = piece

    def ends(owner, column, lane):
        group, slab = div_rem(jnp.clip(owner, 0, devices - 1), slabs)
        moved = pltpu.roll(ends_ref[slab], (lane - column - step * group + 2 * AVG) & (AVG - 1), 1)
        return jnp.where((owner >= 0) & (owner < devices), moved, 0.0)

    def unfold(value):
        return jnp.concatenate([value, pltpu.roll(value, blk, 1)], axis=0)

    lane_half = lane & (blk - 1)
    others = jnp.where(lane_half < 2, ends(device - 1, 2, 0), ends(device + 1, 0, 2))
    shared = finish(unfold(ends(device, 0, 0) + others))
    wide_lane = lax.broadcasted_iota(jnp.int32, (ROWS, AVG), 1)
    first = jnp.where(wide_lane < 2, shared, edge_window_ref[0])
    in_last = (wide_lane >= SUB) & (wide_lane < SUB + 2)
    last = jnp.where(in_last, pltpu.roll(shared, SUB - 2, 1), edge_window_ref[1])
    width = EDGE * AVG
    total = fluctuation_hbm.shape[1]
    first_grain = device * grains - 1
    copies = []
    for end, (table, grain, begin) in enumerate(
        ((first, first_grain, 0), (last, first_grain + grains - SUB, total - width))
    ):
        lanes = slice(end * width, (end + 1) * width)
        picks = selection(edge_ids_ref, end * EDGE, EDGE, grain)
        means = jnp.dot(table[:, :WINDOW].astype(BF16), picks, preferred_element_type=F32)
        edge_ref[:, lanes] = (edge_point_ref[:, lanes] - means)[:COUNT].astype(BF16)
        copies.append(
            pltpu.make_async_copy(
                edge_ref.at[:, lanes], fluctuation_hbm.at[:, begin : begin + width], sems.at[end]
            )
        )
        copies[-1].start()

    tiles, columns = [], []
    sums = jnp.zeros((8, AVG), F32)
    for slot in range(per_device):
        owner, index = div_rem(blocks_ref[device * per_device + slot], per_device)
        owner_chip = div_rem(div_rem(owner, slabs)[1], CORES)[0]
        tiles.append(held_ref[owner_chip, slot].astype(F32))
        low = index == 0
        beside = jnp.where(low, owner - 1, owner + 1)
        both = ends(owner, jnp.where(low, 1, 2), slot) + ends(beside, jnp.where(low, 3, 0), slot)
        sums = jnp.where(lane_half == slot, both, sums)
        columns.append(jnp.where(low, 0, jnp.where(index == per_device - 1, blk - 1, 2 * AVG)))
    repaired = finish(unfold(sums))
    repaired = jnp.where(half, repaired[:8], pltpu.roll(repaired[8:], blk, 1))
    for slot in range(per_device):
        moved = pltpu.roll(repaired, (columns[slot] - slot + AVG) & (AVG - 1), 1)
        tiles[slot] = jnp.where(lane_half == columns[slot], moved, tiles[slot])
    for pair in range(per_device // 2):
        first, second = tiles[2 * pair], tiles[2 * pair + 1]
        lanes = slice(pair * AVG, (pair + 1) * AVG)
        table_ref[:8, lanes] = jnp.where(half, first, pltpu.roll(second, blk, 1))
        table_ref[8:, lanes] = jnp.where(half, pltpu.roll(first, blk, 1), second)[: COUNT - 8]
    for copy in copies:
        copy.wait()


def local(grain_ids, orientation, stress, owner_blocks):
    groups, slabs = lax.axis_size("grp"), lax.axis_size("slab")
    group = lax.axis_index("grp")
    device = group * slabs + lax.axis_index("slab")
    points = grain_ids.shape[0]
    tiles = points // AVG
    grains = tiles
    per_device = owner_blocks.shape[0] // (groups * slabs)
    blk = grains // per_device
    slots = per_device + 1
    chips = slabs // CORES

    ids = grain_ids.reshape(tiles, AVG)
    quads = orientation.reshape(4, tiles, AVG).transpose(1, 0, 2).reshape(4 * tiles, AVG)
    in_hbm = [pltpu.with_memory_space_constraint(x, pltpu.HBM) for x in (ids, quads, stress)]
    place = device.astype(jnp.int32).reshape(1)
    tile_base = place * tiles
    smem = pl.BlockSpec(memory_space=pltpu.SMEM)
    vmem = pl.BlockSpec(memory_space=pltpu.VMEM)
    hbm = pl.BlockSpec(memory_space=pltpu.HBM)
    params = pltpu.CompilerParams(vmem_limit_bytes=20 << 20)

    chunks = 8
    table, windows, point = pl.pallas_call(
        functools.partial(sum_kernel, chunks=chunks, blk=blk),
        out_shape=[
            jax.ShapeDtypeStruct((slots, 8, AVG), BF16),
            jax.ShapeDtypeStruct((tiles // blk, ROWS, AVG), F32),
            jax.ShapeDtypeStruct((ROWS, points), F32),
        ],
        in_specs=[smem, hbm, hbm, hbm],
        out_specs=[vmem, vmem, vmem],
        scratch_shapes=[
            pltpu.VMEM((tiles, AVG), jnp.int32),
            pltpu.VMEM((4 * tiles, AVG), F32),
            pltpu.VMEM((9, points), F32),
            pltpu.VMEM((grains + AVG, AVG), F32),
            pltpu.SemaphoreType.DMA((3, chunks)),
        ],
        compiler_params=params,
        cost_estimate=pl.CostEstimate(
            flops=64 * points * ROWS, bytes_accessed=4 * points * ROWS, transcendentals=0
        ),
        name="sums",
    )(tile_base, *in_hbm)

    held = [table]
    for offset in range(1, groups):
        moves = [(g, int(target(g, offset, groups))) for g in range(groups)]
        held.append(lax.ppermute(table, "grp", moves))

    fluctuation, edge_ids, edge_point, edge_windows = pl.pallas_call(
        fluctuation_kernel,
        out_shape=[
            jax.ShapeDtypeStruct((COUNT, points), BF16),
            jax.ShapeDtypeStruct((2 * EDGE, AVG), jnp.int32),
            jax.ShapeDtypeStruct((ROWS, 2 * EDGE * AVG), F32),
            jax.ShapeDtypeStruct((2, ROWS, AVG), F32),
        ],
        in_specs=[smem, vmem, vmem, vmem],
        out_specs=[hbm, vmem, vmem, vmem],
        scratch_shapes=[
            pltpu.VMEM((COUNT, points), BF16),
            pltpu.SemaphoreType.DMA((tiles // blk,)),
        ],
        compiler_params=params,
        cost_estimate=pl.CostEstimate(
            flops=64 * points * ROWS, bytes_accessed=6 * points * ROWS, transcendentals=0
        ),
        name="fluctuation",
    )(tile_base, ids, point, windows)

    held, edge_ids = lax.optimization_barrier((held, edge_ids))
    mine = pl.pallas_call(
        stack_kernel,
        out_shape=jax.ShapeDtypeStruct((groups, slots, 8, AVG), BF16),
        in_specs=[smem] + [vmem] * groups,
        out_specs=vmem,
        compiler_params=params,
        name="stack",
    )(group.astype(jnp.int32).reshape(1), *held)
    other = lax.ppermute(mine, "slab", [(s, s ^ 1) for s in range(slabs)])
    sent = pl.pallas_call(
        route_kernel,
        out_shape=[jax.ShapeDtypeStruct((per_device + CORES, 8, AVG), BF16)] * chips,
        in_specs=[smem, smem, vmem, vmem],
        out_specs=[vmem] * chips,
        scratch_shapes=[pltpu.VMEM((CORES, groups, slots, 8, AVG), BF16)],
        compiler_params=params,
        name="route",
    )(owner_blocks, place, mine, other)
    got = [sent[0]]
    for offset in range(1, chips):
        moves = [
            (chip * CORES + core, int(target(chip, offset, chips)) * CORES + core)
            for chip in range(chips)
            for core in range(CORES)
        ]
        got.append(lax.ppermute(sent[offset], "slab", moves))
    grain_table, fluctuation = pl.pallas_call(
        functools.partial(place_kernel, groups=groups, chips=chips, blk=blk),
        out_shape=[
            jax.ShapeDtypeStruct((COUNT, grains), F32),
            jax.ShapeDtypeStruct((COUNT, points), BF16),
        ],
        in_specs=[smem, smem] + [vmem] * (chips + 3) + [hbm],
        out_specs=[vmem, hbm],
        scratch_shapes=[
            pltpu.VMEM((chips, per_device + CORES, 8, AVG), BF16),
            pltpu.VMEM((slabs, 8, AVG), F32),
            pltpu.VMEM((COUNT, 2 * EDGE * AVG), BF16),
            pltpu.SemaphoreType.DMA((2,)),
        ],
        input_output_aliases={chips + 5: 1},
        compiler_params=params,
        name="place",
    )(owner_blocks, place, *got, edge_ids, edge_point, edge_windows, fluctuation)
    return (grain_table, fluctuation)


def solution(mesh):
    placed = (P(AXES), P(None, AXES), P(None, AXES), P())
    return jax.shard_map(
        local,
        mesh=mesh,
        in_specs=placed,
        out_specs=(P(None, AXES), P(None, AXES)),
        check_vma=False,
    )
```

time: 29.7 us -> 27.8 us (0.936)
  blocking collectives: 12 us -> 0 us
  waiting for transfers between devices: 0.01 us -> 7.31 us
  starting transfers between devices: 4.63 us -> 9.15 us
  Pallas kernels: 12.1 us -> 10.5 us
    all_to_all x1 -> x0, blocking collectives: 12 us -> none  [local(): got = lax.all_to_all(sent, 'slab', 0, 0, tiled=True)]
    ppermute x0 -> x4, waiting for transfers between devices: none -> 6.61 us  [the longest x3 5.36 us: local(): got.append(lax.ppermute(sent[offset], 'slab', moves))]
    ppermute x0 -> x4, starting transfers between devices: none -> 4.52 us  [the longest x3 4.45 us: local(): got.append(lax.ppermute(sent[offset], 'slab', moves))]
    pallas_call x1, Pallas kernels: 3.86 us -> 2.91 us  [local(): pl.pallas_call(fluctuation_kernel, out_shape=[jax.ShapeDtypeStruct((COUNT...]
    ppermute x3, waiting for transfers between devices: 0.01 us -> 0.7 us  [local(): held.append(lax.ppermute(table, 'grp', moves))]
    pallas_call x2 -> x3, Pallas kernels: 3.44 us -> 2.87 us  [the longest x1 2.2 us: local(): pl.pallas_call(functools.partial(place_kernel, groups=groups, chips=chips...]
  transfers between devices with their start and end apart: 3 -> 7, of which waited for: 0 -> 5; matrix products, arithmetic and copies ran while one was open for 0% -> 0% of each run, Pallas kernels for 13% -> 11%
where the time goes in v3:
time: 27.8 us; the launch traced here: 27.7 us
  Pallas kernels  10.5 us (38%)
  starting transfers between devices  9.15 us (33%)
  waiting for transfers between devices  7.31 us (26%)
  between operations  0.7 us (3%)
    ppermute x3, waiting for transfers between devices, local(): got.append(lax.ppermute(sent[offset], 'slab', moves))  5.36 us
    pallas_call x1, Pallas kernels, local(): pl.pallas_call(functools.partial(sum_kernel, chunks=chunks, blk=blk), out...  4.72 us
    ppermute x3, starting transfers between devices, local(): held.append(lax.ppermute(table, 'grp', moves))  4.62 us
    ppermute x3, starting transfers between devices, local(): got.append(lax.ppermute(sent[offset], 'slab', moves))  4.45 us
    pallas_call x1, Pallas kernels, local(): pl.pallas_call(fluctuation_kernel, out_shape=[jax.ShapeDtypeStruct((COUNT...  2.91 us
    pallas_call x1, Pallas kernels, local(): pl.pallas_call(functools.partial(place_kernel, groups=groups, chips=chips...  2.2 us
    ppermute x1, waiting for transfers between devices, local(): other = lax.ppermute(mine, 'slab', [(s, s ^ 1) for s in range(slabs)])  1.25 us
    ppermute x3, waiting for transfers between devices, local(): held.append(lax.ppermute(table, 'grp', moves))  0.7 us
  transfers between devices with their start and end apart: 7, of which 5 were waited for; matrix products, arithmetic and copies ran while one was open for 0% of the time, Pallas kernels for 11%

profile of v3, /device:TPU:0, one launch (start us, length us, event | category | flops | bytes accessed | tf_op | source)
XLA Modules:
  0.0 27.7 jit_solution(14504383485528232139)
XLA Ops:
  0.6 0.0 copy-start
  0.6 0.0 copy-start.1
  0.7 4.7 %sums.1 = (bf16[9,8,128]{2,1,0:T(8,128)(2,1)S(1)}, f32[8,16,128]{2,1,0:T(8,128)S(1)}, f32[16,65536]{1,0:T(8,128)S(1)}) custom-call(s32[1]{0:T(128)S(6)} %mul.7.tile_base, s32[512,128]{1,0:T(8,128)} %bitcast.8, f32[2048,128]{1,0:T(8,128)} %bitcast.10, f32[9,65536]{1,0:T(8,128)} %s_hbm.1), custom_call_target="tpu_custom_call" | custom-call | flops 67108864 | bytes 4194304 | tf_op jit(solution)/shard_map/sums/pallas_call | solution.py:308
  5.4 4.0 %collective-permute-start.2 = (bf16[9,8,128]{2,1,0:T(8,128)(2,1)S(1)}, bf16[9,8,128]{2,1,0:T(8,128)(2,1)S(1)}, u32[]{:S(2)}, u32[]{:S(2)}) collective-permute-start(bf16[9,8,128]{2,1,0:T(8,128)(2,1)S(1)} %get-tuple-element.22.refs_0_), channel_id=1, source_target_pairs={{0,24},{8,16},{16,8},{24,0},{1,25},{9,17},{17,9},{25,1},{2,26},{10... | collective-permute-start | bytes 55304 | tf_op jit(solution)/shard_map/ppermute | solution.py:334
  9.4 0.5 %collective-permute-start.1 = (bf16[9,8,128]{2,1,0:T(8,128)(2,1)S(1)}, bf16[9,8,128]{2,1,0:T(8,128)(2,1)S(1)}, u32[]{:S(2)}, u32[]{:S(2)}) collective-permute-start(bf16[9,8,128]{2,1,0:T(8,128)(2,1)S(1)} %get-tuple-element.22.refs_0_), channel_id=1, source_target_pairs={{0,16},{8,24},{16,0},{24,8},{1,17},{9,25},{17,1},{25,9},{2,18},{10... | collective-permute-start | bytes 55304 | tf_op jit(solution)/shard_map/ppermute | solution.py:334
  9.9 0.1 collective-permute-start
  10.0 0.0 copy-done
  10.0 2.9 %fluctuation.1 = (bf16[13,65536]{1,0:T(8,128)(2,1)}, s32[4,128]{1,0:T(4,128)S(1)}, f32[16,512]{1,0:T(8,128)S(1)}, f32[2,16,128]{2,1,0:T(8,128)S(1)}) custom-call(s32[1]{0:T(128)S(6)} %mul.7.tile_base, s32[512,128]{1,0:T(8,128)S(1)} %bitcast.9, f32[16,65536]{1,0:T(8,128)S(1)} %get-tuple-element.19.point_ref, f32[8,16,128]{2,1,0:T(8,128)S(1)} %get-tuple-element.20.window_ref), custom_call_target="tpu_custom_call" | custom-call | flops 67108864 | bytes 6291456 | tf_op jit(solution)/shard_map/fluctuation/pallas_call | solution.py:336
  12.9 0.0 collective-permute-done.2.refs_3_
  12.9 0.2 collective-permute-done.1.refs_2_
  13.1 0.5 %collective-permute-done.refs_1_ = bf16[9,8,128]{2,1,0:T(8,128)(2,1)S(1)} collective-permute-done((bf16[9,8,128]{2,1,0:T(8,128)(2,1)S(1)}, bf16[9,8,128]{2,1,0:T(8,128)(2,1)S(1)}, u32[]{:S(2)}, u32[]{:S(2)}) %collective-permute-start) | collective-permute-done | bytes 18464 | tf_op jit(solution)/shard_map/ppermute | solution.py:334
  13.7 0.1 collective-permute-start.3
  13.7 1.3 %collective-permute-done.3.other_ref = bf16[4,9,8,128]{3,2,1,0:T(8,128)(2,1)S(1)} collective-permute-done((bf16[4,9,8,128]{3,2,1,0:T(8,128)(2,1)S(1)}, bf16[4,9,8,128]{3,2,1,0:T(8,128)(2,1)S(1)}, u32[]{:S(2)}, u32[]{:S(2)}) %collective-permute-start.3) | collective-permute-done | bytes 73760 | tf_op jit(solution)/shard_map/ppermute | solution.py:366
  15.0 0.0 copy-done.1
  15.0 0.7 %route.1 = (bf16[10,8,128]{2,1,0:T(8,128)(2,1)S(1)}, bf16[10,8,128]{2,1,0:T(8,128)(2,1)S(1)}, bf16[10,8,128]{2,1,0:T(8,128)(2,1)S(1)}, bf16[10,8,128]{2,1,0:T(8,128)(2,1)S(1)}) custom-call(s32[256]{0:T(256)S(1)} %copy-done.1, s32[1]{0:T(128)} %bitcast.place, bf16[4,9,8,128]{3,2,1,0:T(8,128)(2,1)S(1)} %stack.1.mine_ref, ...), custom_call_target="tpu_custom_call" | custom-call | tf_op jit(solution)/shard_map/route/pallas_call | solution.py:367
  15.7 1.6 %collective-permute-start.4 = (bf16[10,8,128]{2,1,0:T(8,128)(2,1)S(1)}, bf16[10,8,128]{2,1,0:T(8,128)(2,1)S(1)}, u32[]{:S(2)}, u32[]{:S(2)}) collective-permute-start(bf16[10,8,128]{2,1,0:T(8,128)(2,1)S(1)} %get-tuple-element.27), channel_id=1, source_target_pairs={{0,2},{1,3},{2,0},{3,1},{4,6},{5,7},{6,4},{7,5},{8,10},{9,11},{10,... | collective-permute-start | bytes 61448 | tf_op jit(solution)/shard_map/ppermute | solution.py:383
  17.3 2.6 %collective-permute-start.5 = (bf16[10,8,128]{2,1,0:T(8,128)(2,1)S(1)}, bf16[10,8,128]{2,1,0:T(8,128)(2,1)S(1)}, u32[]{:S(2)}, u32[]{:S(2)}) collective-permute-start(bf16[10,8,128]{2,1,0:T(8,128)(2,1)S(1)} %get-tuple-element.28), channel_id=1, source_target_pairs={{0,4},{1,5},{2,6},{3,7},{4,0},{5,1},{6,2},{7,3},{8,12},{9,13},{10,... | collective-permute-start | bytes 61448 | tf_op jit(solution)/shard_map/ppermute | solution.py:383
  19.9 0.2 collective-permute-start.6
  20.1 0.0 collective-permute-done.4.refs_1_
  20.1 2.1 %collective-permute-done.5.refs_2_ = bf16[10,8,128]{2,1,0:T(8,128)(2,1)S(1)} collective-permute-done((bf16[10,8,128]{2,1,0:T(8,128)(2,1)S(1)}, bf16[10,8,128]{2,1,0:T(8,128)(2,1)S(1)}, u32[]{:S(2)}, u32[]{:S(2)}) %collective-permute-start.5) | collective-permute-done | bytes 20512 | tf_op jit(solution)/shard_map/ppermute | solution.py:383
  22.2 3.3 %collective-permute-done.6.refs_3_ = bf16[10,8,128]{2,1,0:T(8,128)(2,1)S(1)} collective-permute-done((bf16[10,8,128]{2,1,0:T(8,128)(2,1)S(1)}, bf16[10,8,128]{2,1,0:T(8,128)(2,1)S(1)}, u32[]{:S(2)}, u32[]{:S(2)}) %collective-permute-start.6) | collective-permute-done | bytes 20512 | tf_op jit(solution)/shard_map/ppermute | solution.py:383
  25.5 2.2 %place.1 = (f32[13,512]{1,0:T(8,128)}, bf16[13,65536]{1,0:T(8,128)(2,1)}) custom-call(s32[256]{0:T(256)S(1)} %copy-done.1, s32[1]{0:T(128)} %bitcast.place, bf16[10,8,128]{2,1,0:T(8,128)(2,1)S(1)} %get-tuple-element.26.refs_0_, bf16[10,8,128]{2,1,0:T(8,128)(2,1)S(1)} %collective-permute-done.4.refs_1_, ...), custom_call_target="tpu_custom_call", output_to_operand_aliasing={{1}: (9, {})} | custom-call | tf_op jit(solution)/shard_map/place/pallas_call | solution.py:384
  (1 shorter events, 0.0 us)
Async XLA Ops:
  0.6 9.4 %copy-start = (s32[65536]{0:T(1024)S(1)}, s32[65536]{0:T(1024)}, u32[]{:S(2)}) copy-start(s32[65536]{0:T(1024)} %param.4) | copy-start | bytes 786436
  0.6 14.3 %copy-start.1 = (s32[256]{0:T(256)S(1)}, s32[256]{0:T(256)}, u32[]{:S(2)}) copy-start(s32[256]{0:T(256)} %blocks_ref.3) | copy-start | bytes 3076
  5.4 7.6 %collective-permute-start.2 = (bf16[9,8,128]{2,1,0:T(8,128)(2,1)S(1)}, bf16[9,8,128]{2,1,0:T(8,128)(2,1)S(1)}, u32[]{:S(2)}, u32[]{:S(2)}) collective-permute-start(bf16[9,8,128]{2,1,0:T(8,128)(2,1)S(1)} %get-tuple-element.22.refs_0_), channel_id=1, source_target_pairs={{0,24},{8,16},{16,8},{24,0},{1,25},{9,17},{17,9},{25,1},{2,26},{10... | collective-permute-start | bytes 55304 | tf_op jit(solution)/shard_map/ppermute | solution.py:334
  9.4 3.8 %collective-permute-start.1 = (bf16[9,8,128]{2,1,0:T(8,128)(2,1)S(1)}, bf16[9,8,128]{2,1,0:T(8,128)(2,1)S(1)}, u32[]{:S(2)}, u32[]{:S(2)}) collective-permute-start(bf16[9,8,128]{2,1,0:T(8,128)(2,1)S(1)} %get-tuple-element.22.refs_0_), channel_id=1, source_target_pairs={{0,16},{8,24},{16,0},{24,8},{1,17},{9,25},{17,1},{25,9},{2,18},{10... | collective-permute-start | bytes 55304 | tf_op jit(solution)/shard_map/ppermute | solution.py:334
  9.9 3.8 %collective-permute-start = (bf16[9,8,128]{2,1,0:T(8,128)(2,1)S(1)}, bf16[9,8,128]{2,1,0:T(8,128)(2,1)S(1)}, u32[]{:S(2)}, u32[]{:S(2)}) collective-permute-start(bf16[9,8,128]{2,1,0:T(8,128)(2,1)S(1)} %get-tuple-element.22.refs_0_), channel_id=1, source_target_pairs={{0,8},{8,0},{16,24},{24,16},{1,9},{9,1},{17,25},{25,17},{2,10},{10... | collective-permute-start | bytes 55304 | tf_op jit(solution)/shard_map/ppermute | solution.py:334
  13.7 1.3 %collective-permute-start.3 = (bf16[4,9,8,128]{3,2,1,0:T(8,128)(2,1)S(1)}, bf16[4,9,8,128]{3,2,1,0:T(8,128)(2,1)S(1)}, u32[]{:S(2)}, u32[]{:S(2)}) collective-permute-start(bf16[4,9,8,128]{3,2,1,0:T(8,128)(2,1)S(1)} %stack.1.mine_ref), channel_id=1, source_target_pairs={{0,1},{1,0},{2,3},{3,2},{4,5},{5,4},{6,7},{7,6},{8,9},{9,8},{10,11... | collective-permute-start | bytes 221192 | tf_op jit(solution)/shard_map/ppermute | solution.py:366
  15.7 4.5 %collective-permute-start.4 = (bf16[10,8,128]{2,1,0:T(8,128)(2,1)S(1)}, bf16[10,8,128]{2,1,0:T(8,128)(2,1)S(1)}, u32[]{:S(2)}, u32[]{:S(2)}) collective-permute-start(bf16[10,8,128]{2,1,0:T(8,128)(2,1)S(1)} %get-tuple-element.27), channel_id=1, source_target_pairs={{0,2},{1,3},{2,0},{3,1},{4,6},{5,7},{6,4},{7,5},{8,10},{9,11},{10,... | collective-permute-start | bytes 61448 | tf_op jit(solution)/shard_map/ppermute | solution.py:383
  17.3 4.9 %collective-permute-start.5 = (bf16[10,8,128]{2,1,0:T(8,128)(2,1)S(1)}, bf16[10,8,128]{2,1,0:T(8,128)(2,1)S(1)}, u32[]{:S(2)}, u32[]{:S(2)}) collective-permute-start(bf16[10,8,128]{2,1,0:T(8,128)(2,1)S(1)} %get-tuple-element.28), channel_id=1, source_target_pairs={{0,4},{1,5},{2,6},{3,7},{4,0},{5,1},{6,2},{7,3},{8,12},{9,13},{10,... | collective-permute-start | bytes 61448 | tf_op jit(solution)/shard_map/ppermute | solution.py:383
  19.9 5.6 %collective-permute-start.6 = (bf16[10,8,128]{2,1,0:T(8,128)(2,1)S(1)}, bf16[10,8,128]{2,1,0:T(8,128)(2,1)S(1)}, u32[]{:S(2)}, u32[]{:S(2)}) collective-permute-start(bf16[10,8,128]{2,1,0:T(8,128)(2,1)S(1)} %get-tuple-element.29), channel_id=1, source_target_pairs={{0,6},{1,7},{2,4},{3,5},{4,2},{5,3},{6,0},{7,1},{8,14},{9,15},{10,... | collective-permute-start | bytes 61448 | tf_op jit(solution)/shard_map/ppermute | solution.py:383

commit v4 on v3

--- a/solution.py
+++ b/solution.py
@@ -22,10 +22,8 @@
 def window_sums(selector, values):
     high = values.astype(BF16)
     low = (values - high.astype(F32)).astype(BF16)
-    dims = (((1,), (1,)), ((), ()))
-    return lax.dot_general(
-        selector, high, dims, preferred_element_type=F32
-    ) + lax.dot_general(selector, low, dims, preferred_element_type=F32)
+    both = jnp.concatenate([high, low], axis=0)
+    return lax.dot_general(selector, both, (((1,), (1,)), ((), ())), preferred_element_type=F32)
 
 
 def finish(total):
@@ -33,6 +31,10 @@
     squares = jnp.sum(jnp.where(row < 4, total * total, 0.0), axis=0, keepdims=True)
     scale = jnp.where(row < 4, jnp.sqrt(squares), total[COUNT : COUNT + 1])
     return total / jnp.where(scale > 0.0, scale, 1.0)
+
+
+def device_index():
+    return lax.axis_index("grp") * lax.axis_size("slab") + lax.axis_index("slab")
 
 
 def div_rem(x, n):
@@ -51,17 +53,18 @@
 
 
 def sum_kernel(
-    tile_base, ids_hbm, q_hbm, s_hbm, table_ref, window_ref, point_ref, ids_ref, q_ref, s_ref, acc_ref, sems,
+    ids_hbm, q_hbm, s_hbm, table_ref, window_ref, point_ref, ids_ref, q_ref, s_ref, acc_ref, sems,
     *, chunks, blk,
 ):
     tiles = ids_hbm.shape[0] // chunks
     points = tiles * AVG
     grains = chunks * tiles
+    tile_base = device_index() * grains
 
     def copies(chunk):
-        rows = pl.ds(pl.multiple_of(chunk * tiles, tiles), tiles)
-        quads = pl.ds(pl.multiple_of(chunk * tiles * 4, tiles * 4), tiles * 4)
-        lanes = pl.ds(pl.multiple_of(chunk * points, points), points)
+        rows = pl.ds(chunk * tiles, tiles)
+        quads = pl.ds(chunk * tiles * 4, tiles * 4)
+        lanes = pl.ds(chunk * points, points)
         return (
             pltpu.make_async_copy(ids_hbm.at[rows], ids_ref.at[rows], sems.at[0, chunk]),
             pltpu.make_async_copy(q_hbm.at[quads], q_ref.at[quads], sems.at[1, chunk]),
@@ -79,13 +82,13 @@
         for copy in copies(chunk):
             copy.wait()
         for sub in range(tiles // SUB):
-            tile = pl.multiple_of(chunk * tiles + sub * SUB, SUB)
-            lanes = pl.ds(pl.multiple_of(tile * AVG, SUB * AVG), SUB * AVG)
-            quad = pl.multiple_of(tile * 4, 4 * SUB)
+            tile = chunk * tiles + sub * SUB
+            lanes = pl.ds(tile * AVG, SUB * AVG)
+            quad = tile * 4
             q = jnp.concatenate([q_ref[pl.ds(quad + 4 * t, 4), :] for t in range(SUB)], axis=1)
             values = jnp.concatenate([q, s_ref[:, lanes], ones], axis=0)
-            sums = window_sums(selection(ids_ref, tile, SUB, tile_base[0] + tile - 1), values)
-            acc_ref[pl.ds(tile, SUB), :ROWS] = carry + sums[:SUB]
+            sums = window_sums(selection(ids_ref, tile, SUB, tile_base + tile - 1), values)
+            acc_ref[pl.ds(tile, SUB), : 2 * ROWS] = carry + sums[:SUB]
             carry = sums[SUB:]
             parts = [q_ref[pl.ds(quad + c, SUB, stride=4), :] for c in range(4)]
             scale = lax.rsqrt(sum(part * part for part in parts))
@@ -96,11 +99,12 @@
             point_ref[8:, lanes] = values[8:]
         return carry
 
-    carry = lax.fori_loop(0, chunks, step, jnp.zeros((SUB, ROWS), F32))
-    acc_ref[grains : grains + SUB, :ROWS] = carry
-    part = jnp.concatenate(
-        [acc_ref[block * AVG : (block + 1) * AVG, :].T[:ROWS] for block in range(grains // AVG + 1)], axis=1
-    )
+    carry = jnp.zeros((SUB, 2 * ROWS), F32)
+    for chunk in range(chunks):
+        carry = step(chunk, carry)
+    acc_ref[grains : grains + SUB, : 2 * ROWS] = carry
+    blocks = [acc_ref[block * AVG : (block + 1) * AVG, :].T for block in range(grains // AVG + 1)]
+    part = jnp.concatenate([block[:ROWS] + block[ROWS : 2 * ROWS] for block in blocks], axis=1)
     rounded = finish(part).astype(BF16).astype(F32)
     for index in range(window_ref.shape[0]):
         window_ref[index] = rounded[:, index * blk : index * blk + AVG]
@@ -122,30 +126,31 @@
 
 
 def fluctuation_kernel(
-    tile_base, ids_ref, point_ref, window_ref, out_hbm, edge_ids_ref, edge_point_ref, edge_window_ref, out_ref, sems
+    ids_ref, point_ref, window_ref, out_hbm, edge_ids_ref, edge_point_ref, edge_window_ref, out_ref, sems
 ):
     windows = window_ref.shape[0]
     total = ids_ref.shape[0]
+    tile_base = device_index() * total
     tiles = total // windows
     points = tiles * AVG
 
     def copy(window):
-        lanes = pl.ds(pl.multiple_of(window * points, points), points)
+        lanes = pl.ds(window * points, points)
         return pltpu.make_async_copy(out_ref.at[:, lanes], out_hbm.at[:, lanes], sems.at[window])
 
-    def step(window, carry):
+    def step(window):
         table = window_ref[window]
         for sub in range(tiles // SUB):
-            tile = pl.multiple_of(window * tiles + sub * SUB, SUB)
-            lanes = pl.ds(pl.multiple_of(tile * AVG, SUB * AVG), SUB * AVG)
+            tile = window * tiles + sub * SUB
+            lanes = pl.ds(tile * AVG, SUB * AVG)
             near = pltpu.roll(table, (AVG - sub * SUB) % AVG, 1)[:, :WINDOW].astype(BF16)
-            picks = selection(ids_ref, tile, SUB, tile_base[0] + tile - 1)
+            picks = selection(ids_ref, tile, SUB, tile_base + tile - 1)
             means = jnp.dot(near, picks, preferred_element_type=F32)
             out_ref[:, lanes] = (point_ref[:, lanes] - means)[:COUNT].astype(BF16)
         copy(window).start()
-        return carry
-
-    lax.fori_loop(0, windows, step, 0)
+
+    for window in range(windows):
+        step(window)
     first, last = slice(0, EDGE), slice(total - EDGE, total)
     edge_ids_ref[:EDGE] = ids_ref[first]
     edge_ids_ref[EDGE:] = ids_ref[last]
@@ -169,20 +174,22 @@
     return (me + offset) % count
 
 
-def stack_kernel(place, *refs):
+def stack_kernel(*refs):
     *held_refs, out_ref = refs
     for offset, ref in enumerate(held_refs):
-        out_ref[source(place[0], offset, len(held_refs))] = ref[...]
-
-
-def route_kernel(blocks_ref, place, mine_ref, other_ref, *refs):
-    *out_refs, held_ref = refs
+        out_ref[source(lax.axis_index("grp"), offset, len(held_refs))] = ref[...]
+
+
+def route_kernel(blocks_any, mine_ref, other_ref, *refs):
+    *out_refs, held_ref, blocks_ref, sem = refs
+    copy = pltpu.make_async_copy(blocks_any, blocks_ref, sem)
+    copy.start()
     chips = len(out_refs)
     groups, slots = mine_ref.shape[:2]
     per_device = slots - 1
     slabs = chips * CORES
-    group, slab = div_rem(place[0], slabs)
-    chip, core = div_rem(slab, CORES)
+    group = lax.axis_index("grp")
+    chip, core = div_rem(lax.axis_index("slab"), CORES)
     held_ref[core] = mine_ref[...]
     held_ref[1 - core] = other_ref[...]
     step = AVG // 2 // groups
@@ -194,6 +201,7 @@
             ends = jnp.where(lane >= owner_group * step, rolled, ends)
         for out_ref in out_refs:
             out_ref[per_device + owner_core] = ends.astype(BF16)
+    copy.wait()
     for offset, out_ref in enumerate(out_refs):
         wanted = (group * slabs + target(chip, offset, chips) * CORES + core) * per_device
         for slot in range(per_device):
@@ -202,21 +210,23 @@
             out_ref[slot] = held_ref[div_rem(owner_slab, CORES)[1], owner_group, index]
 
 
-def place_kernel(blocks_ref, place, *refs, groups, chips, blk):
-    (*got_refs, edge_ids_ref, edge_point_ref, edge_window_ref, _, table_ref, fluctuation_hbm, held_ref, ends_ref,
-     edge_ref, sems) = refs
+def place_kernel(blocks_any, *refs, groups, chips, blk):
+    (*got_refs, edge_ids_ref, edge_point_ref, edge_window_ref, _, table_hbm, fluctuation_hbm, held_ref, ends_ref,
+     edge_ref, table_ref, blocks_ref, sems) = refs
+    blocks_copy = pltpu.make_async_copy(blocks_any, blocks_ref, sems.at[3])
+    blocks_copy.start()
     slots = got_refs[0].shape[0]
     per_device = slots - CORES
     slabs = chips * CORES
     devices = groups * slabs
     grains = table_ref.shape[1]
     step = AVG // 2 // groups
-    device = place[0]
-    chip = div_rem(div_rem(device, slabs)[1], CORES)[0]
+    device = device_index()
+    chip = div_rem(lax.axis_index("slab"), CORES)[0]
     lane = lax.broadcasted_iota(jnp.int32, (8, AVG), 1)
     half = lane < blk
 
-    for offset, ref in enumerate(got_refs):
+    for offset, ref in enumerate(reversed(got_refs)):
         owner_chip = source(chip, offset, chips)
         held_ref[owner_chip] = ref[...]
         for core in range(CORES):
@@ -257,6 +267,7 @@
         )
         copies[-1].start()
 
+    blocks_copy.wait()
     tiles, columns = [], []
     sums = jnp.zeros((8, AVG), F32)
     for slot in range(per_device):
@@ -278,14 +289,14 @@
         lanes = slice(pair * AVG, (pair + 1) * AVG)
         table_ref[:8, lanes] = jnp.where(half, first, pltpu.roll(second, blk, 1))
         table_ref[8:, lanes] = jnp.where(half, pltpu.roll(first, blk, 1), second)[: COUNT - 8]
+    copies.append(pltpu.make_async_copy(table_ref, table_hbm, sems.at[2]))
+    copies[-1].start()
     for copy in copies:
         copy.wait()
 
 
 def local(grain_ids, orientation, stress, owner_blocks):
     groups, slabs = lax.axis_size("grp"), lax.axis_size("slab")
-    group = lax.axis_index("grp")
-    device = group * slabs + lax.axis_index("slab")
     points = grain_ids.shape[0]
     tiles = points // AVG
     grains = tiles
@@ -297,9 +308,7 @@
     ids = grain_ids.reshape(tiles, AVG)
     quads = orientation.reshape(4, tiles, AVG).transpose(1, 0, 2).reshape(4 * tiles, AVG)
     in_hbm = [pltpu.with_memory_space_constraint(x, pltpu.HBM) for x in (ids, quads, stress)]
-    place = device.astype(jnp.int32).reshape(1)
-    tile_base = place * tiles
-    smem = pl.BlockSpec(memory_space=pltpu.SMEM)
+    anywhere = pl.BlockSpec(memory_space=pl.ANY)
     vmem = pl.BlockSpec(memory_space=pltpu.VMEM)
     hbm = pl.BlockSpec(memory_space=pltpu.HBM)
     params = pltpu.CompilerParams(vmem_limit_bytes=20 << 20)
@@ -312,7 +321,7 @@
             jax.ShapeDtypeStruct((tiles // blk, ROWS, AVG), F32),
             jax.ShapeDtypeStruct((ROWS, points), F32),
         ],
-        in_specs=[smem, hbm, hbm, hbm],
+        in_specs=[hbm, hbm, hbm],
         out_specs=[vmem, vmem, vmem],
         scratch_shapes=[
             pltpu.VMEM((tiles, AVG), jnp.int32),
@@ -326,7 +335,7 @@
             flops=64 * points * ROWS, bytes_accessed=4 * points * ROWS, transcendentals=0
         ),
         name="sums",
-    )(tile_base, *in_hbm)
+    )(*in_hbm)
 
     held = [table]
     for offset in range(1, groups):
@@ -341,7 +350,7 @@
             jax.ShapeDtypeStruct((ROWS, 2 * EDGE * AVG), F32),
             jax.ShapeDtypeStruct((2, ROWS, AVG), F32),
         ],
-        in_specs=[smem, vmem, vmem, vmem],
+        in_specs=[vmem, vmem, vmem],
         out_specs=[hbm, vmem, vmem, vmem],
         scratch_shapes=[
             pltpu.VMEM((COUNT, points), BF16),
@@ -352,53 +361,59 @@
             flops=64 * points * ROWS, bytes_accessed=6 * points * ROWS, transcendentals=0
         ),
         name="fluctuation",
-    )(tile_base, ids, point, windows)
+    )(ids, point, windows)
 
     held, edge_ids = lax.optimization_barrier((held, edge_ids))
     mine = pl.pallas_call(
         stack_kernel,
         out_shape=jax.ShapeDtypeStruct((groups, slots, 8, AVG), BF16),
-        in_specs=[smem] + [vmem] * groups,
+        in_specs=[vmem] * groups,
         out_specs=vmem,
         compiler_params=params,
         name="stack",
-    )(group.astype(jnp.int32).reshape(1), *held)
+    )(*held)
     other = lax.ppermute(mine, "slab", [(s, s ^ 1) for s in range(slabs)])
     sent = pl.pallas_call(
         route_kernel,
         out_shape=[jax.ShapeDtypeStruct((per_device + CORES, 8, AVG), BF16)] * chips,
-        in_specs=[smem, smem, vmem, vmem],
+        in_specs=[anywhere, vmem, vmem],
         out_specs=[vmem] * chips,
-        scratch_shapes=[pltpu.VMEM((CORES, groups, slots, 8, AVG), BF16)],
+        scratch_shapes=[
+            pltpu.VMEM((CORES, groups, slots, 8, AVG), BF16),
+            pltpu.SMEM(owner_blocks.shape, jnp.int32),
+            pltpu.SemaphoreType.DMA,
+        ],
         compiler_params=params,
         name="route",
-    )(owner_blocks, place, mine, other)
+    )(owner_blocks, mine, other)
     got = [sent[0]]
-    for offset in range(1, chips):
+    for offset in reversed(range(1, chips)):
         moves = [
             (chip * CORES + core, int(target(chip, offset, chips)) * CORES + core)
             for chip in range(chips)
             for core in range(CORES)
         ]
-        got.append(lax.ppermute(sent[offset], "slab", moves))
+        got.insert(1, lax.ppermute(sent[offset], "slab", moves))
     grain_table, fluctuation = pl.pallas_call(
         functools.partial(place_kernel, groups=groups, chips=chips, blk=blk),
         out_shape=[
             jax.ShapeDtypeStruct((COUNT, grains), F32),
             jax.ShapeDtypeStruct((COUNT, points), BF16),
         ],
-        in_specs=[smem, smem] + [vmem] * (chips + 3) + [hbm],
-        out_specs=[vmem, hbm],
+        in_specs=[anywhere] + [vmem] * (chips + 3) + [hbm],
+        out_specs=[hbm, hbm],
         scratch_shapes=[
             pltpu.VMEM((chips, per_device + CORES, 8, AVG), BF16),
             pltpu.VMEM((slabs, 8, AVG), F32),
             pltpu.VMEM((COUNT, 2 * EDGE * AVG), BF16),
-            pltpu.SemaphoreType.DMA((2,)),
-        ],
-        input_output_aliases={chips + 5: 1},
+            pltpu.VMEM((COUNT, grains), F32),
+            pltpu.SMEM(owner_blocks.shape, jnp.int32),
+            pltpu.SemaphoreType.DMA((4,)),
+        ],
+        input_output_aliases={chips + 4: 1},
         compiler_params=params,
         name="place",
-    )(owner_blocks, place, *got, edge_ids, edge_point, edge_windows, fluctuation)
+    )(owner_blocks, *reversed(got), edge_ids, edge_point, edge_windows, fluctuation)
     return (grain_table, fluctuation)
 
 

time: 27.8 us -> 25 us (0.90)
  Pallas kernels: 10.5 us -> 7.92 us
    ppermute x3, waiting for transfers between devices: 5.36 us -> 3.89 us  [local(): got.insert(1, lax.ppermute(sent[offset], 'slab', moves))]
    pallas_call x1, Pallas kernels: 2.91 us -> 1.67 us  [local(): pl.pallas_call(fluctuation_kernel, out_shape=[jax.ShapeDtypeStruct((COUNT...]
    ppermute x3, waiting for transfers between devices: 0.7 us -> 1.94 us  [local(): held.append(lax.ppermute(table, 'grp', moves))]
    pallas_call x1, Pallas kernels: 4.72 us -> 3.9 us  [local(): pl.pallas_call(functools.partial(sum_kernel, chunks=chunks, blk=blk), out...]
    pallas_call x1, Pallas kernels: 2.2 us -> 1.67 us  [local(): pl.pallas_call(functools.partial(place_kernel, groups=groups, chips=chips...]
  transfers between devices with their start and end apart: 7 -> 7, of which waited for: 5 -> 5; matrix products, arithmetic and copies ran while one was open for 0% -> 0% of each run, Pallas kernels for 11% -> 7%
where the time goes in v4:
time: 25 us; the launch traced here: 24.9 us
  starting transfers between devices  9.16 us (37%)
  Pallas kernels  7.92 us (32%)
  waiting for transfers between devices  7.08 us (28%)
  between operations  0.7 us (3%)
    ppermute x3, starting transfers between devices, local(): held.append(lax.ppermute(table, 'grp', moves))  4.63 us
    ppermute x3, starting transfers between devices, local(): got.insert(1, lax.ppermute(sent[offset], 'slab', moves))  4.45 us
    pallas_call x1, Pallas kernels, local(): pl.pallas_call(functools.partial(sum_kernel, chunks=chunks, blk=blk), out...  3.9 us
    ppermute x3, waiting for transfers between devices, local(): got.insert(1, lax.ppermute(sent[offset], 'slab', moves))  3.89 us
    ppermute x3, waiting for transfers between devices, local(): held.append(lax.ppermute(table, 'grp', moves))  1.94 us
    pallas_call x1, Pallas kernels, local(): pl.pallas_call(functools.partial(place_kernel, groups=groups, chips=chips...  1.67 us
    pallas_call x1, Pallas kernels, local(): pl.pallas_call(fluctuation_kernel, out_shape=[jax.ShapeDtypeStruct((COUNT...  1.67 us
    ppermute x1, waiting for transfers between devices, local(): other = lax.ppermute(mine, 'slab', [(s, s ^ 1) for s in range(slabs)])  1.25 us
  transfers between devices with their start and end apart: 7, of which 5 were waited for; matrix products, arithmetic and copies ran while one was open for 0% of the time, Pallas kernels for 7%

profile of v4, /device:TPU:0, one launch (start us, length us, event | category | flops | bytes accessed | tf_op | source)
XLA Modules:
  0.0 24.9 jit_solution(6866086177085251097)
XLA Ops:
  0.6 0.0 copy-start
  0.6 0.0 copy-start.1
  0.7 3.9 %sums.1 = (bf16[9,8,128]{2,1,0:T(8,128)(2,1)S(1)}, f32[8,16,128]{2,1,0:T(8,128)S(1)}, f32[16,65536]{1,0:T(8,128)S(1)}) custom-call(s32[512,128]{1,0:T(8,128)} %bitcast.6, f32[2048,128]{1,0:T(8,128)} %bitcast.8, f32[9,65536]{1,0:T(8,128)} %s_hbm.1), custom_call_target="tpu_custom_call" | custom-call | flops 67108864 | bytes 4194304 | tf_op jit(solution)/shard_map/sums/pallas_call | solution.py:317
  4.6 4.0 %collective-permute-start.2 = (bf16[9,8,128]{2,1,0:T(8,128)(2,1)S(1)}, bf16[9,8,128]{2,1,0:T(8,128)(2,1)S(1)}, u32[]{:S(2)}, u32[]{:S(2)}) collective-permute-start(bf16[9,8,128]{2,1,0:T(8,128)(2,1)S(1)} %get-tuple-element.22.refs_0_), channel_id=1, source_target_pairs={{0,24},{8,16},{16,8},{24,0},{1,25},{9,17},{17,9},{25,1},{2,26},{10... | collective-permute-start | bytes 55304 | tf_op jit(solution)/shard_map/ppermute | solution.py:343
  8.5 0.5 %collective-permute-start.1 = (bf16[9,8,128]{2,1,0:T(8,128)(2,1)S(1)}, bf16[9,8,128]{2,1,0:T(8,128)(2,1)S(1)}, u32[]{:S(2)}, u32[]{:S(2)}) collective-permute-start(bf16[9,8,128]{2,1,0:T(8,128)(2,1)S(1)} %get-tuple-element.22.refs_0_), channel_id=1, source_target_pairs={{0,16},{8,24},{16,0},{24,8},{1,17},{9,25},{17,1},{25,9},{2,18},{10... | collective-permute-start | bytes 55304 | tf_op jit(solution)/shard_map/ppermute | solution.py:343
  9.1 0.1 collective-permute-start
  9.2 0.0 copy-done
  9.2 1.7 %fluctuation.1 = (bf16[13,65536]{1,0:T(8,128)(2,1)}, s32[4,128]{1,0:T(4,128)S(1)}, f32[16,512]{1,0:T(8,128)S(1)}, f32[2,16,128]{2,1,0:T(8,128)S(1)}) custom-call(s32[512,128]{1,0:T(8,128)S(1)} %bitcast.7, f32[16,65536]{1,0:T(8,128)S(1)} %get-tuple-element.19.point_ref, f32[8,16,128]{2,1,0:T(8,128)S(1)} %get-tuple-element.20.window_ref), custom_call_target="tpu_custom_call" | custom-call | flops 67108864 | bytes 6291456 | tf_op jit(solution)/shard_map/fluctuation/pallas_call | solution.py:345
  10.9 0.0 collective-permute-done.2.refs_3_
  10.9 1.4 %collective-permute-done.1.refs_2_ = bf16[9,8,128]{2,1,0:T(8,128)(2,1)S(1)} collective-permute-done((bf16[9,8,128]{2,1,0:T(8,128)(2,1)S(1)}, bf16[9,8,128]{2,1,0:T(8,128)(2,1)S(1)}, u32[]{:S(2)}, u32[]{:S(2)}) %collective-permute-start.1) | collective-permute-done | bytes 18464 | tf_op jit(solution)/shard_map/ppermute | solution.py:343
  12.3 0.5 %collective-permute-done.refs_1_ = bf16[9,8,128]{2,1,0:T(8,128)(2,1)S(1)} collective-permute-done((bf16[9,8,128]{2,1,0:T(8,128)(2,1)S(1)}, bf16[9,8,128]{2,1,0:T(8,128)(2,1)S(1)}, u32[]{:S(2)}, u32[]{:S(2)}) %collective-permute-start) | collective-permute-done | bytes 18464 | tf_op jit(solution)/shard_map/ppermute | solution.py:343
  12.8 0.1 collective-permute-start.3
  12.9 1.3 %collective-permute-done.3.other_ref = bf16[4,9,8,128]{3,2,1,0:T(8,128)(2,1)S(1)} collective-permute-done((bf16[4,9,8,128]{3,2,1,0:T(8,128)(2,1)S(1)}, bf16[4,9,8,128]{3,2,1,0:T(8,128)(2,1)S(1)}, u32[]{:S(2)}, u32[]{:S(2)}) %collective-permute-start.3) | collective-permute-done | bytes 73760 | tf_op jit(solution)/shard_map/ppermute | solution.py:375
  14.2 0.0 copy-done.1
  14.2 0.7 %route.1 = (bf16[10,8,128]{2,1,0:T(8,128)(2,1)S(1)}, bf16[10,8,128]{2,1,0:T(8,128)(2,1)S(1)}, bf16[10,8,128]{2,1,0:T(8,128)(2,1)S(1)}, bf16[10,8,128]{2,1,0:T(8,128)(2,1)S(1)}) custom-call(s32[256]{0:T(256)S(1)} %copy-done.1, bf16[4,9,8,128]{3,2,1,0:T(8,128)(2,1)S(1)} %stack.1.mine_ref, bf16[4,9,8,128]{3,2,1,0:T(8,128)(2,1)S(1)} %collective-permute-done.3.other_ref), custom_call_target="tpu_custom_call" | custom-call | tf_op jit(solution)/shard_map/route/pallas_call | solution.py:376
  14.8 3.7 %collective-permute-start.4 = (bf16[10,8,128]{2,1,0:T(8,128)(2,1)S(1)}, bf16[10,8,128]{2,1,0:T(8,128)(2,1)S(1)}, u32[]{:S(2)}, u32[]{:S(2)}) collective-permute-start(bf16[10,8,128]{2,1,0:T(8,128)(2,1)S(1)} %get-tuple-element.26), channel_id=1, source_target_pairs={{0,6},{1,7},{2,4},{3,5},{4,2},{5,3},{6,0},{7,1},{8,14},{9,15},{10,... | collective-permute-start | bytes 61448 | tf_op jit(solution)/shard_map/ppermute | solution.py:396
  18.5 0.0 collective-permute-start.5
  18.5 0.8 %collective-permute-start.6 = (bf16[10,8,128]{2,1,0:T(8,128)(2,1)S(1)}, bf16[10,8,128]{2,1,0:T(8,128)(2,1)S(1)}, u32[]{:S(2)}, u32[]{:S(2)}) collective-permute-start(bf16[10,8,128]{2,1,0:T(8,128)(2,1)S(1)} %get-tuple-element.28), channel_id=1, source_target_pairs={{0,2},{1,3},{2,0},{3,1},{4,6},{5,7},{6,4},{7,5},{8,10},{9,11},{10,... | collective-permute-start | bytes 61448 | tf_op jit(solution)/shard_map/ppermute | solution.py:396
  19.3 1.2 %collective-permute-done.4.refs_0_ = bf16[10,8,128]{2,1,0:T(8,128)(2,1)S(1)} collective-permute-done((bf16[10,8,128]{2,1,0:T(8,128)(2,1)S(1)}, bf16[10,8,128]{2,1,0:T(8,128)(2,1)S(1)}, u32[]{:S(2)}, u32[]{:S(2)}) %collective-permute-start.4) | collective-permute-done | bytes 20512 | tf_op jit(solution)/shard_map/ppermute | solution.py:396
  20.5 2.7 %collective-permute-done.5.refs_1_ = bf16[10,8,128]{2,1,0:T(8,128)(2,1)S(1)} collective-permute-done((bf16[10,8,128]{2,1,0:T(8,128)(2,1)S(1)}, bf16[10,8,128]{2,1,0:T(8,128)(2,1)S(1)}, u32[]{:S(2)}, u32[]{:S(2)}) %collective-permute-start.5) | collective-permute-done | bytes 20512 | tf_op jit(solution)/shard_map/ppermute | solution.py:396
  23.2 0.0 collective-permute-done.6.refs_2_
  23.2 1.7 %place.1 = (f32[13,512]{1,0:T(8,128)}, bf16[13,65536]{1,0:T(8,128)(2,1)}) custom-call(s32[256]{0:T(256)S(1)} %copy-done.1, bf16[10,8,128]{2,1,0:T(8,128)(2,1)S(1)} %collective-permute-done.4.refs_0_, bf16[10,8,128]{2,1,0:T(8,128)(2,1)S(1)} %collective-permute-done.5.refs_1_, ...), custom_call_target="tpu_custom_call", output_to_operand_aliasing={{1}: (8, {})} | custom-call | tf_op jit(solution)/shard_map/place/pallas_call | solution.py:397
  (1 shorter events, 0.0 us)
Async XLA Ops:
  0.6 8.6 %copy-start = (s32[65536]{0:T(1024)S(1)}, s32[65536]{0:T(1024)}, u32[]{:S(2)}) copy-start(s32[65536]{0:T(1024)} %param.4) | copy-start | bytes 786436
  0.6 13.5 %copy-start.1 = (s32[256]{0:T(256)S(1)}, s32[256]{0:T(256)}, u32[]{:S(2)}) copy-start(s32[256]{0:T(256)} %blocks_any.3) | copy-start | bytes 3076
  4.6 6.3 %collective-permute-start.2 = (bf16[9,8,128]{2,1,0:T(8,128)(2,1)S(1)}, bf16[9,8,128]{2,1,0:T(8,128)(2,1)S(1)}, u32[]{:S(2)}, u32[]{:S(2)}) collective-permute-start(bf16[9,8,128]{2,1,0:T(8,128)(2,1)S(1)} %get-tuple-element.22.refs_0_), channel_id=1, source_target_pairs={{0,24},{8,16},{16,8},{24,0},{1,25},{9,17},{17,9},{25,1},{2,26},{10... | collective-permute-start | bytes 55304 | tf_op jit(solution)/shard_map/ppermute | solution.py:343
  8.5 3.8 %collective-permute-start.1 = (bf16[9,8,128]{2,1,0:T(8,128)(2,1)S(1)}, bf16[9,8,128]{2,1,0:T(8,128)(2,1)S(1)}, u32[]{:S(2)}, u32[]{:S(2)}) collective-permute-start(bf16[9,8,128]{2,1,0:T(8,128)(2,1)S(1)} %get-tuple-element.22.refs_0_), channel_id=1, source_target_pairs={{0,16},{8,24},{16,0},{24,8},{1,17},{9,25},{17,1},{25,9},{2,18},{10... | collective-permute-start | bytes 55304 | tf_op jit(solution)/shard_map/ppermute | solution.py:343
  9.1 3.8 %collective-permute-start = (bf16[9,8,128]{2,1,0:T(8,128)(2,1)S(1)}, bf16[9,8,128]{2,1,0:T(8,128)(2,1)S(1)}, u32[]{:S(2)}, u32[]{:S(2)}) collective-permute-start(bf16[9,8,128]{2,1,0:T(8,128)(2,1)S(1)} %get-tuple-element.22.refs_0_), channel_id=1, source_target_pairs={{0,8},{8,0},{16,24},{24,16},{1,9},{9,1},{17,25},{25,17},{2,10},{10... | collective-permute-start | bytes 55304 | tf_op jit(solution)/shard_map/ppermute | solution.py:343
  12.8 1.3 %collective-permute-start.3 = (bf16[4,9,8,128]{3,2,1,0:T(8,128)(2,1)S(1)}, bf16[4,9,8,128]{3,2,1,0:T(8,128)(2,1)S(1)}, u32[]{:S(2)}, u32[]{:S(2)}) collective-permute-start(bf16[4,9,8,128]{3,2,1,0:T(8,128)(2,1)S(1)} %stack.1.mine_ref), channel_id=1, source_target_pairs={{0,1},{1,0},{2,3},{3,2},{4,5},{5,4},{6,7},{7,6},{8,9},{9,8},{10,11... | collective-permute-start | bytes 221192 | tf_op jit(solution)/shard_map/ppermute | solution.py:375
  14.8 5.6 %collective-permute-start.4 = (bf16[10,8,128]{2,1,0:T(8,128)(2,1)S(1)}, bf16[10,8,128]{2,1,0:T(8,128)(2,1)S(1)}, u32[]{:S(2)}, u32[]{:S(2)}) collective-permute-start(bf16[10,8,128]{2,1,0:T(8,128)(2,1)S(1)} %get-tuple-element.26), channel_id=1, source_target_pairs={{0,6},{1,7},{2,4},{3,5},{4,2},{5,3},{6,0},{7,1},{8,14},{9,15},{10,... | collective-permute-start | bytes 61448 | tf_op jit(solution)/shard_map/ppermute | solution.py:396
  18.5 4.7 %collective-permute-start.5 = (bf16[10,8,128]{2,1,0:T(8,128)(2,1)S(1)}, bf16[10,8,128]{2,1,0:T(8,128)(2,1)S(1)}, u32[]{:S(2)}, u32[]{:S(2)}) collective-permute-start(bf16[10,8,128]{2,1,0:T(8,128)(2,1)S(1)} %get-tuple-element.27), channel_id=1, source_target_pairs={{0,4},{1,5},{2,6},{3,7},{4,0},{5,1},{6,2},{7,3},{8,12},{9,13},{10,... | collective-permute-start | bytes 61448 | tf_op jit(solution)/shard_map/ppermute | solution.py:396
  18.5 4.7 %collective-permute-start.6 = (bf16[10,8,128]{2,1,0:T(8,128)(2,1)S(1)}, bf16[10,8,128]{2,1,0:T(8,128)(2,1)S(1)}, u32[]{:S(2)}, u32[]{:S(2)}) collective-permute-start(bf16[10,8,128]{2,1,0:T(8,128)(2,1)S(1)} %get-tuple-element.28), channel_id=1, source_target_pairs={{0,2},{1,3},{2,0},{3,1},{4,6},{5,7},{6,4},{7,5},{8,10},{9,11},{10,... | collective-permute-start | bytes 61448 | tf_op jit(solution)/shard_map/ppermute | solution.py:396

commit v5 on v4

v5 whole, which is shorter than its diff:
```python
import functools

import jax
import jax.numpy as jnp
from jax import lax
from jax.experimental import pallas as pl
from jax.experimental.pallas import tpu as pltpu
from jax.sharding import PartitionSpec as P

AVG = 128
AXES = ("grp", "slab")
SUB = 8
WINDOW = 16
ROWS = 16
COUNT = 13
CORES = 2
CUTS = (0, 1, 3, 5, 8)
EDGE = 2
F32 = jnp.float32
BF16 = jnp.bfloat16


def window_sums(selector, values):
    high = values.astype(BF16)
    low = (values - high.astype(F32)).astype(BF16)
    both = jnp.concatenate([high, low], axis=0)
    return lax.dot_general(selector, both, (((1,), (1,)), ((), ())), preferred_element_type=F32)


def finish(total):
    row = lax.broadcasted_iota(jnp.int32, total.shape, 0)
    squares = jnp.sum(jnp.where(row < 4, total * total, 0.0), axis=0, keepdims=True)
    scale = jnp.where(row < 4, jnp.sqrt(squares), total[COUNT : COUNT + 1])
    return total / jnp.where(scale > 0.0, scale, 1.0)


def device_index():
    return lax.axis_index("grp") * lax.axis_size("slab") + lax.axis_index("slab")


def div_rem(x, n):
    if n & (n - 1) == 0:
        return x >> (n.bit_length() - 1), x & (n - 1)
    return lax.div(x, n), lax.rem(x, n)


def selection(ids_ref, first_tile, tiles, first_grain):
    grain_row = lax.broadcasted_iota(jnp.int32, (WINDOW, AVG), 0) + first_grain
    picks = []
    for tile in range(tiles):
        ids = jnp.broadcast_to(ids_ref[pl.ds(first_tile + tile, 1), :], (WINDOW, AVG))
        picks.append((ids == grain_row).astype(F32).astype(BF16))
    return jnp.concatenate(picks, axis=1)


def sum_kernel(
    ids_hbm, q_hbm, s_hbm, table_ref, window_ref, ids_ref, q_ref, s_ref, acc_ref, sems, *, cuts, blk
):
    grains = ids_hbm.shape[0]
    tile_base = device_index() * grains
    chunks = list(zip(cuts[:-1], cuts[1:]))

    def copies(chunk):
        begin, end = chunks[chunk]
        rows, quads = slice(begin, end), slice(4 * begin, 4 * end)
        lanes = slice(begin * AVG, end * AVG)
        return (
            pltpu.make_async_copy(ids_hbm.at[rows], ids_ref.at[rows], sems.at[0, chunk]),
            pltpu.make_async_copy(q_hbm.at[quads], q_ref.at[quads], sems.at[1, chunk]),
            pltpu.make_async_copy(s_hbm.at[:, lanes], s_ref.at[:, lanes], sems.at[2, chunk]),
        )

    for chunk in range(len(chunks)):
        for copy in copies(chunk):
            copy.start()

    ones = jnp.ones((ROWS - COUNT, SUB * AVG), F32)
    carry = jnp.zeros((SUB, 2 * ROWS), F32)
    for chunk, (begin, end) in enumerate(chunks):
        for copy in copies(chunk):
            copy.wait()
        for tile in range(begin, end, SUB):
            values = jnp.concatenate([components(q_ref, s_ref, tile, SUB), ones], axis=0)
            sums = window_sums(selection(ids_ref, tile, SUB, tile_base + tile - 1), values)
            acc_ref[tile : tile + SUB, : 2 * ROWS] = carry + sums[:SUB]
            carry = sums[SUB:]
    acc_ref[grains : grains + SUB, : 2 * ROWS] = carry
    blocks = [acc_ref[block * AVG : (block + 1) * AVG, :].T for block in range(grains // AVG + 1)]
    part = jnp.concatenate([block[:ROWS] + block[ROWS : 2 * ROWS] for block in blocks], axis=1)
    rounded = finish(part).astype(BF16).astype(F32)
    own = rounded[:, 1 : 1 + grains]
    half = lax.broadcasted_iota(jnp.int32, (8, AVG), 1) < blk
    for pair in range(grains // AVG):
        top = own[:8, pair * AVG : (pair + 1) * AVG]
        low = own[8:, pair * AVG : (pair + 1) * AVG]
        table_ref[2 * pair] = jnp.where(half, top, pltpu.roll(low, blk, 1)).astype(BF16)
        table_ref[2 * pair + 1] = jnp.where(half, pltpu.roll(top, blk, 1), low).astype(BF16)
    lane = lax.broadcasted_iota(jnp.int32, (ROWS, AVG), 1)
    ends = jnp.where(lane < 2, part[:, :AVG], pltpu.roll(part[:, grains:], 2, 1))
    high = ends.astype(BF16).astype(F32)
    mid = (ends - high).astype(BF16).astype(F32)
    rest = ends - high - mid
    pieces = jnp.where(lane < 4, high, jnp.where(lane < 8, pltpu.roll(mid, 4, 1), pltpu.roll(rest, 8, 1)))
    pieces = jnp.where(lane < 12, pieces, 0.0)
    table_ref[grains // blk] = jnp.where(half, pieces[:8], pltpu.roll(pieces[8:], blk, 1)).astype(BF16)
    for index in range(window_ref.shape[0]):
        window_ref[index] = rounded[:, index * blk : index * blk + AVG]


def components(q_ref, s_ref, tile, tiles):
    q = [q_ref[4 * t : 4 * t + 4, :] for t in range(tile, tile + tiles)]
    return jnp.concatenate([jnp.concatenate(q, axis=1), s_ref[:, tile * AVG : (tile + tiles) * AVG]], axis=0)


def differences(ids_ref, q_ref, s_ref, table, tile, tiles, first_grain):
    picks = selection(ids_ref, tile, tiles, first_grain)
    means = jnp.dot(table[:, :WINDOW].astype(BF16), picks, preferred_element_type=F32)
    parts = [q_ref[pl.ds(4 * tile + c, tiles, stride=4), :] for c in range(4)]
    scale = lax.rsqrt(sum(part * part for part in parts))
    quaternion = lax.broadcasted_iota(jnp.int32, (8, AVG), 0) < 4
    scales = [jnp.where(quaternion, jnp.broadcast_to(scale[t : t + 1], (8, AVG)), 1.0) for t in range(tiles)]
    values = components(q_ref, s_ref, tile, tiles)
    values = jnp.concatenate([values[:8] * jnp.concatenate(scales, axis=1), values[8:]], axis=0)
    return (values - means[:COUNT]).astype(BF16)


def fluctuation_kernel(ids_ref, q_ref, s_ref, window_ref, *refs, begin, end):
    *_, out_hbm, out_ref, sems = refs
    total = ids_ref.shape[0]
    tile_base = device_index() * total
    tiles = total // window_ref.shape[0]

    def copy(window):
        lanes = slice(window * tiles * AVG, (window + 1) * tiles * AVG)
        local = slice((window - begin) * tiles * AVG, (window - begin + 1) * tiles * AVG)
        return pltpu.make_async_copy(out_ref.at[:, local], out_hbm.at[:, lanes], sems.at[window - begin])

    for window in range(begin, end):
        table = window_ref[window]
        for sub in range(tiles // SUB):
            tile = window * tiles + sub * SUB
            near = pltpu.roll(table, (AVG - sub * SUB) % AVG, 1)
            local = tile - begin * tiles
            out_ref[:, local * AVG : (local + SUB) * AVG] = differences(
                ids_ref, q_ref, s_ref, near, tile, SUB, tile_base + tile - 1
            )
        copy(window).start()
    for window in range(begin, end):
        copy(window).wait()


def stack_kernel(mine_ref, other_ref, out_ref, *, bit):
    upper = (lax.axis_index("grp") // bit) & 1
    out_ref[upper] = mine_ref[...]
    out_ref[1 - upper] = other_ref[...]


def route_kernel(blocks_any, mine_ref, other_ref, *refs):
    *out_refs, held_ref, blocks_ref, sem = refs
    copy = pltpu.make_async_copy(blocks_any, blocks_ref, sem)
    copy.start()
    chips = len(out_refs)
    groups, slots = mine_ref.shape[:2]
    per_device = slots - 1
    slabs = chips * CORES
    group = lax.axis_index("grp")
    chip, core = div_rem(lax.axis_index("slab"), CORES)
    held_ref[core] = mine_ref[...]
    held_ref[1 - core] = other_ref[...]
    step = AVG // 2 // groups
    lane = lax.broadcasted_iota(jnp.int32, (8, AVG), 1) & (AVG // 2 - 1)
    for owner_core in range(CORES):
        ends = held_ref[owner_core, 0, per_device].astype(F32)
        for owner_group in range(1, groups):
            rolled = pltpu.roll(held_ref[owner_core, owner_group, per_device].astype(F32), owner_group * step, 1)
            ends = jnp.where(lane >= owner_group * step, rolled, ends)
        for out_ref in out_refs:
            out_ref[per_device + owner_core] = ends.astype(BF16)
    copy.wait()
    for offset, out_ref in enumerate(out_refs):
        wanted = (group * slabs + (chip ^ offset) * CORES + core) * per_device
        for slot in range(per_device):
            owner, index = div_rem(blocks_ref[wanted + slot], per_device)
            owner_group, owner_slab = div_rem(owner, slabs)
            out_ref[slot] = held_ref[div_rem(owner_slab, CORES)[1], owner_group, index]


def place_kernel(blocks_any, *refs, groups, chips, blk):
    (*got_refs, ids_ref, q_ref, s_ref, window_ref, _, table_hbm, fluctuation_hbm, held_ref, ends_ref,
     edge_ref, table_ref, blocks_ref, sems) = refs
    blocks_copy = pltpu.make_async_copy(blocks_any, blocks_ref, sems.at[3])
    blocks_copy.start()
    slots = got_refs[0].shape[0]
    per_device = slots - CORES
    slabs = chips * CORES
    devices = groups * slabs
    grains = table_ref.shape[1]
    step = AVG // 2 // groups
    device = device_index()
    chip = div_rem(lax.axis_index("slab"), CORES)[0]
    lane = lax.broadcasted_iota(jnp.int32, (8, AVG), 1)
    half = lane < blk

    for offset, ref in enumerate(reversed(got_refs)):
        owner_chip = chip ^ offset
        held_ref[owner_chip] = ref[...]
        for core in range(CORES):
            piece = ref[per_device + core].astype(F32)
            piece = piece + pltpu.roll(piece, AVG - 4, 1) + pltpu.roll(piece, AVG - 8, 1)
            ends_ref[owner_chip * CORES + core] = piece

    def ends(owner, column, lane):
        group, slab = div_rem(jnp.clip(owner, 0, devices - 1), slabs)
        moved = pltpu.roll(ends_ref[slab], (lane - column - step * group + 2 * AVG) & (AVG - 1), 1)
        return jnp.where((owner >= 0) & (owner < devices), moved, 0.0)

    def unfold(value):
        return jnp.concatenate([value, pltpu.roll(value, blk, 1)], axis=0)

    lane_half = lane & (blk - 1)
    others = jnp.where(lane_half < 2, ends(device - 1, 2, 0), ends(device + 1, 0, 2))
    shared = finish(unfold(ends(device, 0, 0) + others))
    wide_lane = lax.broadcasted_iota(jnp.int32, (ROWS, AVG), 1)
    windows = window_ref.shape[0]
    first = jnp.where(wide_lane < 2, shared, window_ref[0])
    in_last = (wide_lane >= SUB) & (wide_lane < SUB + 2)
    last = pltpu.roll(window_ref[windows - 1], AVG - grains // windows + SUB, 1)
    last = jnp.where(in_last, pltpu.roll(shared, SUB - 2, 1), last)
    width = EDGE * AVG
    first_grain = device * grains - 1
    copies = []
    for end, (table, tile, grain) in enumerate(
        ((first, 0, first_grain), (last, grains - EDGE, first_grain + grains - SUB))
    ):
        lanes = slice(end * width, (end + 1) * width)
        edge_ref[:, lanes] = differences(ids_ref, q_ref, s_ref, table, tile, EDGE, grain)
        points = slice(tile * AVG, tile * AVG + width)
        copies.append(pltpu.make_async_copy(edge_ref.at[:, lanes], fluctuation_hbm.at[:, points], sems.at[end]))
        copies[-1].start()

    blocks_copy.wait()
    tiles, columns = [], []
    sums = jnp.zeros((8, AVG), F32)
    for slot in range(per_device):
        owner, index = div_rem(blocks_ref[device * per_device + slot], per_device)
        owner_chip = div_rem(div_rem(owner, slabs)[1], CORES)[0]
        tiles.append(held_ref[owner_chip, slot].astype(F32))
        low = index == 0
        beside = jnp.where(low, owner - 1, owner + 1)
        both = ends(owner, jnp.where(low, 1, 2), slot) + ends(beside, jnp.where(low, 3, 0), slot)
        sums = jnp.where(lane_half == slot, both, sums)
        columns.append(jnp.where(low, 0, jnp.where(index == per_device - 1, blk - 1, 2 * AVG)))
    repaired = finish(unfold(sums))
    repaired = jnp.where(half, repaired[:8], pltpu.roll(repaired[8:], blk, 1))
    for slot in range(per_device):
        moved = pltpu.roll(repaired, (columns[slot] - slot + AVG) & (AVG - 1), 1)
        tiles[slot] = jnp.where(lane_half == columns[slot], moved, tiles[slot])
    for pair in range(per_device // 2):
        first, second = tiles[2 * pair], tiles[2 * pair + 1]
        lanes = slice(pair * AVG, (pair + 1) * AVG)
        table_ref[:8, lanes] = jnp.where(half, first, pltpu.roll(second, blk, 1))
        table_ref[8:, lanes] = jnp.where(half, pltpu.roll(first, blk, 1), second)[: COUNT - 8]
    copies.append(pltpu.make_async_copy(table_ref, table_hbm, sems.at[2]))
    copies[-1].start()
    for copy in copies:
        copy.wait()


def local(grain_ids, orientation, stress, owner_blocks):
    groups, slabs = lax.axis_size("grp"), lax.axis_size("slab")
    points = grain_ids.shape[0]
    tiles = points // AVG
    grains = tiles
    per_device = owner_blocks.shape[0] // (groups * slabs)
    blk = grains // per_device
    slots = per_device + 1
    chips = slabs // CORES

    ids = grain_ids.reshape(tiles, AVG)
    quads = orientation.reshape(4, tiles, AVG).transpose(1, 0, 2).reshape(4 * tiles, AVG)
    in_hbm = [pltpu.with_memory_space_constraint(x, pltpu.HBM) for x in (ids, quads, stress)]
    anywhere = pl.BlockSpec(memory_space=pl.ANY)
    vmem = pl.BlockSpec(memory_space=pltpu.VMEM)
    hbm = pl.BlockSpec(memory_space=pltpu.HBM)
    params = pltpu.CompilerParams(vmem_limit_bytes=20 << 20)

    cuts = [tiles * part // 8 for part in CUTS]
    windows = tiles // blk
    table, means, ids, q, s = pl.pallas_call(
        functools.partial(sum_kernel, cuts=cuts, blk=blk),
        out_shape=[
            jax.ShapeDtypeStruct((slots, 8, AVG), BF16),
            jax.ShapeDtypeStruct((windows, ROWS, AVG), F32),
            jax.ShapeDtypeStruct((tiles, AVG), jnp.int32),
            jax.ShapeDtypeStruct((4 * tiles, AVG), F32),
            jax.ShapeDtypeStruct((9, points), F32),
        ],
        in_specs=[hbm, hbm, hbm],
        out_specs=[vmem] * 5,
        scratch_shapes=[
            pltpu.VMEM((grains + AVG, AVG), F32),
            pltpu.SemaphoreType.DMA((3, len(cuts) - 1)),
        ],
        compiler_params=params,
        cost_estimate=pl.CostEstimate(
            flops=64 * points * ROWS, bytes_accessed=4 * points * ROWS, transcendentals=0
        ),
        name="sums",
    )(*in_hbm)
    on_chip = (ids, q, s, means)

    def look_up(begin, end, earlier):
        share = (end - begin) * points // windows
        return pl.pallas_call(
            functools.partial(fluctuation_kernel, begin=begin, end=end),
            out_shape=jax.ShapeDtypeStruct((COUNT, points), BF16),
            in_specs=[vmem] * 4 + [hbm] * len(earlier),
            out_specs=hbm,
            scratch_shapes=[pltpu.VMEM((COUNT, share), BF16), pltpu.SemaphoreType.DMA((end - begin,))],
            input_output_aliases={4: 0} if earlier else {},
            compiler_params=params,
            cost_estimate=pl.CostEstimate(
                flops=64 * share * ROWS, bytes_accessed=6 * share * ROWS, transcendentals=0
            ),
            name="fluctuation",
        )(*on_chip, *earlier)

    stages = [("grp", 1 << bit) for bit in range((groups - 1).bit_length())] + [("slab", 1)]
    held = table[None]
    fluctuation = []
    for stage, (axis, bit) in enumerate(stages):
        size = lax.axis_size(axis)
        other = lax.ppermute(held, axis, [(member, member ^ bit) for member in range(size)])
        begin, end = (windows * step // len(stages) for step in (stage, stage + 1))
        fluctuation = [look_up(begin, end, fluctuation)]
        other, fluctuation = lax.optimization_barrier((other, fluctuation))
        if axis == "grp":
            held = pl.pallas_call(
                functools.partial(stack_kernel, bit=bit),
                out_shape=jax.ShapeDtypeStruct((2, *held.shape), BF16),
                in_specs=[vmem, vmem],
                out_specs=vmem,
                compiler_params=params,
                name="stack",
            )(held, other).reshape(-1, slots, 8, AVG)
    sent = pl.pallas_call(
        route_kernel,
        out_shape=[jax.ShapeDtypeStruct((per_device + CORES, 8, AVG), BF16)] * chips,
        in_specs=[anywhere, vmem, vmem],
        out_specs=[vmem] * chips,
        scratch_shapes=[
            pltpu.VMEM((CORES, groups, slots, 8, AVG), BF16),
            pltpu.SMEM(owner_blocks.shape, jnp.int32),
            pltpu.SemaphoreType.DMA,
        ],
        compiler_params=params,
        name="route",
    )(owner_blocks, held, other)
    got = [sent[0]]
    for offset in reversed(range(1, chips)):
        moves = [
            (chip * CORES + core, (chip ^ offset) * CORES + core)
            for chip in range(chips)
            for core in range(CORES)
        ]
        got.insert(1, lax.ppermute(sent[offset], "slab", moves))
    grain_table, fluctuation = pl.pallas_call(
        functools.partial(place_kernel, groups=groups, chips=chips, blk=blk),
        out_shape=[
            jax.ShapeDtypeStruct((COUNT, grains), F32),
            jax.ShapeDtypeStruct((COUNT, points), BF16),
        ],
        in_specs=[anywhere] + [vmem] * (chips + 4) + [hbm],
        out_specs=[hbm, hbm],
        scratch_shapes=[
            pltpu.VMEM((chips, per_device + CORES, 8, AVG), BF16),
            pltpu.VMEM((slabs, 8, AVG), F32),
            pltpu.VMEM((COUNT, 2 * EDGE * AVG), BF16),
            pltpu.VMEM((COUNT, grains), F32),
            pltpu.SMEM(owner_blocks.shape, jnp.int32),
            pltpu.SemaphoreType.DMA((4,)),
        ],
        input_output_aliases={chips + 5: 1},
        compiler_params=params,
        name="place",
    )(owner_blocks, *reversed(got), *on_chip, *fluctuation)
    return (grain_table, fluctuation)


def solution(mesh):
    placed = (P(AXES), P(None, AXES), P(None, AXES), P())
    return jax.shard_map(
        local,
        mesh=mesh,
        in_specs=placed,
        out_specs=(P(None, AXES), P(None, AXES)),
        check_vma=False,
    )
```

time: 25 us -> 26 us (1.040)
  Pallas kernels: 7.92 us -> 9.87 us
  waiting for transfers between devices: 7.08 us -> 5.3 us
  starting transfers between devices: 9.16 us -> 9.96 us
    ppermute x4 -> x3, waiting for transfers between devices: 3.19 us -> 1.26 us  [local(): lax.ppermute(held, axis, [(member, member ^ bit) for member in range(size)])]
    pallas_call x3 -> x6, Pallas kernels: 5.58 us -> 7.3 us  [the longest x3 3.69 us: look_up(): pl.pallas_call(functools.partial(fluctuation_kernel, begin=begin, end=end...]
    ppermute x4 -> x3, starting transfers between devices: 4.7 us -> 5.15 us  [local(): lax.ppermute(held, axis, [(member, member ^ bit) for member in range(size)])]
    ppermute x3, starting transfers between devices: 4.45 us -> 4.81 us  [local(): got.insert(1, lax.ppermute(sent[offset], 'slab', moves))]
  transfers between devices with their start and end apart: 7 -> 6, of which waited for: 5 -> 4; matrix products, arithmetic and copies ran while one was open for 0% -> 0% of each run, Pallas kernels for 7% -> 14%
where the time goes in v5:
time: 26 us; the launch traced here: 25.8 us
  starting transfers between devices  9.96 us (38%)
  Pallas kernels  9.87 us (38%)
  waiting for transfers between devices  5.3 us (20%)
  between operations  0.71 us (3%)
    ppermute x3, starting transfers between devices, local(): lax.ppermute(held, axis, [(member, member ^ bit) for member in range(size)])  5.15 us
    ppermute x3, starting transfers between devices, local(): got.insert(1, lax.ppermute(sent[offset], 'slab', moves))  4.81 us
    ppermute x3, waiting for transfers between devices, local(): got.insert(1, lax.ppermute(sent[offset], 'slab', moves))  4.04 us
    pallas_call x3, Pallas kernels, look_up(): pl.pallas_call(functools.partial(fluctuation_kernel, begin=begin, end=end...  3.69 us
    pallas_call x1, Pallas kernels, local(): pl.pallas_call(functools.partial(sum_kernel, cuts=cuts, blk=blk), out_sha...  3.6 us
    pallas_call x1, Pallas kernels, local(): pl.pallas_call(functools.partial(place_kernel, groups=groups, chips=chips...  1.88 us
    ppermute x3, waiting for transfers between devices, local(): lax.ppermute(held, axis, [(member, member ^ bit) for member in range(size)])  1.26 us
    pallas_call x1, Pallas kernels, local(): pl.pallas_call(route_kernel, out_shape=[jax.ShapeDtypeStruct((per_device...  0.68 us
  transfers between devices with their start and end apart: 6, of which 4 were waited for; matrix products, arithmetic and copies ran while one was open for 0% of the time, Pallas kernels for 14%

profile of v5, /device:TPU:0, one launch (start us, length us, event | category | flops | bytes accessed | tf_op | source)
XLA Modules:
  0.0 25.8 jit_solution(17562196949741217111)
XLA Ops:
  0.6 3.6 %sums.1 = (bf16[9,8,128]{2,1,0:T(8,128)(2,1)S(1)}, f32[8,16,128]{2,1,0:T(8,128)S(1)}, s32[512,128]{1,0:T(8,128)S(1)}, f32[2048,128]{1,0:T(8,128)S(1)}, f32[9,65536]{1,0:T(8,128)S(1)}) custom-call(s32[512,128]{1,0:T(8,128)} %bitcast.16, f32[2048,128]{1,0:T(8,128)} %bitcast.15, f32[9,65536]{1,0:T(8,128)} %s_hbm.1), custom_call_target="tpu_custom_call" | custom-call | flops 67108864 | bytes 4194304 | tf_op jit(solution)/shard_map/sums/pallas_call | solution.py:289
  4.2 3.0 %collective-permute-start = (bf16[1,9,8,128]{3,2,1,0:T(8,128)(2,1)S(1)}, bf16[1,9,8,128]{3,2,1,0:T(8,128)(2,1)S(1)}, u32[]{:S(2)}, u32[]{:S(2)}) collective-permute-start(bf16[1,9,8,128]{3,2,1,0:T(8,128)(2,1)S(1)} %bitcast.13), channel_id=1, source_target_pairs={{0,8},{8,0},{16,24},{24,16},{1,9},{9,1},{17,25},{25,17},{2,10},{10... | collective-permute-start | bytes 55304 | tf_op jit(solution)/shard_map/ppermute | solution.py:333
  7.3 1.1 %fluctuation.3.refs_0_ = bf16[13,65536]{1,0:T(8,128)(2,1)} custom-call(s32[512,128]{1,0:T(8,128)S(1)} %get-tuple-element.18.ids_ref.refs_4_, f32[2048,128]{1,0:T(8,128)S(1)} %get-tuple-element.19.q_ref.refs_5_, f32[9,65536]{1,0:T(8,128)S(1)} %get-tuple-element.20.s_ref.refs_6_, f32[8,16,128]{2,1,0:T(8,128)S(1)} %get-tuple-element.21.window_ref.refs_7_), custom_call_target="tpu_custom_call" | custom-call | flops 16777216 | bytes 1572864 | tf_op jit(solution)/shard_map/fluctuation/pallas_call | solution.py:314
  8.4 0.6 %collective-permute-done.other_ref = bf16[1,9,8,128]{3,2,1,0:T(8,128)(2,1)S(1)} collective-permute-done((bf16[1,9,8,128]{3,2,1,0:T(8,128)(2,1)S(1)}, bf16[1,9,8,128]{3,2,1,0:T(8,128)(2,1)S(1)}, u32[]{:S(2)}, u32[]{:S(2)}) %collective-permute-start) | collective-permute-done | bytes 18464 | tf_op jit(solution)/shard_map/ppermute | solution.py:333
  9.0 2.0 %collective-permute-start.1 = (bf16[2,9,8,128]{3,2,1,0:T(8,128)(2,1)S(1)}, bf16[2,9,8,128]{3,2,1,0:T(8,128)(2,1)S(1)}, u32[]{:S(2)}, u32[]{:S(2)}) collective-permute-start(bf16[2,9,8,128]{3,2,1,0:T(8,128)(2,1)S(1)} %bitcast.11), channel_id=1, source_target_pairs={{0,16},{8,24},{16,0},{24,8},{1,17},{9,25},{17,1},{25,9},{2,18},{10... | collective-permute-start | bytes 110600 | tf_op jit(solution)/shard_map/ppermute | solution.py:333
  11.1 1.3 %fluctuation.4.refs_0_ = bf16[13,65536]{1,0:T(8,128)(2,1)} custom-call(s32[512,128]{1,0:T(8,128)S(1)} %get-tuple-element.18.ids_ref.refs_4_, f32[2048,128]{1,0:T(8,128)S(1)} %get-tuple-element.19.q_ref.refs_5_, f32[9,65536]{1,0:T(8,128)S(1)} %get-tuple-element.20.s_ref.refs_6_, ...), custom_call_target="tpu_custom_call", output_to_operand_aliasing={{}: (4, {})} | custom-call | flops 25165824 | bytes 2359296 | tf_op jit(solution)/shard_map/fluctuation/pallas_call | solution.py:314
  12.4 0.6 %collective-permute-done.1.other_ref = bf16[2,9,8,128]{3,2,1,0:T(8,128)(2,1)S(1)} collective-permute-done((bf16[2,9,8,128]{3,2,1,0:T(8,128)(2,1)S(1)}, bf16[2,9,8,128]{3,2,1,0:T(8,128)(2,1)S(1)}, u32[]{:S(2)}, u32[]{:S(2)}) %collective-permute-start.1) | collective-permute-done | bytes 36896 | tf_op jit(solution)/shard_map/ppermute | solution.py:333
  13.0 0.0 copy-start
  13.0 0.1 collective-permute-start.2
  13.1 1.3 %fluctuation.5.refs_8_ = bf16[13,65536]{1,0:T(8,128)(2,1)} custom-call(s32[512,128]{1,0:T(8,128)S(1)} %get-tuple-element.18.ids_ref.refs_4_, f32[2048,128]{1,0:T(8,128)S(1)} %get-tuple-element.19.q_ref.refs_5_, f32[9,65536]{1,0:T(8,128)S(1)} %get-tuple-element.20.s_ref.refs_6_, ...), custom_call_target="tpu_custom_call", output_to_operand_aliasing={{}: (4, {})} | custom-call | flops 25165824 | bytes 2359296 | tf_op jit(solution)/shard_map/fluctuation/pallas_call | solution.py:314
  14.4 0.0 collective-permute-done.2.other_ref
  14.4 0.0 copy-done
  14.4 0.7 %route.1 = (bf16[10,8,128]{2,1,0:T(8,128)(2,1)S(1)}, bf16[10,8,128]{2,1,0:T(8,128)(2,1)S(1)}, bf16[10,8,128]{2,1,0:T(8,128)(2,1)S(1)}, bf16[10,8,128]{2,1,0:T(8,128)(2,1)S(1)}) custom-call(s32[256]{0:T(256)S(1)} %copy-done, bf16[4,9,8,128]{3,2,1,0:T(8,128)(2,1)S(1)} %bitcast.10, bf16[4,9,8,128]{3,2,1,0:T(8,128)(2,1)S(1)} %collective-permute-done.2.other_ref), custom_call_target="tpu_custom_call" | custom-call | tf_op jit(solution)/shard_map/route/pallas_call | solution.py:346
  15.1 4.2 %collective-permute-start.3 = (bf16[10,8,128]{2,1,0:T(8,128)(2,1)S(1)}, bf16[10,8,128]{2,1,0:T(8,128)(2,1)S(1)}, u32[]{:S(2)}, u32[]{:S(2)}) collective-permute-start(bf16[10,8,128]{2,1,0:T(8,128)(2,1)S(1)} %get-tuple-element.27), channel_id=1, source_target_pairs={{0,6},{1,7},{2,4},{3,5},{4,2},{5,3},{6,0},{7,1},{8,14},{9,15},{10,... | collective-permute-start | bytes 61448 | tf_op jit(solution)/shard_map/ppermute | solution.py:366
  19.3 0.0 collective-permute-start.4
  19.3 0.6 %collective-permute-start.5 = (bf16[10,8,128]{2,1,0:T(8,128)(2,1)S(1)}, bf16[10,8,128]{2,1,0:T(8,128)(2,1)S(1)}, u32[]{:S(2)}, u32[]{:S(2)}) collective-permute-start(bf16[10,8,128]{2,1,0:T(8,128)(2,1)S(1)} %get-tuple-element.29), channel_id=1, source_target_pairs={{0,2},{1,3},{2,0},{3,1},{4,6},{5,7},{6,4},{7,5},{8,10},{9,11},{10,... | collective-permute-start | bytes 61448 | tf_op jit(solution)/shard_map/ppermute | solution.py:366
  19.9 1.1 %collective-permute-done.3.refs_0_ = bf16[10,8,128]{2,1,0:T(8,128)(2,1)S(1)} collective-permute-done((bf16[10,8,128]{2,1,0:T(8,128)(2,1)S(1)}, bf16[10,8,128]{2,1,0:T(8,128)(2,1)S(1)}, u32[]{:S(2)}, u32[]{:S(2)}) %collective-permute-start.3) | collective-permute-done | bytes 20512 | tf_op jit(solution)/shard_map/ppermute | solution.py:366
  21.1 2.9 %collective-permute-done.4.refs_1_ = bf16[10,8,128]{2,1,0:T(8,128)(2,1)S(1)} collective-permute-done((bf16[10,8,128]{2,1,0:T(8,128)(2,1)S(1)}, bf16[10,8,128]{2,1,0:T(8,128)(2,1)S(1)}, u32[]{:S(2)}, u32[]{:S(2)}) %collective-permute-start.4) | collective-permute-done | bytes 20512 | tf_op jit(solution)/shard_map/ppermute | solution.py:366
  24.0 0.0 collective-permute-done.5.refs_2_
  24.0 1.9 %place.1 = (f32[13,512]{1,0:T(8,128)}, bf16[13,65536]{1,0:T(8,128)(2,1)}) custom-call(s32[256]{0:T(256)S(1)} %copy-done, bf16[10,8,128]{2,1,0:T(8,128)(2,1)S(1)} %collective-permute-done.3.refs_0_, bf16[10,8,128]{2,1,0:T(8,128)(2,1)S(1)} %collective-permute-done.4.refs_1_, ...), custom_call_target="tpu_custom_call", output_to_operand_aliasing={{1}: (9, {})} | custom-call | tf_op jit(solution)/shard_map/place/pallas_call | solution.py:367
  (2 shorter events, 0.0 us)
Async XLA Ops:
  4.2 4.8 %collective-permute-start = (bf16[1,9,8,128]{3,2,1,0:T(8,128)(2,1)S(1)}, bf16[1,9,8,128]{3,2,1,0:T(8,128)(2,1)S(1)}, u32[]{:S(2)}, u32[]{:S(2)}) collective-permute-start(bf16[1,9,8,128]{3,2,1,0:T(8,128)(2,1)S(1)} %bitcast.13), channel_id=1, source_target_pairs={{0,8},{8,0},{16,24},{24,16},{1,9},{9,1},{17,25},{25,17},{2,10},{10... | collective-permute-start | bytes 55304 | tf_op jit(solution)/shard_map/ppermute | solution.py:333
  9.0 4.0 %collective-permute-start.1 = (bf16[2,9,8,128]{3,2,1,0:T(8,128)(2,1)S(1)}, bf16[2,9,8,128]{3,2,1,0:T(8,128)(2,1)S(1)}, u32[]{:S(2)}, u32[]{:S(2)}) collective-permute-start(bf16[2,9,8,128]{3,2,1,0:T(8,128)(2,1)S(1)} %bitcast.11), channel_id=1, source_target_pairs={{0,16},{8,24},{16,0},{24,8},{1,17},{9,25},{17,1},{25,9},{2,18},{10... | collective-permute-start | bytes 110600 | tf_op jit(solution)/shard_map/ppermute | solution.py:333
  13.0 1.4 %copy-start = (s32[256]{0:T(256)S(1)}, s32[256]{0:T(256)}, u32[]{:S(2)}) copy-start(s32[256]{0:T(256)} %blocks_any.3) | copy-start | bytes 3076
  13.0 1.4 %collective-permute-start.2 = (bf16[4,9,8,128]{3,2,1,0:T(8,128)(2,1)S(1)}, bf16[4,9,8,128]{3,2,1,0:T(8,128)(2,1)S(1)}, u32[]{:S(2)}, u32[]{:S(2)}) collective-permute-start(bf16[4,9,8,128]{3,2,1,0:T(8,128)(2,1)S(1)} %bitcast.9), channel_id=1, source_target_pairs={{0,1},{1,0},{2,3},{3,2},{4,5},{5,4},{6,7},{7,6},{8,9},{9,8},{10,11... | collective-permute-start | bytes 221192 | tf_op jit(solution)/shard_map/ppermute | solution.py:333
  15.1 6.0 %collective-permute-start.3 = (bf16[10,8,128]{2,1,0:T(8,128)(2,1)S(1)}, bf16[10,8,128]{2,1,0:T(8,128)(2,1)S(1)}, u32[]{:S(2)}, u32[]{:S(2)}) collective-permute-start(bf16[10,8,128]{2,1,0:T(8,128)(2,1)S(1)} %get-tuple-element.27), channel_id=1, source_target_pairs={{0,6},{1,7},{2,4},{3,5},{4,2},{5,3},{6,0},{7,1},{8,14},{9,15},{10,... | collective-permute-start | bytes 61448 | tf_op jit(solution)/shard_map/ppermute | solution.py:366
  19.3 4.7 %collective-permute-start.4 = (bf16[10,8,128]{2,1,0:T(8,128)(2,1)S(1)}, bf16[10,8,128]{2,1,0:T(8,128)(2,1)S(1)}, u32[]{:S(2)}, u32[]{:S(2)}) collective-permute-start(bf16[10,8,128]{2,1,0:T(8,128)(2,1)S(1)} %get-tuple-element.28), channel_id=1, source_target_pairs={{0,4},{1,5},{2,6},{3,7},{4,0},{5,1},{6,2},{7,3},{8,12},{9,13},{10,... | collective-permute-start | bytes 61448 | tf_op jit(solution)/shard_map/ppermute | solution.py:366
  19.3 4.7 %collective-permute-start.5 = (bf16[10,8,128]{2,1,0:T(8,128)(2,1)S(1)}, bf16[10,8,128]{2,1,0:T(8,128)(2,1)S(1)}, u32[]{:S(2)}, u32[]{:S(2)}) collective-permute-start(bf16[10,8,128]{2,1,0:T(8,128)(2,1)S(1)} %get-tuple-element.29), channel_id=1, source_target_pairs={{0,2},{1,3},{2,0},{3,1},{4,6},{5,7},{6,4},{7,5},{8,10},{9,11},{10,... | collective-permute-start | bytes 61448 | tf_op jit(solution)/shard_map/ppermute | solution.py:366

commit v6 on v4

--- a/solution.py
+++ b/solution.py
@@ -14,6 +14,7 @@
 ROWS = 16
 COUNT = 13
 CORES = 2
+CUTS = (0, 1, 2, 3, 4)
 EDGE = 2
 F32 = jnp.float32
 BF16 = jnp.bfloat16
@@ -53,55 +54,47 @@
 
 
 def sum_kernel(
-    ids_hbm, q_hbm, s_hbm, table_ref, window_ref, point_ref, ids_ref, q_ref, s_ref, acc_ref, sems,
-    *, chunks, blk,
+    ids_hbm, q_hbm, s_hbm, table_ref, window_ref, point_ref, ids_ref, q_ref, s_ref, acc_ref, sems, *, cuts, blk
 ):
-    tiles = ids_hbm.shape[0] // chunks
-    points = tiles * AVG
-    grains = chunks * tiles
+    grains = ids_hbm.shape[0]
     tile_base = device_index() * grains
+    chunks = list(zip(cuts[:-1], cuts[1:]))
 
     def copies(chunk):
-        rows = pl.ds(chunk * tiles, tiles)
-        quads = pl.ds(chunk * tiles * 4, tiles * 4)
-        lanes = pl.ds(chunk * points, points)
+        begin, end = chunks[chunk]
+        rows, quads = slice(begin, end), slice(4 * begin, 4 * end)
+        lanes = slice(begin * AVG, end * AVG)
         return (
             pltpu.make_async_copy(ids_hbm.at[rows], ids_ref.at[rows], sems.at[0, chunk]),
             pltpu.make_async_copy(q_hbm.at[quads], q_ref.at[quads], sems.at[1, chunk]),
             pltpu.make_async_copy(s_hbm.at[:, lanes], s_ref.at[:, lanes], sems.at[2, chunk]),
         )
 
-    for chunk in range(chunks):
+    for chunk in range(len(chunks)):
         for copy in copies(chunk):
             copy.start()
 
     quaternion = lax.broadcasted_iota(jnp.int32, (8, AVG), 0) < 4
     ones = jnp.ones((ROWS - COUNT, SUB * AVG), F32)
 
-    def step(chunk, carry):
+    carry = jnp.zeros((SUB, 2 * ROWS), F32)
+    for chunk, (begin, end) in enumerate(chunks):
         for copy in copies(chunk):
             copy.wait()
-        for sub in range(tiles // SUB):
-            tile = chunk * tiles + sub * SUB
-            lanes = pl.ds(tile * AVG, SUB * AVG)
-            quad = tile * 4
-            q = jnp.concatenate([q_ref[pl.ds(quad + 4 * t, 4), :] for t in range(SUB)], axis=1)
+        for tile in range(begin, end, SUB):
+            lanes = slice(tile * AVG, (tile + SUB) * AVG)
+            q = jnp.concatenate([q_ref[4 * t : 4 * t + 4, :] for t in range(tile, tile + SUB)], axis=1)
             values = jnp.concatenate([q, s_ref[:, lanes], ones], axis=0)
             sums = window_sums(selection(ids_ref, tile, SUB, tile_base + tile - 1), values)
-            acc_ref[pl.ds(tile, SUB), : 2 * ROWS] = carry + sums[:SUB]
+            acc_ref[tile : tile + SUB, : 2 * ROWS] = carry + sums[:SUB]
             carry = sums[SUB:]
-            parts = [q_ref[pl.ds(quad + c, SUB, stride=4), :] for c in range(4)]
+            parts = [q_ref[pl.ds(4 * tile + c, SUB, stride=4), :] for c in range(4)]
             scale = lax.rsqrt(sum(part * part for part in parts))
             scales = [
                 jnp.where(quaternion, jnp.broadcast_to(scale[t : t + 1], (8, AVG)), 1.0) for t in range(SUB)
             ]
             point_ref[:8, lanes] = values[:8] * jnp.concatenate(scales, axis=1)
             point_ref[8:, lanes] = values[8:]
-        return carry
-
-    carry = jnp.zeros((SUB, 2 * ROWS), F32)
-    for chunk in range(chunks):
-        carry = step(chunk, carry)
     acc_ref[grains : grains + SUB, : 2 * ROWS] = carry
     blocks = [acc_ref[block * AVG : (block + 1) * AVG, :].T for block in range(grains // AVG + 1)]
     part = jnp.concatenate([block[:ROWS] + block[ROWS : 2 * ROWS] for block in blocks], axis=1)
@@ -313,9 +306,9 @@
     hbm = pl.BlockSpec(memory_space=pltpu.HBM)
     params = pltpu.CompilerParams(vmem_limit_bytes=20 << 20)
 
-    chunks = 8
+    cuts = [tiles * part // CUTS[-1] for part in CUTS]
     table, windows, point = pl.pallas_call(
-        functools.partial(sum_kernel, chunks=chunks, blk=blk),
+        functools.partial(sum_kernel, cuts=cuts, blk=blk),
         out_shape=[
             jax.ShapeDtypeStruct((slots, 8, AVG), BF16),
             jax.ShapeDtypeStruct((tiles // blk, ROWS, AVG), F32),
@@ -328,7 +321,7 @@
             pltpu.VMEM((4 * tiles, AVG), F32),
             pltpu.VMEM((9, points), F32),
             pltpu.VMEM((grains + AVG, AVG), F32),
-            pltpu.SemaphoreType.DMA((3, chunks)),
+            pltpu.SemaphoreType.DMA((3, len(cuts) - 1)),
         ],
         compiler_params=params,
         cost_estimate=pl.CostEstimate(

time: 25 us -> 24.6 us (0.984)
  Pallas kernels: 7.92 us -> 7.52 us
    pallas_call x1, Pallas kernels: 3.9 us -> 3.5 us  [local(): pl.pallas_call(functools.partial(sum_kernel, cuts=cuts, blk=blk), out_sha...]
where the time goes in v6:
time: 24.6 us; the launch traced here: 24.5 us
  starting transfers between devices  9.15 us (37%)
  Pallas kernels  7.52 us (31%)
  waiting for transfers between devices  7.1 us (29%)
  between operations  0.7 us (3%)
    ppermute x3, starting transfers between devices, local(): held.append(lax.ppermute(table, 'grp', moves))  4.63 us
    ppermute x3, starting transfers between devices, local(): got.insert(1, lax.ppermute(sent[offset], 'slab', moves))  4.45 us
    ppermute x3, waiting for transfers between devices, local(): got.insert(1, lax.ppermute(sent[offset], 'slab', moves))  3.9 us
    pallas_call x1, Pallas kernels, local(): pl.pallas_call(functools.partial(sum_kernel, cuts=cuts, blk=blk), out_sha...  3.5 us
    ppermute x3, waiting for transfers between devices, local(): held.append(lax.ppermute(table, 'grp', moves))  1.95 us
    pallas_call x1, Pallas kernels, local(): pl.pallas_call(functools.partial(place_kernel, groups=groups, chips=chips...  1.67 us
    pallas_call x1, Pallas kernels, local(): pl.pallas_call(fluctuation_kernel, out_shape=[jax.ShapeDtypeStruct((COUNT...  1.66 us
    ppermute x1, waiting for transfers between devices, local(): other = lax.ppermute(mine, 'slab', [(s, s ^ 1) for s in range(slabs)])  1.25 us
  transfers between devices with their start and end apart: 7, of which 5 were waited for; matrix products, arithmetic and copies ran while one was open for 0% of the time, Pallas kernels for 7%

profile of v6, /device:TPU:0, one launch (start us, length us, event | category | flops | bytes accessed | tf_op | source)
XLA Modules:
  0.0 24.5 jit_solution(1159109828130303110)
XLA Ops:
  0.6 0.0 copy-start
  0.6 0.0 copy-start.1
  0.7 3.5 %sums.1 = (bf16[9,8,128]{2,1,0:T(8,128)(2,1)S(1)}, f32[8,16,128]{2,1,0:T(8,128)S(1)}, f32[16,65536]{1,0:T(8,128)S(1)}) custom-call(s32[512,128]{1,0:T(8,128)} %bitcast.6, f32[2048,128]{1,0:T(8,128)} %bitcast.8, f32[9,65536]{1,0:T(8,128)} %s_hbm.1), custom_call_target="tpu_custom_call" | custom-call | flops 67108864 | bytes 4194304 | tf_op jit(solution)/shard_map/sums/pallas_call | solution.py:310
  4.2 4.0 %collective-permute-start.2 = (bf16[9,8,128]{2,1,0:T(8,128)(2,1)S(1)}, bf16[9,8,128]{2,1,0:T(8,128)(2,1)S(1)}, u32[]{:S(2)}, u32[]{:S(2)}) collective-permute-start(bf16[9,8,128]{2,1,0:T(8,128)(2,1)S(1)} %get-tuple-element.22.refs_0_), channel_id=1, source_target_pairs={{0,24},{8,16},{16,8},{24,0},{1,25},{9,17},{17,9},{25,1},{2,26},{10... | collective-permute-start | bytes 55304 | tf_op jit(solution)/shard_map/ppermute | solution.py:336
  8.1 0.5 %collective-permute-start.1 = (bf16[9,8,128]{2,1,0:T(8,128)(2,1)S(1)}, bf16[9,8,128]{2,1,0:T(8,128)(2,1)S(1)}, u32[]{:S(2)}, u32[]{:S(2)}) collective-permute-start(bf16[9,8,128]{2,1,0:T(8,128)(2,1)S(1)} %get-tuple-element.22.refs_0_), channel_id=1, source_target_pairs={{0,16},{8,24},{16,0},{24,8},{1,17},{9,25},{17,1},{25,9},{2,18},{10... | collective-permute-start | bytes 55304 | tf_op jit(solution)/shard_map/ppermute | solution.py:336
  8.6 0.1 collective-permute-start
  8.8 0.0 copy-done
  8.8 1.7 %fluctuation.1 = (bf16[13,65536]{1,0:T(8,128)(2,1)}, s32[4,128]{1,0:T(4,128)S(1)}, f32[16,512]{1,0:T(8,128)S(1)}, f32[2,16,128]{2,1,0:T(8,128)S(1)}) custom-call(s32[512,128]{1,0:T(8,128)S(1)} %bitcast.7, f32[16,65536]{1,0:T(8,128)S(1)} %get-tuple-element.19.point_ref, f32[8,16,128]{2,1,0:T(8,128)S(1)} %get-tuple-element.20.window_ref), custom_call_target="tpu_custom_call" | custom-call | flops 67108864 | bytes 6291456 | tf_op jit(solution)/shard_map/fluctuation/pallas_call | solution.py:338
  10.5 0.0 collective-permute-done.2.refs_3_
  10.5 1.4 %collective-permute-done.1.refs_2_ = bf16[9,8,128]{2,1,0:T(8,128)(2,1)S(1)} collective-permute-done((bf16[9,8,128]{2,1,0:T(8,128)(2,1)S(1)}, bf16[9,8,128]{2,1,0:T(8,128)(2,1)S(1)}, u32[]{:S(2)}, u32[]{:S(2)}) %collective-permute-start.1) | collective-permute-done | bytes 18464 | tf_op jit(solution)/shard_map/ppermute | solution.py:336
  11.9 0.5 %collective-permute-done.refs_1_ = bf16[9,8,128]{2,1,0:T(8,128)(2,1)S(1)} collective-permute-done((bf16[9,8,128]{2,1,0:T(8,128)(2,1)S(1)}, bf16[9,8,128]{2,1,0:T(8,128)(2,1)S(1)}, u32[]{:S(2)}, u32[]{:S(2)}) %collective-permute-start) | collective-permute-done | bytes 18464 | tf_op jit(solution)/shard_map/ppermute | solution.py:336
  12.4 0.1 collective-permute-start.3
  12.5 1.3 %collective-permute-done.3.other_ref = bf16[4,9,8,128]{3,2,1,0:T(8,128)(2,1)S(1)} collective-permute-done((bf16[4,9,8,128]{3,2,1,0:T(8,128)(2,1)S(1)}, bf16[4,9,8,128]{3,2,1,0:T(8,128)(2,1)S(1)}, u32[]{:S(2)}, u32[]{:S(2)}) %collective-permute-start.3) | collective-permute-done | bytes 73760 | tf_op jit(solution)/shard_map/ppermute | solution.py:368
  13.8 0.0 copy-done.1
  13.8 0.7 %route.1 = (bf16[10,8,128]{2,1,0:T(8,128)(2,1)S(1)}, bf16[10,8,128]{2,1,0:T(8,128)(2,1)S(1)}, bf16[10,8,128]{2,1,0:T(8,128)(2,1)S(1)}, bf16[10,8,128]{2,1,0:T(8,128)(2,1)S(1)}) custom-call(s32[256]{0:T(256)S(1)} %copy-done.1, bf16[4,9,8,128]{3,2,1,0:T(8,128)(2,1)S(1)} %stack.1.mine_ref, bf16[4,9,8,128]{3,2,1,0:T(8,128)(2,1)S(1)} %collective-permute-done.3.other_ref), custom_call_target="tpu_custom_call" | custom-call | tf_op jit(solution)/shard_map/route/pallas_call | solution.py:369
  14.4 3.7 %collective-permute-start.4 = (bf16[10,8,128]{2,1,0:T(8,128)(2,1)S(1)}, bf16[10,8,128]{2,1,0:T(8,128)(2,1)S(1)}, u32[]{:S(2)}, u32[]{:S(2)}) collective-permute-start(bf16[10,8,128]{2,1,0:T(8,128)(2,1)S(1)} %get-tuple-element.26), channel_id=1, source_target_pairs={{0,6},{1,7},{2,4},{3,5},{4,2},{5,3},{6,0},{7,1},{8,14},{9,15},{10,... | collective-permute-start | bytes 61448 | tf_op jit(solution)/shard_map/ppermute | solution.py:389
  18.1 0.0 collective-permute-start.5
  18.1 0.8 %collective-permute-start.6 = (bf16[10,8,128]{2,1,0:T(8,128)(2,1)S(1)}, bf16[10,8,128]{2,1,0:T(8,128)(2,1)S(1)}, u32[]{:S(2)}, u32[]{:S(2)}) collective-permute-start(bf16[10,8,128]{2,1,0:T(8,128)(2,1)S(1)} %get-tuple-element.28), channel_id=1, source_target_pairs={{0,2},{1,3},{2,0},{3,1},{4,6},{5,7},{6,4},{7,5},{8,10},{9,11},{10,... | collective-permute-start | bytes 61448 | tf_op jit(solution)/shard_map/ppermute | solution.py:389
  18.9 1.2 %collective-permute-done.4.refs_0_ = bf16[10,8,128]{2,1,0:T(8,128)(2,1)S(1)} collective-permute-done((bf16[10,8,128]{2,1,0:T(8,128)(2,1)S(1)}, bf16[10,8,128]{2,1,0:T(8,128)(2,1)S(1)}, u32[]{:S(2)}, u32[]{:S(2)}) %collective-permute-start.4) | collective-permute-done | bytes 20512 | tf_op jit(solution)/shard_map/ppermute | solution.py:389
  20.1 2.7 %collective-permute-done.5.refs_1_ = bf16[10,8,128]{2,1,0:T(8,128)(2,1)S(1)} collective-permute-done((bf16[10,8,128]{2,1,0:T(8,128)(2,1)S(1)}, bf16[10,8,128]{2,1,0:T(8,128)(2,1)S(1)}, u32[]{:S(2)}, u32[]{:S(2)}) %collective-permute-start.5) | collective-permute-done | bytes 20512 | tf_op jit(solution)/shard_map/ppermute | solution.py:389
  22.8 0.0 collective-permute-done.6.refs_2_
  22.8 1.7 %place.1 = (f32[13,512]{1,0:T(8,128)}, bf16[13,65536]{1,0:T(8,128)(2,1)}) custom-call(s32[256]{0:T(256)S(1)} %copy-done.1, bf16[10,8,128]{2,1,0:T(8,128)(2,1)S(1)} %collective-permute-done.4.refs_0_, bf16[10,8,128]{2,1,0:T(8,128)(2,1)S(1)} %collective-permute-done.5.refs_1_, ...), custom_call_target="tpu_custom_call", output_to_operand_aliasing={{1}: (8, {})} | custom-call | tf_op jit(solution)/shard_map/place/pallas_call | solution.py:390
  (1 shorter events, 0.0 us)
Async XLA Ops:
  0.6 8.2 %copy-start = (s32[65536]{0:T(1024)S(1)}, s32[65536]{0:T(1024)}, u32[]{:S(2)}) copy-start(s32[65536]{0:T(1024)} %param.4) | copy-start | bytes 786436
  0.6 13.1 %copy-start.1 = (s32[256]{0:T(256)S(1)}, s32[256]{0:T(256)}, u32[]{:S(2)}) copy-start(s32[256]{0:T(256)} %blocks_any.3) | copy-start | bytes 3076
  4.2 6.3 %collective-permute-start.2 = (bf16[9,8,128]{2,1,0:T(8,128)(2,1)S(1)}, bf16[9,8,128]{2,1,0:T(8,128)(2,1)S(1)}, u32[]{:S(2)}, u32[]{:S(2)}) collective-permute-start(bf16[9,8,128]{2,1,0:T(8,128)(2,1)S(1)} %get-tuple-element.22.refs_0_), channel_id=1, source_target_pairs={{0,24},{8,16},{16,8},{24,0},{1,25},{9,17},{17,9},{25,1},{2,26},{10... | collective-permute-start | bytes 55304 | tf_op jit(solution)/shard_map/ppermute | solution.py:336
  8.1 3.8 %collective-permute-start.1 = (bf16[9,8,128]{2,1,0:T(8,128)(2,1)S(1)}, bf16[9,8,128]{2,1,0:T(8,128)(2,1)S(1)}, u32[]{:S(2)}, u32[]{:S(2)}) collective-permute-start(bf16[9,8,128]{2,1,0:T(8,128)(2,1)S(1)} %get-tuple-element.22.refs_0_), channel_id=1, source_target_pairs={{0,16},{8,24},{16,0},{24,8},{1,17},{9,25},{17,1},{25,9},{2,18},{10... | collective-permute-start | bytes 55304 | tf_op jit(solution)/shard_map/ppermute | solution.py:336
  8.6 3.8 %collective-permute-start = (bf16[9,8,128]{2,1,0:T(8,128)(2,1)S(1)}, bf16[9,8,128]{2,1,0:T(8,128)(2,1)S(1)}, u32[]{:S(2)}, u32[]{:S(2)}) collective-permute-start(bf16[9,8,128]{2,1,0:T(8,128)(2,1)S(1)} %get-tuple-element.22.refs_0_), channel_id=1, source_target_pairs={{0,8},{8,0},{16,24},{24,16},{1,9},{9,1},{17,25},{25,17},{2,10},{10... | collective-permute-start | bytes 55304 | tf_op jit(solution)/shard_map/ppermute | solution.py:336
  12.4 1.3 %collective-permute-start.3 = (bf16[4,9,8,128]{3,2,1,0:T(8,128)(2,1)S(1)}, bf16[4,9,8,128]{3,2,1,0:T(8,128)(2,1)S(1)}, u32[]{:S(2)}, u32[]{:S(2)}) collective-permute-start(bf16[4,9,8,128]{3,2,1,0:T(8,128)(2,1)S(1)} %stack.1.mine_ref), channel_id=1, source_target_pairs={{0,1},{1,0},{2,3},{3,2},{4,5},{5,4},{6,7},{7,6},{8,9},{9,8},{10,11... | collective-permute-start | bytes 221192 | tf_op jit(solution)/shard_map/ppermute | solution.py:368
  14.4 5.6 %collective-permute-start.4 = (bf16[10,8,128]{2,1,0:T(8,128)(2,1)S(1)}, bf16[10,8,128]{2,1,0:T(8,128)(2,1)S(1)}, u32[]{:S(2)}, u32[]{:S(2)}) collective-permute-start(bf16[10,8,128]{2,1,0:T(8,128)(2,1)S(1)} %get-tuple-element.26), channel_id=1, source_target_pairs={{0,6},{1,7},{2,4},{3,5},{4,2},{5,3},{6,0},{7,1},{8,14},{9,15},{10,... | collective-permute-start | bytes 61448 | tf_op jit(solution)/shard_map/ppermute | solution.py:389
  18.1 4.7 %collective-permute-start.5 = (bf16[10,8,128]{2,1,0:T(8,128)(2,1)S(1)}, bf16[10,8,128]{2,1,0:T(8,128)(2,1)S(1)}, u32[]{:S(2)}, u32[]{:S(2)}) collective-permute-start(bf16[10,8,128]{2,1,0:T(8,128)(2,1)S(1)} %get-tuple-element.27), channel_id=1, source_target_pairs={{0,4},{1,5},{2,6},{3,7},{4,0},{5,1},{6,2},{7,3},{8,12},{9,13},{10,... | collective-permute-start | bytes 61448 | tf_op jit(solution)/shard_map/ppermute | solution.py:389
  18.1 4.7 %collective-permute-start.6 = (bf16[10,8,128]{2,1,0:T(8,128)(2,1)S(1)}, bf16[10,8,128]{2,1,0:T(8,128)(2,1)S(1)}, u32[]{:S(2)}, u32[]{:S(2)}) collective-permute-start(bf16[10,8,128]{2,1,0:T(8,128)(2,1)S(1)} %get-tuple-element.28), channel_id=1, source_target_pairs={{0,2},{1,3},{2,0},{3,1},{4,6},{5,7},{6,4},{7,5},{8,10},{9,11},{10,... | collective-permute-start | bytes 61448 | tf_op jit(solution)/shard_map/ppermute | solution.py:389

commit v7 on v6

--- a/solution.py
+++ b/solution.py
@@ -54,7 +54,8 @@
 
 
 def sum_kernel(
-    ids_hbm, q_hbm, s_hbm, table_ref, window_ref, point_ref, ids_ref, q_ref, s_ref, acc_ref, sems, *, cuts, blk
+    ids_hbm, q_hbm, s_hbm, blocks_any, table_ref, window_ref, point_ref, blocks_ref, ids_ref, q_ref, s_ref, acc_ref,
+    sems, blocks_sem, *, cuts, blk,
 ):
     grains = ids_hbm.shape[0]
     tile_base = device_index() * grains
@@ -73,6 +74,8 @@
     for chunk in range(len(chunks)):
         for copy in copies(chunk):
             copy.start()
+    blocks_copy = pltpu.make_async_copy(blocks_any, blocks_ref, blocks_sem)
+    blocks_copy.start()
 
     quaternion = lax.broadcasted_iota(jnp.int32, (8, AVG), 0) < 4
     ones = jnp.ones((ROWS - COUNT, SUB * AVG), F32)
@@ -95,6 +98,7 @@
             ]
             point_ref[:8, lanes] = values[:8] * jnp.concatenate(scales, axis=1)
             point_ref[8:, lanes] = values[8:]
+    blocks_copy.wait()
     acc_ref[grains : grains + SUB, : 2 * ROWS] = carry
     blocks = [acc_ref[block * AVG : (block + 1) * AVG, :].T for block in range(grains // AVG + 1)]
     part = jnp.concatenate([block[:ROWS] + block[ROWS : 2 * ROWS] for block in blocks], axis=1)
@@ -173,10 +177,8 @@
         out_ref[source(lax.axis_index("grp"), offset, len(held_refs))] = ref[...]
 
 
-def route_kernel(blocks_any, mine_ref, other_ref, *refs):
-    *out_refs, held_ref, blocks_ref, sem = refs
-    copy = pltpu.make_async_copy(blocks_any, blocks_ref, sem)
-    copy.start()
+def route_kernel(blocks_ref, mine_ref, other_ref, *refs):
+    *out_refs, held_ref = refs
     chips = len(out_refs)
     groups, slots = mine_ref.shape[:2]
     per_device = slots - 1
@@ -194,7 +196,6 @@
             ends = jnp.where(lane >= owner_group * step, rolled, ends)
         for out_ref in out_refs:
             out_ref[per_device + owner_core] = ends.astype(BF16)
-    copy.wait()
     for offset, out_ref in enumerate(out_refs):
         wanted = (group * slabs + target(chip, offset, chips) * CORES + core) * per_device
         for slot in range(per_device):
@@ -203,11 +204,9 @@
             out_ref[slot] = held_ref[div_rem(owner_slab, CORES)[1], owner_group, index]
 
 
-def place_kernel(blocks_any, *refs, groups, chips, blk):
+def place_kernel(blocks_ref, *refs, groups, chips, blk):
     (*got_refs, edge_ids_ref, edge_point_ref, edge_window_ref, _, table_hbm, fluctuation_hbm, held_ref, ends_ref,
-     edge_ref, table_ref, blocks_ref, sems) = refs
-    blocks_copy = pltpu.make_async_copy(blocks_any, blocks_ref, sems.at[3])
-    blocks_copy.start()
+     edge_ref, table_ref, sems) = refs
     slots = got_refs[0].shape[0]
     per_device = slots - CORES
     slabs = chips * CORES
@@ -260,7 +259,6 @@
         )
         copies[-1].start()
 
-    blocks_copy.wait()
     tiles, columns = [], []
     sums = jnp.zeros((8, AVG), F32)
     for slot in range(per_device):
@@ -302,33 +300,37 @@
     quads = orientation.reshape(4, tiles, AVG).transpose(1, 0, 2).reshape(4 * tiles, AVG)
     in_hbm = [pltpu.with_memory_space_constraint(x, pltpu.HBM) for x in (ids, quads, stress)]
     anywhere = pl.BlockSpec(memory_space=pl.ANY)
+    smem = pl.BlockSpec(memory_space=pltpu.SMEM)
     vmem = pl.BlockSpec(memory_space=pltpu.VMEM)
     hbm = pl.BlockSpec(memory_space=pltpu.HBM)
     params = pltpu.CompilerParams(vmem_limit_bytes=20 << 20)
 
     cuts = [tiles * part // CUTS[-1] for part in CUTS]
-    table, windows, point = pl.pallas_call(
+    table, windows, point, blocks = pl.pallas_call(
         functools.partial(sum_kernel, cuts=cuts, blk=blk),
         out_shape=[
             jax.ShapeDtypeStruct((slots, 8, AVG), BF16),
             jax.ShapeDtypeStruct((tiles // blk, ROWS, AVG), F32),
             jax.ShapeDtypeStruct((ROWS, points), F32),
-        ],
-        in_specs=[hbm, hbm, hbm],
-        out_specs=[vmem, vmem, vmem],
+            pltpu.SMEM(owner_blocks.shape, jnp.int32),
+        ],
+        in_specs=[hbm, hbm, hbm, anywhere],
+        out_specs=[vmem, vmem, vmem, smem],
         scratch_shapes=[
             pltpu.VMEM((tiles, AVG), jnp.int32),
             pltpu.VMEM((4 * tiles, AVG), F32),
             pltpu.VMEM((9, points), F32),
             pltpu.VMEM((grains + AVG, AVG), F32),
             pltpu.SemaphoreType.DMA((3, len(cuts) - 1)),
+            pltpu.SemaphoreType.DMA,
         ],
         compiler_params=params,
         cost_estimate=pl.CostEstimate(
             flops=64 * points * ROWS, bytes_accessed=4 * points * ROWS, transcendentals=0
         ),
         name="sums",
-    )(*in_hbm)
+    )(*in_hbm, owner_blocks)
+    blocks = pltpu.with_memory_space_constraint(blocks, pltpu.SMEM)
 
     held = [table]
     for offset in range(1, groups):
@@ -369,16 +371,12 @@
     sent = pl.pallas_call(
         route_kernel,
         out_shape=[jax.ShapeDtypeStruct((per_device + CORES, 8, AVG), BF16)] * chips,
-        in_specs=[anywhere, vmem, vmem],
+        in_specs=[smem, vmem, vmem],
         out_specs=[vmem] * chips,
-        scratch_shapes=[
-            pltpu.VMEM((CORES, groups, slots, 8, AVG), BF16),
-            pltpu.SMEM(owner_blocks.shape, jnp.int32),
-            pltpu.SemaphoreType.DMA,
-        ],
+        scratch_shapes=[pltpu.VMEM((CORES, groups, slots, 8, AVG), BF16)],
         compiler_params=params,
         name="route",
-    )(owner_blocks, mine, other)
+    )(blocks, mine, other)
     got = [sent[0]]
     for offset in reversed(range(1, chips)):
         moves = [
@@ -393,20 +391,19 @@
             jax.ShapeDtypeStruct((COUNT, grains), F32),
             jax.ShapeDtypeStruct((COUNT, points), BF16),
         ],
-        in_specs=[anywhere] + [vmem] * (chips + 3) + [hbm],
+        in_specs=[smem] + [vmem] * (chips + 3) + [hbm],
         out_specs=[hbm, hbm],
         scratch_shapes=[
             pltpu.VMEM((chips, per_device + CORES, 8, AVG), BF16),
             pltpu.VMEM((slabs, 8, AVG), F32),
             pltpu.VMEM((COUNT, 2 * EDGE * AVG), BF16),
             pltpu.VMEM((COUNT, grains), F32),
-            pltpu.SMEM(owner_blocks.shape, jnp.int32),
-            pltpu.SemaphoreType.DMA((4,)),
+            pltpu.SemaphoreType.DMA((3,)),
         ],
         input_output_aliases={chips + 4: 1},
         compiler_params=params,
         name="place",
-    )(owner_blocks, *reversed(got), edge_ids, edge_point, edge_windows, fluctuation)
+    )(blocks, *reversed(got), edge_ids, edge_point, edge_windows, fluctuation)
     return (grain_table, fluctuation)
 
 

time: 24.6 us -> 24.3 us (0.988)
  Pallas kernels: 7.52 us -> 6.45 us
  local copies, waits for them, and re-layouts: 0.01 us -> 0.72 us
    unnamed x4, local copies, waits for them, and re-layouts: 0.01 us -> 0.72 us
    pallas_call x1, Pallas kernels: 0.68 us -> 0.12 us  [local(): pl.pallas_call(route_kernel, out_shape=[jax.ShapeDtypeStruct((per_device...]
    pallas_call x1, Pallas kernels: 1.67 us -> 1.17 us  [local(): pl.pallas_call(functools.partial(place_kernel, groups=groups, chips=chips...]
where the time goes in v7:
time: 24.3 us; the launch traced here: 24.1 us
  starting transfers between devices  9.15 us (38%)
  waiting for transfers between devices  7.1 us (29%)
  Pallas kernels  6.45 us (27%)
  local copies, waits for them, and re-layouts  0.72 us (3%)
  between operations  0.7 us (3%)
    ppermute x3, starting transfers between devices, local(): held.append(lax.ppermute(table, 'grp', moves))  4.63 us
    ppermute x3, starting transfers between devices, local(): got.insert(1, lax.ppermute(sent[offset], 'slab', moves))  4.45 us
    ppermute x3, waiting for transfers between devices, local(): got.insert(1, lax.ppermute(sent[offset], 'slab', moves))  3.9 us
    pallas_call x1, Pallas kernels, local(): pl.pallas_call(functools.partial(sum_kernel, cuts=cuts, blk=blk), out_sha...  3.5 us
    ppermute x3, waiting for transfers between devices, local(): held.append(lax.ppermute(table, 'grp', moves))  1.95 us
    pallas_call x1, Pallas kernels, local(): pl.pallas_call(fluctuation_kernel, out_shape=[jax.ShapeDtypeStruct((COUNT...  1.66 us
    ppermute x1, waiting for transfers between devices, local(): other = lax.ppermute(mine, 'slab', [(s, s ^ 1) for s in range(slabs)])  1.25 us
    pallas_call x1, Pallas kernels, local(): pl.pallas_call(functools.partial(place_kernel, groups=groups, chips=chips...  1.17 us
  transfers between devices with their start and end apart: 7, of which 5 were waited for; matrix products, arithmetic and copies ran while one was open for 0% of the time, Pallas kernels for 7%

profile of v7, /device:TPU:0, one launch (start us, length us, event | category | flops | bytes accessed | tf_op | source)
XLA Modules:
  0.0 24.1 jit_solution(15649727239421055255)
XLA Ops:
  0.6 0.0 copy-start
  0.6 0.0 copy-start.1
  0.7 0.7 %copy-done.1 = s32[256]{0:T(256)S(1)} copy-done((s32[256]{0:T(256)S(1)}, s32[256]{0:T(256)}, u32[]{:S(2)}) %copy-start.1) | copy-done | bytes 1048
  1.4 3.5 %sums.1 = (bf16[9,8,128]{2,1,0:T(8,128)(2,1)S(1)}, f32[8,16,128]{2,1,0:T(8,128)S(1)}, f32[16,65536]{1,0:T(8,128)S(1)}, s32[256]{0:T(256)S(4)}) custom-call(s32[512,128]{1,0:T(8,128)} %bitcast.6, f32[2048,128]{1,0:T(8,128)} %bitcast.8, f32[9,65536]{1,0:T(8,128)} %s_hbm.1, s32[256]{0:T(256)S(1)} %copy-done.1), custom_call_target="tpu_custom_call" | custom-call | flops 67108864 | bytes 4194304 | tf_op jit(solution)/shard_map/sums/pallas_call | solution.py:309
  4.9 4.0 %collective-permute-start.2 = (bf16[9,8,128]{2,1,0:T(8,128)(2,1)S(1)}, bf16[9,8,128]{2,1,0:T(8,128)(2,1)S(1)}, u32[]{:S(2)}, u32[]{:S(2)}) collective-permute-start(bf16[9,8,128]{2,1,0:T(8,128)(2,1)S(1)} %get-tuple-element.24.refs_0_), channel_id=1, source_target_pairs={{0,24},{8,16},{16,8},{24,0},{1,25},{9,17},{17,9},{25,1},{2,26},{10... | collective-permute-start | bytes 55304 | tf_op jit(solution)/shard_map/ppermute | solution.py:338
  8.9 0.5 %collective-permute-start.1 = (bf16[9,8,128]{2,1,0:T(8,128)(2,1)S(1)}, bf16[9,8,128]{2,1,0:T(8,128)(2,1)S(1)}, u32[]{:S(2)}, u32[]{:S(2)}) collective-permute-start(bf16[9,8,128]{2,1,0:T(8,128)(2,1)S(1)} %get-tuple-element.24.refs_0_), channel_id=1, source_target_pairs={{0,16},{8,24},{16,0},{24,8},{1,17},{9,25},{17,1},{25,9},{2,18},{10... | collective-permute-start | bytes 55304 | tf_op jit(solution)/shard_map/ppermute | solution.py:338
  9.4 0.1 collective-permute-start
  9.5 0.0 copy-done
  9.5 1.7 %fluctuation.1 = (bf16[13,65536]{1,0:T(8,128)(2,1)}, s32[4,128]{1,0:T(4,128)S(1)}, f32[16,512]{1,0:T(8,128)S(1)}, f32[2,16,128]{2,1,0:T(8,128)S(1)}) custom-call(s32[512,128]{1,0:T(8,128)S(1)} %bitcast.7, f32[16,65536]{1,0:T(8,128)S(1)} %get-tuple-element.21.point_ref, f32[8,16,128]{2,1,0:T(8,128)S(1)} %get-tuple-element.22.window_ref), custom_call_target="tpu_custom_call" | custom-call | flops 67108864 | bytes 6291456 | tf_op jit(solution)/shard_map/fluctuation/pallas_call | solution.py:340
  11.2 0.0 collective-permute-done.2.refs_3_
  11.2 1.4 %collective-permute-done.1.refs_2_ = bf16[9,8,128]{2,1,0:T(8,128)(2,1)S(1)} collective-permute-done((bf16[9,8,128]{2,1,0:T(8,128)(2,1)S(1)}, bf16[9,8,128]{2,1,0:T(8,128)(2,1)S(1)}, u32[]{:S(2)}, u32[]{:S(2)}) %collective-permute-start.1) | collective-permute-done | bytes 18464 | tf_op jit(solution)/shard_map/ppermute | solution.py:338
  12.6 0.5 %collective-permute-done.refs_1_ = bf16[9,8,128]{2,1,0:T(8,128)(2,1)S(1)} collective-permute-done((bf16[9,8,128]{2,1,0:T(8,128)(2,1)S(1)}, bf16[9,8,128]{2,1,0:T(8,128)(2,1)S(1)}, u32[]{:S(2)}, u32[]{:S(2)}) %collective-permute-start) | collective-permute-done | bytes 18464 | tf_op jit(solution)/shard_map/ppermute | solution.py:338
  13.1 0.1 collective-permute-start.3
  13.2 1.3 %collective-permute-done.3.other_ref = bf16[4,9,8,128]{3,2,1,0:T(8,128)(2,1)S(1)} collective-permute-done((bf16[4,9,8,128]{3,2,1,0:T(8,128)(2,1)S(1)}, bf16[4,9,8,128]{3,2,1,0:T(8,128)(2,1)S(1)}, u32[]{:S(2)}, u32[]{:S(2)}) %collective-permute-start.3) | collective-permute-done | bytes 73760 | tf_op jit(solution)/shard_map/ppermute | solution.py:370
  14.5 0.1 route.1
  14.6 3.7 %collective-permute-start.4 = (bf16[10,8,128]{2,1,0:T(8,128)(2,1)S(1)}, bf16[10,8,128]{2,1,0:T(8,128)(2,1)S(1)}, u32[]{:S(2)}, u32[]{:S(2)}) collective-permute-start(bf16[10,8,128]{2,1,0:T(8,128)(2,1)S(1)} %get-tuple-element.28), channel_id=1, source_target_pairs={{0,6},{1,7},{2,4},{3,5},{4,2},{5,3},{6,0},{7,1},{8,14},{9,15},{10,... | collective-permute-start | bytes 61448 | tf_op jit(solution)/shard_map/ppermute | solution.py:387
  18.3 0.0 collective-permute-start.5
  18.3 0.8 %collective-permute-start.6 = (bf16[10,8,128]{2,1,0:T(8,128)(2,1)S(1)}, bf16[10,8,128]{2,1,0:T(8,128)(2,1)S(1)}, u32[]{:S(2)}, u32[]{:S(2)}) collective-permute-start(bf16[10,8,128]{2,1,0:T(8,128)(2,1)S(1)} %get-tuple-element.30), channel_id=1, source_target_pairs={{0,2},{1,3},{2,0},{3,1},{4,6},{5,7},{6,4},{7,5},{8,10},{9,11},{10,... | collective-permute-start | bytes 61448 | tf_op jit(solution)/shard_map/ppermute | solution.py:387
  19.1 1.2 %collective-permute-done.4.refs_0_ = bf16[10,8,128]{2,1,0:T(8,128)(2,1)S(1)} collective-permute-done((bf16[10,8,128]{2,1,0:T(8,128)(2,1)S(1)}, bf16[10,8,128]{2,1,0:T(8,128)(2,1)S(1)}, u32[]{:S(2)}, u32[]{:S(2)}) %collective-permute-start.4) | collective-permute-done | bytes 20512 | tf_op jit(solution)/shard_map/ppermute | solution.py:387
  20.2 2.7 %collective-permute-done.5.refs_1_ = bf16[10,8,128]{2,1,0:T(8,128)(2,1)S(1)} collective-permute-done((bf16[10,8,128]{2,1,0:T(8,128)(2,1)S(1)}, bf16[10,8,128]{2,1,0:T(8,128)(2,1)S(1)}, u32[]{:S(2)}, u32[]{:S(2)}) %collective-permute-start.5) | collective-permute-done | bytes 20512 | tf_op jit(solution)/shard_map/ppermute | solution.py:387
  22.9 0.0 collective-permute-done.6.refs_2_
  22.9 1.2 %place.1 = (f32[13,512]{1,0:T(8,128)}, bf16[13,65536]{1,0:T(8,128)(2,1)}) custom-call(s32[256]{0:T(256)S(4)} %get-tuple-element.19.blocks_ref, bf16[10,8,128]{2,1,0:T(8,128)(2,1)S(1)} %collective-permute-done.4.refs_0_, bf16[10,8,128]{2,1,0:T(8,128)(2,1)S(1)} %collective-permute-done.5.refs_1_, ...), custom_call_target="tpu_custom_call", output_to_operand_aliasing={{1}: (8, {})} | custom-call | tf_op jit(solution)/shard_map/place/pallas_call | solution.py:388
  (1 shorter events, 0.0 us)
Async XLA Ops:
  0.6 8.9 %copy-start = (s32[65536]{0:T(1024)S(1)}, s32[65536]{0:T(1024)}, u32[]{:S(2)}) copy-start(s32[65536]{0:T(1024)} %param.4) | copy-start | bytes 786436
  0.6 0.7 %copy-start.1 = (s32[256]{0:T(256)S(1)}, s32[256]{0:T(256)}, u32[]{:S(2)}) copy-start(s32[256]{0:T(256)} %blocks_any.1) | copy-start | bytes 3076
  4.9 6.3 %collective-permute-start.2 = (bf16[9,8,128]{2,1,0:T(8,128)(2,1)S(1)}, bf16[9,8,128]{2,1,0:T(8,128)(2,1)S(1)}, u32[]{:S(2)}, u32[]{:S(2)}) collective-permute-start(bf16[9,8,128]{2,1,0:T(8,128)(2,1)S(1)} %get-tuple-element.24.refs_0_), channel_id=1, source_target_pairs={{0,24},{8,16},{16,8},{24,0},{1,25},{9,17},{17,9},{25,1},{2,26},{10... | collective-permute-start | bytes 55304 | tf_op jit(solution)/shard_map/ppermute | solution.py:338
  8.9 3.8 %collective-permute-start.1 = (bf16[9,8,128]{2,1,0:T(8,128)(2,1)S(1)}, bf16[9,8,128]{2,1,0:T(8,128)(2,1)S(1)}, u32[]{:S(2)}, u32[]{:S(2)}) collective-permute-start(bf16[9,8,128]{2,1,0:T(8,128)(2,1)S(1)} %get-tuple-element.24.refs_0_), channel_id=1, source_target_pairs={{0,16},{8,24},{16,0},{24,8},{1,17},{9,25},{17,1},{25,9},{2,18},{10... | collective-permute-start | bytes 55304 | tf_op jit(solution)/shard_map/ppermute | solution.py:338
  9.4 3.8 %collective-permute-start = (bf16[9,8,128]{2,1,0:T(8,128)(2,1)S(1)}, bf16[9,8,128]{2,1,0:T(8,128)(2,1)S(1)}, u32[]{:S(2)}, u32[]{:S(2)}) collective-permute-start(bf16[9,8,128]{2,1,0:T(8,128)(2,1)S(1)} %get-tuple-element.24.refs_0_), channel_id=1, source_target_pairs={{0,8},{8,0},{16,24},{24,16},{1,9},{9,1},{17,25},{25,17},{2,10},{10... | collective-permute-start | bytes 55304 | tf_op jit(solution)/shard_map/ppermute | solution.py:338
  13.1 1.3 %collective-permute-start.3 = (bf16[4,9,8,128]{3,2,1,0:T(8,128)(2,1)S(1)}, bf16[4,9,8,128]{3,2,1,0:T(8,128)(2,1)S(1)}, u32[]{:S(2)}, u32[]{:S(2)}) collective-permute-start(bf16[4,9,8,128]{3,2,1,0:T(8,128)(2,1)S(1)} %stack.1.mine_ref), channel_id=1, source_target_pairs={{0,1},{1,0},{2,3},{3,2},{4,5},{5,4},{6,7},{7,6},{8,9},{9,8},{10,11... | collective-permute-start | bytes 221192 | tf_op jit(solution)/shard_map/ppermute | solution.py:370
  14.6 5.6 %collective-permute-start.4 = (bf16[10,8,128]{2,1,0:T(8,128)(2,1)S(1)}, bf16[10,8,128]{2,1,0:T(8,128)(2,1)S(1)}, u32[]{:S(2)}, u32[]{:S(2)}) collective-permute-start(bf16[10,8,128]{2,1,0:T(8,128)(2,1)S(1)} %get-tuple-element.28), channel_id=1, source_target_pairs={{0,6},{1,7},{2,4},{3,5},{4,2},{5,3},{6,0},{7,1},{8,14},{9,15},{10,... | collective-permute-start | bytes 61448 | tf_op jit(solution)/shard_map/ppermute | solution.py:387
  18.3 4.7 %collective-permute-start.5 = (bf16[10,8,128]{2,1,0:T(8,128)(2,1)S(1)}, bf16[10,8,128]{2,1,0:T(8,128)(2,1)S(1)}, u32[]{:S(2)}, u32[]{:S(2)}) collective-permute-start(bf16[10,8,128]{2,1,0:T(8,128)(2,1)S(1)} %get-tuple-element.29), channel_id=1, source_target_pairs={{0,4},{1,5},{2,6},{3,7},{4,0},{5,1},{6,2},{7,3},{8,12},{9,13},{10,... | collective-permute-start | bytes 61448 | tf_op jit(solution)/shard_map/ppermute | solution.py:387
  18.3 4.7 %collective-permute-start.6 = (bf16[10,8,128]{2,1,0:T(8,128)(2,1)S(1)}, bf16[10,8,128]{2,1,0:T(8,128)(2,1)S(1)}, u32[]{:S(2)}, u32[]{:S(2)}) collective-permute-start(bf16[10,8,128]{2,1,0:T(8,128)(2,1)S(1)} %get-tuple-element.30), channel_id=1, source_target_pairs={{0,2},{1,3},{2,0},{3,1},{4,6},{5,7},{6,4},{7,5},{8,10},{9,11},{10,... | collective-permute-start | bytes 61448 | tf_op jit(solution)/shard_map/ppermute | solution.py:387

commit v8 on v7

--- a/solution.py
+++ b/solution.py
@@ -54,7 +54,7 @@
 
 
 def sum_kernel(
-    ids_hbm, q_hbm, s_hbm, blocks_any, table_ref, window_ref, point_ref, blocks_ref, ids_ref, q_ref, s_ref, acc_ref,
+    ids_hbm, q_hbm, s_hbm, blocks_hbm, table_ref, window_ref, point_ref, blocks_ref, ids_ref, q_ref, s_ref, acc_ref,
     sems, blocks_sem, *, cuts, blk,
 ):
     grains = ids_hbm.shape[0]
@@ -74,7 +74,7 @@
     for chunk in range(len(chunks)):
         for copy in copies(chunk):
             copy.start()
-    blocks_copy = pltpu.make_async_copy(blocks_any, blocks_ref, blocks_sem)
+    blocks_copy = pltpu.make_async_copy(blocks_hbm, blocks_ref, blocks_sem)
     blocks_copy.start()
 
     quaternion = lax.broadcasted_iota(jnp.int32, (8, AVG), 0) < 4
@@ -298,8 +298,7 @@
 
     ids = grain_ids.reshape(tiles, AVG)
     quads = orientation.reshape(4, tiles, AVG).transpose(1, 0, 2).reshape(4 * tiles, AVG)
-    in_hbm = [pltpu.with_memory_space_constraint(x, pltpu.HBM) for x in (ids, quads, stress)]
-    anywhere = pl.BlockSpec(memory_space=pl.ANY)
+    in_hbm = [pltpu.with_memory_space_constraint(x, pltpu.HBM) for x in (ids, quads, stress, owner_blocks)]
     smem = pl.BlockSpec(memory_space=pltpu.SMEM)
     vmem = pl.BlockSpec(memory_space=pltpu.VMEM)
     hbm = pl.BlockSpec(memory_space=pltpu.HBM)
@@ -314,7 +313,7 @@
             jax.ShapeDtypeStruct((ROWS, points), F32),
             pltpu.SMEM(owner_blocks.shape, jnp.int32),
         ],
-        in_specs=[hbm, hbm, hbm, anywhere],
+        in_specs=[hbm] * 4,
         out_specs=[vmem, vmem, vmem, smem],
         scratch_shapes=[
             pltpu.VMEM((tiles, AVG), jnp.int32),
@@ -329,7 +328,7 @@
             flops=64 * points * ROWS, bytes_accessed=4 * points * ROWS, transcendentals=0
         ),
         name="sums",
-    )(*in_hbm, owner_blocks)
+    )(*in_hbm)
     blocks = pltpu.with_memory_space_constraint(blocks, pltpu.SMEM)
 
     held = [table]

time: 24.3 us -> 23.6 us (0.971)
  local copies, waits for them, and re-layouts: 0.72 us -> 0.01 us
    unnamed x4 -> x2, local copies, waits for them, and re-layouts: 0.72 us -> 0.01 us
where the time goes in v8:
time: 23.6 us; the launch traced here: 23.4 us
  starting transfers between devices  9.15 us (39%)
  waiting for transfers between devices  7.09 us (30%)
  Pallas kernels  6.5 us (28%)
  between operations  0.69 us (3%)
    ppermute x3, starting transfers between devices, local(): held.append(lax.ppermute(table, 'grp', moves))  4.63 us
    ppermute x3, starting transfers between devices, local(): got.insert(1, lax.ppermute(sent[offset], 'slab', moves))  4.45 us
    ppermute x3, waiting for transfers between devices, local(): got.insert(1, lax.ppermute(sent[offset], 'slab', moves))  3.9 us
    pallas_call x1, Pallas kernels, local(): pl.pallas_call(functools.partial(sum_kernel, cuts=cuts, blk=blk), out_sha...  3.54 us
    ppermute x3, waiting for transfers between devices, local(): held.append(lax.ppermute(table, 'grp', moves))  1.94 us
    pallas_call x1, Pallas kernels, local(): pl.pallas_call(fluctuation_kernel, out_shape=[jax.ShapeDtypeStruct((COUNT...  1.67 us
    ppermute x1, waiting for transfers between devices, local(): other = lax.ppermute(mine, 'slab', [(s, s ^ 1) for s in range(slabs)])  1.25 us
    pallas_call x1, Pallas kernels, local(): pl.pallas_call(functools.partial(place_kernel, groups=groups, chips=chips...  1.16 us
  transfers between devices with their start and end apart: 7, of which 5 were waited for; matrix products, arithmetic and copies ran while one was open for 0% of the time, Pallas kernels for 7%

profile of v8, /device:TPU:0, one launch (start us, length us, event | category | flops | bytes accessed | tf_op | source)
XLA Modules:
  0.0 23.4 jit_solution(8454619567959494525)
XLA Ops:
  0.6 0.0 copy-start
  0.6 3.5 %sums.1 = (bf16[9,8,128]{2,1,0:T(8,128)(2,1)S(1)}, f32[8,16,128]{2,1,0:T(8,128)S(1)}, f32[16,65536]{1,0:T(8,128)S(1)}, s32[256]{0:T(256)S(4)}) custom-call(s32[512,128]{1,0:T(8,128)} %bitcast.6, f32[2048,128]{1,0:T(8,128)} %bitcast.8, f32[9,65536]{1,0:T(8,128)} %s_hbm.1, s32[256]{0:T(256)} %blocks_hbm.1), custom_call_target="tpu_custom_call" | custom-call | flops 67108864 | bytes 4194304 | tf_op jit(solution)/shard_map/sums/pallas_call | solution.py:308
  4.2 4.0 %collective-permute-start.2 = (bf16[9,8,128]{2,1,0:T(8,128)(2,1)S(1)}, bf16[9,8,128]{2,1,0:T(8,128)(2,1)S(1)}, u32[]{:S(2)}, u32[]{:S(2)}) collective-permute-start(bf16[9,8,128]{2,1,0:T(8,128)(2,1)S(1)} %get-tuple-element.24.refs_0_), channel_id=1, source_target_pairs={{0,24},{8,16},{16,8},{24,0},{1,25},{9,17},{17,9},{25,1},{2,26},{10... | collective-permute-start | bytes 55304 | tf_op jit(solution)/shard_map/ppermute | solution.py:337
  8.2 0.5 %collective-permute-start.1 = (bf16[9,8,128]{2,1,0:T(8,128)(2,1)S(1)}, bf16[9,8,128]{2,1,0:T(8,128)(2,1)S(1)}, u32[]{:S(2)}, u32[]{:S(2)}) collective-permute-start(bf16[9,8,128]{2,1,0:T(8,128)(2,1)S(1)} %get-tuple-element.24.refs_0_), channel_id=1, source_target_pairs={{0,16},{8,24},{16,0},{24,8},{1,17},{9,25},{17,1},{25,9},{2,18},{10... | collective-permute-start | bytes 55304 | tf_op jit(solution)/shard_map/ppermute | solution.py:337
  8.7 0.1 collective-permute-start
  8.8 0.0 copy-done
  8.8 1.7 %fluctuation.1 = (bf16[13,65536]{1,0:T(8,128)(2,1)}, s32[4,128]{1,0:T(4,128)S(1)}, f32[16,512]{1,0:T(8,128)S(1)}, f32[2,16,128]{2,1,0:T(8,128)S(1)}) custom-call(s32[512,128]{1,0:T(8,128)S(1)} %bitcast.7, f32[16,65536]{1,0:T(8,128)S(1)} %get-tuple-element.21.point_ref, f32[8,16,128]{2,1,0:T(8,128)S(1)} %get-tuple-element.22.window_ref), custom_call_target="tpu_custom_call" | custom-call | flops 67108864 | bytes 6291456 | tf_op jit(solution)/shard_map/fluctuation/pallas_call | solution.py:339
  10.5 0.0 collective-permute-done.2.refs_3_
  10.5 1.4 %collective-permute-done.1.refs_2_ = bf16[9,8,128]{2,1,0:T(8,128)(2,1)S(1)} collective-permute-done((bf16[9,8,128]{2,1,0:T(8,128)(2,1)S(1)}, bf16[9,8,128]{2,1,0:T(8,128)(2,1)S(1)}, u32[]{:S(2)}, u32[]{:S(2)}) %collective-permute-start.1) | collective-permute-done | bytes 18464 | tf_op jit(solution)/shard_map/ppermute | solution.py:337
  11.9 0.5 %collective-permute-done.refs_1_ = bf16[9,8,128]{2,1,0:T(8,128)(2,1)S(1)} collective-permute-done((bf16[9,8,128]{2,1,0:T(8,128)(2,1)S(1)}, bf16[9,8,128]{2,1,0:T(8,128)(2,1)S(1)}, u32[]{:S(2)}, u32[]{:S(2)}) %collective-permute-start) | collective-permute-done | bytes 18464 | tf_op jit(solution)/shard_map/ppermute | solution.py:337
  12.5 0.1 collective-permute-start.3
  12.5 1.3 %collective-permute-done.3.other_ref = bf16[4,9,8,128]{3,2,1,0:T(8,128)(2,1)S(1)} collective-permute-done((bf16[4,9,8,128]{3,2,1,0:T(8,128)(2,1)S(1)}, bf16[4,9,8,128]{3,2,1,0:T(8,128)(2,1)S(1)}, u32[]{:S(2)}, u32[]{:S(2)}) %collective-permute-start.3) | collective-permute-done | bytes 73760 | tf_op jit(solution)/shard_map/ppermute | solution.py:369
  13.8 0.1 route.1
  13.9 3.7 %collective-permute-start.4 = (bf16[10,8,128]{2,1,0:T(8,128)(2,1)S(1)}, bf16[10,8,128]{2,1,0:T(8,128)(2,1)S(1)}, u32[]{:S(2)}, u32[]{:S(2)}) collective-permute-start(bf16[10,8,128]{2,1,0:T(8,128)(2,1)S(1)} %get-tuple-element.28), channel_id=1, source_target_pairs={{0,6},{1,7},{2,4},{3,5},{4,2},{5,3},{6,0},{7,1},{8,14},{9,15},{10,... | collective-permute-start | bytes 61448 | tf_op jit(solution)/shard_map/ppermute | solution.py:386
  17.6 0.0 collective-permute-start.5
  17.6 0.8 %collective-permute-start.6 = (bf16[10,8,128]{2,1,0:T(8,128)(2,1)S(1)}, bf16[10,8,128]{2,1,0:T(8,128)(2,1)S(1)}, u32[]{:S(2)}, u32[]{:S(2)}) collective-permute-start(bf16[10,8,128]{2,1,0:T(8,128)(2,1)S(1)} %get-tuple-element.30), channel_id=1, source_target_pairs={{0,2},{1,3},{2,0},{3,1},{4,6},{5,7},{6,4},{7,5},{8,10},{9,11},{10,... | collective-permute-start | bytes 61448 | tf_op jit(solution)/shard_map/ppermute | solution.py:386
  18.4 1.2 %collective-permute-done.4.refs_0_ = bf16[10,8,128]{2,1,0:T(8,128)(2,1)S(1)} collective-permute-done((bf16[10,8,128]{2,1,0:T(8,128)(2,1)S(1)}, bf16[10,8,128]{2,1,0:T(8,128)(2,1)S(1)}, u32[]{:S(2)}, u32[]{:S(2)}) %collective-permute-start.4) | collective-permute-done | bytes 20512 | tf_op jit(solution)/shard_map/ppermute | solution.py:386
  19.6 2.7 %collective-permute-done.5.refs_1_ = bf16[10,8,128]{2,1,0:T(8,128)(2,1)S(1)} collective-permute-done((bf16[10,8,128]{2,1,0:T(8,128)(2,1)S(1)}, bf16[10,8,128]{2,1,0:T(8,128)(2,1)S(1)}, u32[]{:S(2)}, u32[]{:S(2)}) %collective-permute-start.5) | collective-permute-done | bytes 20512 | tf_op jit(solution)/shard_map/ppermute | solution.py:386
  22.3 0.0 collective-permute-done.6.refs_2_
  22.3 1.2 %place.1 = (f32[13,512]{1,0:T(8,128)}, bf16[13,65536]{1,0:T(8,128)(2,1)}) custom-call(s32[256]{0:T(256)S(4)} %get-tuple-element.19.blocks_ref, bf16[10,8,128]{2,1,0:T(8,128)(2,1)S(1)} %collective-permute-done.4.refs_0_, bf16[10,8,128]{2,1,0:T(8,128)(2,1)S(1)} %collective-permute-done.5.refs_1_, ...), custom_call_target="tpu_custom_call", output_to_operand_aliasing={{1}: (8, {})} | custom-call | tf_op jit(solution)/shard_map/place/pallas_call | solution.py:387
  (1 shorter events, 0.0 us)
Async XLA Ops:
  0.6 8.2 %copy-start = (s32[65536]{0:T(1024)S(1)}, s32[65536]{0:T(1024)}, u32[]{:S(2)}) copy-start(s32[65536]{0:T(1024)} %param.4) | copy-start | bytes 786436
  4.2 6.3 %collective-permute-start.2 = (bf16[9,8,128]{2,1,0:T(8,128)(2,1)S(1)}, bf16[9,8,128]{2,1,0:T(8,128)(2,1)S(1)}, u32[]{:S(2)}, u32[]{:S(2)}) collective-permute-start(bf16[9,8,128]{2,1,0:T(8,128)(2,1)S(1)} %get-tuple-element.24.refs_0_), channel_id=1, source_target_pairs={{0,24},{8,16},{16,8},{24,0},{1,25},{9,17},{17,9},{25,1},{2,26},{10... | collective-permute-start | bytes 55304 | tf_op jit(solution)/shard_map/ppermute | solution.py:337
  8.2 3.8 %collective-permute-start.1 = (bf16[9,8,128]{2,1,0:T(8,128)(2,1)S(1)}, bf16[9,8,128]{2,1,0:T(8,128)(2,1)S(1)}, u32[]{:S(2)}, u32[]{:S(2)}) collective-permute-start(bf16[9,8,128]{2,1,0:T(8,128)(2,1)S(1)} %get-tuple-element.24.refs_0_), channel_id=1, source_target_pairs={{0,16},{8,24},{16,0},{24,8},{1,17},{9,25},{17,1},{25,9},{2,18},{10... | collective-permute-start | bytes 55304 | tf_op jit(solution)/shard_map/ppermute | solution.py:337
  8.7 3.8 %collective-permute-start = (bf16[9,8,128]{2,1,0:T(8,128)(2,1)S(1)}, bf16[9,8,128]{2,1,0:T(8,128)(2,1)S(1)}, u32[]{:S(2)}, u32[]{:S(2)}) collective-permute-start(bf16[9,8,128]{2,1,0:T(8,128)(2,1)S(1)} %get-tuple-element.24.refs_0_), channel_id=1, source_target_pairs={{0,8},{8,0},{16,24},{24,16},{1,9},{9,1},{17,25},{25,17},{2,10},{10... | collective-permute-start | bytes 55304 | tf_op jit(solution)/shard_map/ppermute | solution.py:337
  12.5 1.3 %collective-permute-start.3 = (bf16[4,9,8,128]{3,2,1,0:T(8,128)(2,1)S(1)}, bf16[4,9,8,128]{3,2,1,0:T(8,128)(2,1)S(1)}, u32[]{:S(2)}, u32[]{:S(2)}) collective-permute-start(bf16[4,9,8,128]{3,2,1,0:T(8,128)(2,1)S(1)} %stack.1.mine_ref), channel_id=1, source_target_pairs={{0,1},{1,0},{2,3},{3,2},{4,5},{5,4},{6,7},{7,6},{8,9},{9,8},{10,11... | collective-permute-start | bytes 221192 | tf_op jit(solution)/shard_map/ppermute | solution.py:369
  13.9 5.6 %collective-permute-start.4 = (bf16[10,8,128]{2,1,0:T(8,128)(2,1)S(1)}, bf16[10,8,128]{2,1,0:T(8,128)(2,1)S(1)}, u32[]{:S(2)}, u32[]{:S(2)}) collective-permute-start(bf16[10,8,128]{2,1,0:T(8,128)(2,1)S(1)} %get-tuple-element.28), channel_id=1, source_target_pairs={{0,6},{1,7},{2,4},{3,5},{4,2},{5,3},{6,0},{7,1},{8,14},{9,15},{10,... | collective-permute-start | bytes 61448 | tf_op jit(solution)/shard_map/ppermute | solution.py:386
  17.6 4.7 %collective-permute-start.5 = (bf16[10,8,128]{2,1,0:T(8,128)(2,1)S(1)}, bf16[10,8,128]{2,1,0:T(8,128)(2,1)S(1)}, u32[]{:S(2)}, u32[]{:S(2)}) collective-permute-start(bf16[10,8,128]{2,1,0:T(8,128)(2,1)S(1)} %get-tuple-element.29), channel_id=1, source_target_pairs={{0,4},{1,5},{2,6},{3,7},{4,0},{5,1},{6,2},{7,3},{8,12},{9,13},{10,... | collective-permute-start | bytes 61448 | tf_op jit(solution)/shard_map/ppermute | solution.py:386
  17.6 4.7 %collective-permute-start.6 = (bf16[10,8,128]{2,1,0:T(8,128)(2,1)S(1)}, bf16[10,8,128]{2,1,0:T(8,128)(2,1)S(1)}, u32[]{:S(2)}, u32[]{:S(2)}) collective-permute-start(bf16[10,8,128]{2,1,0:T(8,128)(2,1)S(1)} %get-tuple-element.30), channel_id=1, source_target_pairs={{0,2},{1,3},{2,0},{3,1},{4,6},{5,7},{6,4},{7,5},{8,10},{9,11},{10,... | collective-permute-start | bytes 61448 | tf_op jit(solution)/shard_map/ppermute | solution.py:386

commit v9 on v8

--- a/solution.py
+++ b/solution.py
@@ -122,40 +122,29 @@
     table_ref[grains // blk] = jnp.where(half, pieces[:8], pltpu.roll(pieces[8:], blk, 1)).astype(BF16)
 
 
-def fluctuation_kernel(
-    ids_ref, point_ref, window_ref, out_hbm, edge_ids_ref, edge_point_ref, edge_window_ref, out_ref, sems
-):
-    windows = window_ref.shape[0]
+def fluctuation_kernel(ids_ref, point_ref, window_ref, *refs, begin, end):
+    *_, out_hbm, out_ref, sems = refs
     total = ids_ref.shape[0]
     tile_base = device_index() * total
-    tiles = total // windows
+    tiles = total // window_ref.shape[0]
     points = tiles * AVG
 
     def copy(window):
-        lanes = pl.ds(window * points, points)
-        return pltpu.make_async_copy(out_ref.at[:, lanes], out_hbm.at[:, lanes], sems.at[window])
-
-    def step(window):
+        here = slice((window - begin) * points, (window - begin + 1) * points)
+        there = slice(window * points, (window + 1) * points)
+        return pltpu.make_async_copy(out_ref.at[:, here], out_hbm.at[:, there], sems.at[window - begin])
+
+    for window in range(begin, end):
         table = window_ref[window]
         for sub in range(tiles // SUB):
             tile = window * tiles + sub * SUB
-            lanes = pl.ds(tile * AVG, SUB * AVG)
+            lanes = slice(tile * AVG, (tile + SUB) * AVG)
             near = pltpu.roll(table, (AVG - sub * SUB) % AVG, 1)[:, :WINDOW].astype(BF16)
-            picks = selection(ids_ref, tile, SUB, tile_base + tile - 1)
-            means = jnp.dot(near, picks, preferred_element_type=F32)
-            out_ref[:, lanes] = (point_ref[:, lanes] - means)[:COUNT].astype(BF16)
+            means = jnp.dot(near, selection(ids_ref, tile, SUB, tile_base + tile - 1), preferred_element_type=F32)
+            here = slice((tile - begin * tiles) * AVG, (tile - begin * tiles + SUB) * AVG)
+            out_ref[:, here] = (point_ref[:, lanes] - means)[:COUNT].astype(BF16)
         copy(window).start()
-
-    for window in range(windows):
-        step(window)
-    first, last = slice(0, EDGE), slice(total - EDGE, total)
-    edge_ids_ref[:EDGE] = ids_ref[first]
-    edge_ids_ref[EDGE:] = ids_ref[last]
-    edge_point_ref[:, : EDGE * AVG] = point_ref[:, : EDGE * AVG]
-    edge_point_ref[:, EDGE * AVG :] = point_ref[:, (total - EDGE) * AVG :]
-    edge_window_ref[0] = window_ref[0]
-    edge_window_ref[1] = pltpu.roll(window_ref[windows - 1], AVG - tiles + SUB, 1)
-    for window in range(windows):
+    for window in range(begin, end):
         copy(window).wait()
 
 
@@ -205,7 +194,7 @@
 
 
 def place_kernel(blocks_ref, *refs, groups, chips, blk):
-    (*got_refs, edge_ids_ref, edge_point_ref, edge_window_ref, _, table_hbm, fluctuation_hbm, held_ref, ends_ref,
+    (*got_refs, ids_ref, point_ref, window_ref, _, table_hbm, fluctuation_hbm, held_ref, ends_ref,
      edge_ref, table_ref, sems) = refs
     slots = got_refs[0].shape[0]
     per_device = slots - CORES
@@ -238,23 +227,25 @@
     others = jnp.where(lane_half < 2, ends(device - 1, 2, 0), ends(device + 1, 0, 2))
     shared = finish(unfold(ends(device, 0, 0) + others))
     wide_lane = lax.broadcasted_iota(jnp.int32, (ROWS, AVG), 1)
-    first = jnp.where(wide_lane < 2, shared, edge_window_ref[0])
+    windows = window_ref.shape[0]
+    first = jnp.where(wide_lane < 2, shared, window_ref[0])
     in_last = (wide_lane >= SUB) & (wide_lane < SUB + 2)
-    last = jnp.where(in_last, pltpu.roll(shared, SUB - 2, 1), edge_window_ref[1])
+    last = pltpu.roll(window_ref[windows - 1], AVG - grains // windows + SUB, 1)
+    last = jnp.where(in_last, pltpu.roll(shared, SUB - 2, 1), last)
     width = EDGE * AVG
-    total = fluctuation_hbm.shape[1]
     first_grain = device * grains - 1
     copies = []
-    for end, (table, grain, begin) in enumerate(
-        ((first, first_grain, 0), (last, first_grain + grains - SUB, total - width))
+    for end, (table, tile, grain) in enumerate(
+        ((first, 0, first_grain), (last, grains - EDGE, first_grain + grains - SUB))
     ):
         lanes = slice(end * width, (end + 1) * width)
-        picks = selection(edge_ids_ref, end * EDGE, EDGE, grain)
+        points = slice(tile * AVG, tile * AVG + width)
+        picks = selection(ids_ref, tile, EDGE, grain)
         means = jnp.dot(table[:, :WINDOW].astype(BF16), picks, preferred_element_type=F32)
-        edge_ref[:, lanes] = (edge_point_ref[:, lanes] - means)[:COUNT].astype(BF16)
+        edge_ref[:, lanes] = (point_ref[:, points] - means)[:COUNT].astype(BF16)
         copies.append(
             pltpu.make_async_copy(
-                edge_ref.at[:, lanes], fluctuation_hbm.at[:, begin : begin + width], sems.at[end]
+                edge_ref.at[:, lanes], fluctuation_hbm.at[:, points], sems.at[end]
             )
         )
         copies[-1].start()
@@ -305,18 +296,18 @@
     params = pltpu.CompilerParams(vmem_limit_bytes=20 << 20)
 
     cuts = [tiles * part // CUTS[-1] for part in CUTS]
-    table, windows, point, blocks = pl.pallas_call(
+    table, windows, point, blocks, on_chip_ids = pl.pallas_call(
         functools.partial(sum_kernel, cuts=cuts, blk=blk),
         out_shape=[
             jax.ShapeDtypeStruct((slots, 8, AVG), BF16),
             jax.ShapeDtypeStruct((tiles // blk, ROWS, AVG), F32),
             jax.ShapeDtypeStruct((ROWS, points), F32),
             pltpu.SMEM(owner_blocks.shape, jnp.int32),
+            jax.ShapeDtypeStruct((tiles, AVG), jnp.int32),
         ],
         in_specs=[hbm] * 4,
-        out_specs=[vmem, vmem, vmem, smem],
+        out_specs=[vmem, vmem, vmem, smem, vmem],
         scratch_shapes=[
-            pltpu.VMEM((tiles, AVG), jnp.int32),
             pltpu.VMEM((4 * tiles, AVG), F32),
             pltpu.VMEM((9, points), F32),
             pltpu.VMEM((grains + AVG, AVG), F32),
@@ -336,28 +327,27 @@
         moves = [(g, int(target(g, offset, groups))) for g in range(groups)]
         held.append(lax.ppermute(table, "grp", moves))
 
-    fluctuation, edge_ids, edge_point, edge_windows = pl.pallas_call(
-        fluctuation_kernel,
-        out_shape=[
-            jax.ShapeDtypeStruct((COUNT, points), BF16),
-            jax.ShapeDtypeStruct((2 * EDGE, AVG), jnp.int32),
-            jax.ShapeDtypeStruct((ROWS, 2 * EDGE * AVG), F32),
-            jax.ShapeDtypeStruct((2, ROWS, AVG), F32),
-        ],
-        in_specs=[vmem, vmem, vmem],
-        out_specs=[hbm, vmem, vmem, vmem],
-        scratch_shapes=[
-            pltpu.VMEM((COUNT, points), BF16),
-            pltpu.SemaphoreType.DMA((tiles // blk,)),
-        ],
-        compiler_params=params,
-        cost_estimate=pl.CostEstimate(
-            flops=64 * points * ROWS, bytes_accessed=6 * points * ROWS, transcendentals=0
-        ),
-        name="fluctuation",
-    )(ids, point, windows)
-
-    held, edge_ids = lax.optimization_barrier((held, edge_ids))
+    on_chip = (on_chip_ids, point, windows)
+    count = tiles // blk
+
+    def look_up(begin, end, earlier):
+        share = (end - begin) * points // count
+        return pl.pallas_call(
+            functools.partial(fluctuation_kernel, begin=begin, end=end),
+            out_shape=jax.ShapeDtypeStruct((COUNT, points), BF16),
+            in_specs=[vmem] * 3 + [hbm] * len(earlier),
+            out_specs=hbm,
+            scratch_shapes=[pltpu.VMEM((COUNT, share), BF16), pltpu.SemaphoreType.DMA((end - begin,))],
+            input_output_aliases={3: 0} if earlier else {},
+            compiler_params=params,
+            cost_estimate=pl.CostEstimate(
+                flops=64 * share * ROWS, bytes_accessed=6 * share * ROWS, transcendentals=0
+            ),
+            name="fluctuation",
+        )(*on_chip, *earlier)
+
+    fluctuation = look_up(0, count // 2, [])
+    held, fluctuation = lax.optimization_barrier((held, fluctuation))
     mine = pl.pallas_call(
         stack_kernel,
         out_shape=jax.ShapeDtypeStruct((groups, slots, 8, AVG), BF16),
@@ -367,6 +357,8 @@
         name="stack",
     )(*held)
     other = lax.ppermute(mine, "slab", [(s, s ^ 1) for s in range(slabs)])
+    fluctuation = look_up(count // 2, count, [fluctuation])
+    other, fluctuation = lax.optimization_barrier((other, fluctuation))
     sent = pl.pallas_call(
         route_kernel,
         out_shape=[jax.ShapeDtypeStruct((per_device + CORES, 8, AVG), BF16)] * chips,
@@ -402,7 +394,7 @@
         input_output_aliases={chips + 4: 1},
         compiler_params=params,
         name="place",
-    )(blocks, *reversed(got), edge_ids, edge_point, edge_windows, fluctuation)
+    )(blocks, *reversed(got), *on_chip, fluctuation)
     return (grain_table, fluctuation)
 
 

time: 23.6 us -> 24.5 us (1.038)
  Pallas kernels: 6.5 us -> 7.34 us
    ppermute x3, waiting for transfers between devices: 1.94 us -> 3.35 us  [local(): held.append(lax.ppermute(table, 'grp', moves))]
    ppermute x1, waiting for transfers between devices: 1.25 us -> 0.01 us  [local(): other = lax.ppermute(mine, 'slab', [(s, s ^ 1) for s in range(slabs)])]
    pallas_call x1 -> x2, Pallas kernels: 1.67 us -> 2.54 us  [look_up(): pl.pallas_call(functools.partial(fluctuation_kernel, begin=begin, end=end...]
  transfers between devices with their start and end apart: 7 -> 7, of which waited for: 5 -> 4; matrix products, arithmetic and copies ran while one was open for 0% -> 0% of each run, Pallas kernels for 7% -> 10%
where the time goes in v9:
time: 24.5 us; the launch traced here: 24.4 us
  starting transfers between devices  9.1 us (37%)
  Pallas kernels  7.34 us (30%)
  waiting for transfers between devices  7.26 us (30%)
  between operations  0.69 us (3%)
    ppermute x3, starting transfers between devices, local(): held.append(lax.ppermute(table, 'grp', moves))  4.57 us
    ppermute x3, starting transfers between devices, local(): got.insert(1, lax.ppermute(sent[offset], 'slab', moves))  4.45 us
    ppermute x3, waiting for transfers between devices, local(): got.insert(1, lax.ppermute(sent[offset], 'slab', moves))  3.91 us
    pallas_call x1, Pallas kernels, local(): pl.pallas_call(functools.partial(sum_kernel, cuts=cuts, blk=blk), out_sha...  3.5 us
    ppermute x3, waiting for transfers between devices, local(): held.append(lax.ppermute(table, 'grp', moves))  3.35 us
    pallas_call x2, Pallas kernels, look_up(): pl.pallas_call(functools.partial(fluctuation_kernel, begin=begin, end=end...  2.54 us
    pallas_call x1, Pallas kernels, local(): pl.pallas_call(functools.partial(place_kernel, groups=groups, chips=chips...  1.16 us
  transfers between devices with their start and end apart: 7, of which 4 were waited for; matrix products, arithmetic and copies ran while one was open for 0% of the time, Pallas kernels for 10%

profile of v9, /device:TPU:0, one launch (start us, length us, event | category | flops | bytes accessed | tf_op | source)
XLA Modules:
  0.0 24.4 jit_solution(10776021451749858500)
XLA Ops:
  0.6 3.5 %sums.1 = (bf16[9,8,128]{2,1,0:T(8,128)(2,1)S(1)}, f32[8,16,128]{2,1,0:T(8,128)S(1)}, f32[16,65536]{1,0:T(8,128)S(1)}, s32[256]{0:T(256)S(4)}, s32[512,128]{1,0:T(8,128)S(1)}) custom-call(s32[512,128]{1,0:T(8,128)} %bitcast.7, f32[2048,128]{1,0:T(8,128)} %bitcast.6, f32[9,65536]{1,0:T(8,128)} %s_hbm.1, s32[256]{0:T(256)} %blocks_hbm.1), custom_call_target="tpu_custom_call" | custom-call | flops 67108864 | bytes 4194304 | tf_op jit(solution)/shard_map/sums/pallas_call | solution.py:299
  4.1 3.0 %collective-permute-start = (bf16[9,8,128]{2,1,0:T(8,128)(2,1)S(1)}, bf16[9,8,128]{2,1,0:T(8,128)(2,1)S(1)}, u32[]{:S(2)}, u32[]{:S(2)}) collective-permute-start(bf16[9,8,128]{2,1,0:T(8,128)(2,1)S(1)} %get-tuple-element.23.refs_0_), channel_id=1, source_target_pairs={{0,8},{8,0},{16,24},{24,16},{1,9},{9,1},{17,25},{25,17},{2,10},{10... | collective-permute-start | bytes 55304 | tf_op jit(solution)/shard_map/ppermute | solution.py:328
  7.2 1.5 %collective-permute-start.1 = (bf16[9,8,128]{2,1,0:T(8,128)(2,1)S(1)}, bf16[9,8,128]{2,1,0:T(8,128)(2,1)S(1)}, u32[]{:S(2)}, u32[]{:S(2)}) collective-permute-start(bf16[9,8,128]{2,1,0:T(8,128)(2,1)S(1)} %get-tuple-element.23.refs_0_), channel_id=1, source_target_pairs={{0,16},{8,24},{16,0},{24,8},{1,17},{9,25},{17,1},{25,9},{2,18},{10... | collective-permute-start | bytes 55304 | tf_op jit(solution)/shard_map/ppermute | solution.py:328
  8.7 0.0 collective-permute-start.2
  8.7 1.3 %fluctuation.2.refs_0_ = bf16[13,65536]{1,0:T(8,128)(2,1)} custom-call(s32[512,128]{1,0:T(8,128)S(1)} %get-tuple-element.20.ids_ref.refs_4_, f32[16,65536]{1,0:T(8,128)S(1)} %get-tuple-element.21.point_ref.refs_5_, f32[8,16,128]{2,1,0:T(8,128)S(1)} %get-tuple-element.22.window_ref.refs_6_), custom_call_target="tpu_custom_call" | custom-call | flops 33554432 | bytes 3145728 | tf_op jit(solution)/shard_map/fluctuation/pallas_call | solution.py:335
  10.0 0.0 collective-permute-done.refs_1_
  10.0 0.9 %collective-permute-done.1.refs_2_ = bf16[9,8,128]{2,1,0:T(8,128)(2,1)S(1)} collective-permute-done((bf16[9,8,128]{2,1,0:T(8,128)(2,1)S(1)}, bf16[9,8,128]{2,1,0:T(8,128)(2,1)S(1)}, u32[]{:S(2)}, u32[]{:S(2)}) %collective-permute-start.1) | collective-permute-done | bytes 18464 | tf_op jit(solution)/shard_map/ppermute | solution.py:328
  10.9 2.4 %collective-permute-done.2.refs_3_ = bf16[9,8,128]{2,1,0:T(8,128)(2,1)S(1)} collective-permute-done((bf16[9,8,128]{2,1,0:T(8,128)(2,1)S(1)}, bf16[9,8,128]{2,1,0:T(8,128)(2,1)S(1)}, u32[]{:S(2)}, u32[]{:S(2)}) %collective-permute-start.2) | collective-permute-done | bytes 18464 | tf_op jit(solution)/shard_map/ppermute | solution.py:328
  13.4 0.1 collective-permute-start.3
  13.4 1.3 %fluctuation.3.refs_7_ = bf16[13,65536]{1,0:T(8,128)(2,1)} custom-call(s32[512,128]{1,0:T(8,128)S(1)} %get-tuple-element.20.ids_ref.refs_4_, f32[16,65536]{1,0:T(8,128)S(1)} %get-tuple-element.21.point_ref.refs_5_, f32[8,16,128]{2,1,0:T(8,128)S(1)} %get-tuple-element.22.window_ref.refs_6_, ...), custom_call_target="tpu_custom_call", output_to_operand_aliasing={{}: (3, {})} | custom-call | flops 33554432 | bytes 3145728 | tf_op jit(solution)/shard_map/fluctuation/pallas_call | solution.py:335
  14.7 0.0 collective-permute-done.3.other_ref
  14.7 0.1 route.1
  14.9 3.7 %collective-permute-start.4 = (bf16[10,8,128]{2,1,0:T(8,128)(2,1)S(1)}, bf16[10,8,128]{2,1,0:T(8,128)(2,1)S(1)}, u32[]{:S(2)}, u32[]{:S(2)}) collective-permute-start(bf16[10,8,128]{2,1,0:T(8,128)(2,1)S(1)} %get-tuple-element.29), channel_id=1, source_target_pairs={{0,6},{1,7},{2,4},{3,5},{4,2},{5,3},{6,0},{7,1},{8,14},{9,15},{10,... | collective-permute-start | bytes 61448 | tf_op jit(solution)/shard_map/ppermute | solution.py:378
  18.5 0.0 collective-permute-start.5
  18.5 0.8 %collective-permute-start.6 = (bf16[10,8,128]{2,1,0:T(8,128)(2,1)S(1)}, bf16[10,8,128]{2,1,0:T(8,128)(2,1)S(1)}, u32[]{:S(2)}, u32[]{:S(2)}) collective-permute-start(bf16[10,8,128]{2,1,0:T(8,128)(2,1)S(1)} %get-tuple-element.31), channel_id=1, source_target_pairs={{0,2},{1,3},{2,0},{3,1},{4,6},{5,7},{6,4},{7,5},{8,10},{9,11},{10,... | collective-permute-start | bytes 61448 | tf_op jit(solution)/shard_map/ppermute | solution.py:378
  19.3 1.2 %collective-permute-done.4.refs_0_ = bf16[10,8,128]{2,1,0:T(8,128)(2,1)S(1)} collective-permute-done((bf16[10,8,128]{2,1,0:T(8,128)(2,1)S(1)}, bf16[10,8,128]{2,1,0:T(8,128)(2,1)S(1)}, u32[]{:S(2)}, u32[]{:S(2)}) %collective-permute-start.4) | collective-permute-done | bytes 20512 | tf_op jit(solution)/shard_map/ppermute | solution.py:378
  20.5 2.7 %collective-permute-done.5.refs_1_ = bf16[10,8,128]{2,1,0:T(8,128)(2,1)S(1)} collective-permute-done((bf16[10,8,128]{2,1,0:T(8,128)(2,1)S(1)}, bf16[10,8,128]{2,1,0:T(8,128)(2,1)S(1)}, u32[]{:S(2)}, u32[]{:S(2)}) %collective-permute-start.5) | collective-permute-done | bytes 20512 | tf_op jit(solution)/shard_map/ppermute | solution.py:378
  23.2 0.0 collective-permute-done.6.refs_2_
  23.2 1.2 %place.1 = (f32[13,512]{1,0:T(8,128)}, bf16[13,65536]{1,0:T(8,128)(2,1)}) custom-call(s32[256]{0:T(256)S(4)} %get-tuple-element.18.blocks_ref, bf16[10,8,128]{2,1,0:T(8,128)(2,1)S(1)} %collective-permute-done.4.refs_0_, bf16[10,8,128]{2,1,0:T(8,128)(2,1)S(1)} %collective-permute-done.5.refs_1_, ...), custom_call_target="tpu_custom_call", output_to_operand_aliasing={{1}: (8, {})} | custom-call | tf_op jit(solution)/shard_map/place/pallas_call | solution.py:379
  (1 shorter events, 0.0 us)
Async XLA Ops:
  4.1 5.9 %collective-permute-start = (bf16[9,8,128]{2,1,0:T(8,128)(2,1)S(1)}, bf16[9,8,128]{2,1,0:T(8,128)(2,1)S(1)}, u32[]{:S(2)}, u32[]{:S(2)}) collective-permute-start(bf16[9,8,128]{2,1,0:T(8,128)(2,1)S(1)} %get-tuple-element.23.refs_0_), channel_id=1, source_target_pairs={{0,8},{8,0},{16,24},{24,16},{1,9},{9,1},{17,25},{25,17},{2,10},{10... | collective-permute-start | bytes 55304 | tf_op jit(solution)/shard_map/ppermute | solution.py:328
  7.2 3.8 %collective-permute-start.1 = (bf16[9,8,128]{2,1,0:T(8,128)(2,1)S(1)}, bf16[9,8,128]{2,1,0:T(8,128)(2,1)S(1)}, u32[]{:S(2)}, u32[]{:S(2)}) collective-permute-start(bf16[9,8,128]{2,1,0:T(8,128)(2,1)S(1)} %get-tuple-element.23.refs_0_), channel_id=1, source_target_pairs={{0,16},{8,24},{16,0},{24,8},{1,17},{9,25},{17,1},{25,9},{2,18},{10... | collective-permute-start | bytes 55304 | tf_op jit(solution)/shard_map/ppermute | solution.py:328
  8.7 4.7 %collective-permute-start.2 = (bf16[9,8,128]{2,1,0:T(8,128)(2,1)S(1)}, bf16[9,8,128]{2,1,0:T(8,128)(2,1)S(1)}, u32[]{:S(2)}, u32[]{:S(2)}) collective-permute-start(bf16[9,8,128]{2,1,0:T(8,128)(2,1)S(1)} %get-tuple-element.23.refs_0_), channel_id=1, source_target_pairs={{0,24},{8,16},{16,8},{24,0},{1,25},{9,17},{17,9},{25,1},{2,26},{10... | collective-permute-start | bytes 55304 | tf_op jit(solution)/shard_map/ppermute | solution.py:328
  13.4 1.4 %collective-permute-start.3 = (bf16[4,9,8,128]{3,2,1,0:T(8,128)(2,1)S(1)}, bf16[4,9,8,128]{3,2,1,0:T(8,128)(2,1)S(1)}, u32[]{:S(2)}, u32[]{:S(2)}) collective-permute-start(bf16[4,9,8,128]{3,2,1,0:T(8,128)(2,1)S(1)} %stack.1.mine_ref), channel_id=1, source_target_pairs={{0,1},{1,0},{2,3},{3,2},{4,5},{5,4},{6,7},{7,6},{8,9},{9,8},{10,11... | collective-permute-start | bytes 221192 | tf_op jit(solution)/shard_map/ppermute | solution.py:359
  14.9 5.6 %collective-permute-start.4 = (bf16[10,8,128]{2,1,0:T(8,128)(2,1)S(1)}, bf16[10,8,128]{2,1,0:T(8,128)(2,1)S(1)}, u32[]{:S(2)}, u32[]{:S(2)}) collective-permute-start(bf16[10,8,128]{2,1,0:T(8,128)(2,1)S(1)} %get-tuple-element.29), channel_id=1, source_target_pairs={{0,6},{1,7},{2,4},{3,5},{4,2},{5,3},{6,0},{7,1},{8,14},{9,15},{10,... | collective-permute-start | bytes 61448 | tf_op jit(solution)/shard_map/ppermute | solution.py:378
  18.5 4.7 %collective-permute-start.5 = (bf16[10,8,128]{2,1,0:T(8,128)(2,1)S(1)}, bf16[10,8,128]{2,1,0:T(8,128)(2,1)S(1)}, u32[]{:S(2)}, u32[]{:S(2)}) collective-permute-start(bf16[10,8,128]{2,1,0:T(8,128)(2,1)S(1)} %get-tuple-element.30), channel_id=1, source_target_pairs={{0,4},{1,5},{2,6},{3,7},{4,0},{5,1},{6,2},{7,3},{8,12},{9,13},{10,... | collective-permute-start | bytes 61448 | tf_op jit(solution)/shard_map/ppermute | solution.py:378
  18.5 4.7 %collective-permute-start.6 = (bf16[10,8,128]{2,1,0:T(8,128)(2,1)S(1)}, bf16[10,8,128]{2,1,0:T(8,128)(2,1)S(1)}, u32[]{:S(2)}, u32[]{:S(2)}) collective-permute-start(bf16[10,8,128]{2,1,0:T(8,128)(2,1)S(1)} %get-tuple-element.31), channel_id=1, source_target_pairs={{0,2},{1,3},{2,0},{3,1},{4,6},{5,7},{6,4},{7,5},{8,10},{9,11},{10,... | collective-permute-start | bytes 61448 | tf_op jit(solution)/shard_map/ppermute | solution.py:378

commit v10 on v9

--- a/solution.py
+++ b/solution.py
@@ -357,8 +357,6 @@
         name="stack",
     )(*held)
     other = lax.ppermute(mine, "slab", [(s, s ^ 1) for s in range(slabs)])
-    fluctuation = look_up(count // 2, count, [fluctuation])
-    other, fluctuation = lax.optimization_barrier((other, fluctuation))
     sent = pl.pallas_call(
         route_kernel,
         out_shape=[jax.ShapeDtypeStruct((per_device + CORES, 8, AVG), BF16)] * chips,
@@ -368,6 +366,8 @@
         compiler_params=params,
         name="route",
     )(blocks, mine, other)
+    sent, fluctuation = lax.optimization_barrier((sent, fluctuation))
+    fluctuation = look_up(count // 2, count, [fluctuation])
     got = [sent[0]]
     for offset in reversed(range(1, chips)):
         moves = [

time: 24.5 us -> 23.5 us (0.959)
  waiting for transfers between devices: 7.26 us -> 6.21 us
    ppermute x3, waiting for transfers between devices: 3.91 us -> 2.61 us  [local(): got.insert(1, lax.ppermute(sent[offset], 'slab', moves))]
    ppermute x1, waiting for transfers between devices: 0.01 us -> 1.25 us  [local(): other = lax.ppermute(mine, 'slab', [(s, s ^ 1) for s in range(slabs)])]
    ppermute x3, waiting for transfers between devices: 3.35 us -> 2.34 us  [local(): held.append(lax.ppermute(table, 'grp', moves))]
  transfers between devices with their start and end apart: 7 -> 7, of which waited for: 4 -> 4; matrix products, arithmetic and copies ran while one was open for 0% -> 0% of each run, Pallas kernels for 10% -> 11%
where the time goes in v10:
time: 23.5 us; the launch traced here: 23.4 us
  starting transfers between devices  9.15 us (39%)
  Pallas kernels  7.33 us (31%)
  waiting for transfers between devices  6.21 us (26%)
  between operations  0.69 us (3%)
    ppermute x3, starting transfers between devices, local(): held.append(lax.ppermute(table, 'grp', moves))  4.63 us
    ppermute x3, starting transfers between devices, local(): got.insert(1, lax.ppermute(sent[offset], 'slab', moves))  4.45 us
    pallas_call x1, Pallas kernels, local(): pl.pallas_call(functools.partial(sum_kernel, cuts=cuts, blk=blk), out_sha...  3.5 us
    ppermute x3, waiting for transfers between devices, local(): got.insert(1, lax.ppermute(sent[offset], 'slab', moves))  2.61 us
    pallas_call x2, Pallas kernels, look_up(): pl.pallas_call(functools.partial(fluctuation_kernel, begin=begin, end=end...  2.54 us
    ppermute x3, waiting for transfers between devices, local(): held.append(lax.ppermute(table, 'grp', moves))  2.34 us
    ppermute x1, waiting for transfers between devices, local(): other = lax.ppermute(mine, 'slab', [(s, s ^ 1) for s in range(slabs)])  1.25 us
    pallas_call x1, Pallas kernels, local(): pl.pallas_call(functools.partial(place_kernel, groups=groups, chips=chips...  1.16 us
  transfers between devices with their start and end apart: 7, of which 4 were waited for; matrix products, arithmetic and copies ran while one was open for 0% of the time, Pallas kernels for 11%

profile of v10, /device:TPU:0, one launch (start us, length us, event | category | flops | bytes accessed | tf_op | source)
XLA Modules:
  0.0 23.4 jit_solution(10632053082688855740)
XLA Ops:
  0.6 3.5 %sums.1 = (bf16[9,8,128]{2,1,0:T(8,128)(2,1)S(1)}, f32[8,16,128]{2,1,0:T(8,128)S(1)}, f32[16,65536]{1,0:T(8,128)S(1)}, s32[256]{0:T(256)S(4)}, s32[512,128]{1,0:T(8,128)S(1)}) custom-call(s32[512,128]{1,0:T(8,128)} %bitcast.7, f32[2048,128]{1,0:T(8,128)} %bitcast.6, f32[9,65536]{1,0:T(8,128)} %s_hbm.1, s32[256]{0:T(256)} %blocks_hbm.1), custom_call_target="tpu_custom_call" | custom-call | flops 67108864 | bytes 4194304 | tf_op jit(solution)/shard_map/sums/pallas_call | solution.py:299
  4.1 4.0 %collective-permute-start.2 = (bf16[9,8,128]{2,1,0:T(8,128)(2,1)S(1)}, bf16[9,8,128]{2,1,0:T(8,128)(2,1)S(1)}, u32[]{:S(2)}, u32[]{:S(2)}) collective-permute-start(bf16[9,8,128]{2,1,0:T(8,128)(2,1)S(1)} %get-tuple-element.26.refs_0_), channel_id=1, source_target_pairs={{0,24},{8,16},{16,8},{24,0},{1,25},{9,17},{17,9},{25,1},{2,26},{10... | collective-permute-start | bytes 55304 | tf_op jit(solution)/shard_map/ppermute | solution.py:328
  8.1 0.5 %collective-permute-start.1 = (bf16[9,8,128]{2,1,0:T(8,128)(2,1)S(1)}, bf16[9,8,128]{2,1,0:T(8,128)(2,1)S(1)}, u32[]{:S(2)}, u32[]{:S(2)}) collective-permute-start(bf16[9,8,128]{2,1,0:T(8,128)(2,1)S(1)} %get-tuple-element.26.refs_0_), channel_id=1, source_target_pairs={{0,16},{8,24},{16,0},{24,8},{1,17},{9,25},{17,1},{25,9},{2,18},{10... | collective-permute-start | bytes 55304 | tf_op jit(solution)/shard_map/ppermute | solution.py:328
  8.6 0.1 collective-permute-start
  8.8 1.3 %fluctuation.2.refs_0_ = bf16[13,65536]{1,0:T(8,128)(2,1)} custom-call(s32[512,128]{1,0:T(8,128)S(1)} %get-tuple-element.23.ids_ref.refs_4_, f32[16,65536]{1,0:T(8,128)S(1)} %get-tuple-element.24.point_ref.refs_5_, f32[8,16,128]{2,1,0:T(8,128)S(1)} %get-tuple-element.25.window_ref.refs_6_), custom_call_target="tpu_custom_call" | custom-call | flops 33554432 | bytes 3145728 | tf_op jit(solution)/shard_map/fluctuation/pallas_call | solution.py:335
  10.0 0.0 collective-permute-done.2.refs_3_
  10.1 1.8 %collective-permute-done.1.refs_2_ = bf16[9,8,128]{2,1,0:T(8,128)(2,1)S(1)} collective-permute-done((bf16[9,8,128]{2,1,0:T(8,128)(2,1)S(1)}, bf16[9,8,128]{2,1,0:T(8,128)(2,1)S(1)}, u32[]{:S(2)}, u32[]{:S(2)}) %collective-permute-start.1) | collective-permute-done | bytes 18464 | tf_op jit(solution)/shard_map/ppermute | solution.py:328
  11.9 0.5 %collective-permute-done.refs_1_ = bf16[9,8,128]{2,1,0:T(8,128)(2,1)S(1)} collective-permute-done((bf16[9,8,128]{2,1,0:T(8,128)(2,1)S(1)}, bf16[9,8,128]{2,1,0:T(8,128)(2,1)S(1)}, u32[]{:S(2)}, u32[]{:S(2)}) %collective-permute-start) | collective-permute-done | bytes 18464 | tf_op jit(solution)/shard_map/ppermute | solution.py:328
  12.4 0.1 collective-permute-start.3
  12.5 1.3 %collective-permute-done.3.other_ref = bf16[4,9,8,128]{3,2,1,0:T(8,128)(2,1)S(1)} collective-permute-done((bf16[4,9,8,128]{3,2,1,0:T(8,128)(2,1)S(1)}, bf16[4,9,8,128]{3,2,1,0:T(8,128)(2,1)S(1)}, u32[]{:S(2)}, u32[]{:S(2)}) %collective-permute-start.3) | collective-permute-done | bytes 73760 | tf_op jit(solution)/shard_map/ppermute | solution.py:359
  13.7 0.1 route.1
  13.9 3.7 %collective-permute-start.4 = (bf16[10,8,128]{2,1,0:T(8,128)(2,1)S(1)}, bf16[10,8,128]{2,1,0:T(8,128)(2,1)S(1)}, u32[]{:S(2)}, u32[]{:S(2)}) collective-permute-start(bf16[10,8,128]{2,1,0:T(8,128)(2,1)S(1)} %get-tuple-element.35), channel_id=1, source_target_pairs={{0,6},{1,7},{2,4},{3,5},{4,2},{5,3},{6,0},{7,1},{8,14},{9,15},{10,... | collective-permute-start | bytes 61448 | tf_op jit(solution)/shard_map/ppermute | solution.py:378
  17.5 0.0 collective-permute-start.5
  17.5 0.8 %collective-permute-start.6 = (bf16[10,8,128]{2,1,0:T(8,128)(2,1)S(1)}, bf16[10,8,128]{2,1,0:T(8,128)(2,1)S(1)}, u32[]{:S(2)}, u32[]{:S(2)}) collective-permute-start(bf16[10,8,128]{2,1,0:T(8,128)(2,1)S(1)} %get-tuple-element.37), channel_id=1, source_target_pairs={{0,2},{1,3},{2,0},{3,1},{4,6},{5,7},{6,4},{7,5},{8,10},{9,11},{10,... | collective-permute-start | bytes 61448 | tf_op jit(solution)/shard_map/ppermute | solution.py:378
  18.3 1.3 %fluctuation.3.refs_7_ = bf16[13,65536]{1,0:T(8,128)(2,1)} custom-call(s32[512,128]{1,0:T(8,128)S(1)} %get-tuple-element.23.ids_ref.refs_4_, f32[16,65536]{1,0:T(8,128)S(1)} %get-tuple-element.24.point_ref.refs_5_, f32[8,16,128]{2,1,0:T(8,128)S(1)} %get-tuple-element.25.window_ref.refs_6_, ...), custom_call_target="tpu_custom_call", output_to_operand_aliasing={{}: (3, {})} | custom-call | flops 33554432 | bytes 3145728 | tf_op jit(solution)/shard_map/fluctuation/pallas_call | solution.py:335
  19.6 0.0 collective-permute-done.4.refs_0_
  19.6 2.6 %collective-permute-done.5.refs_1_ = bf16[10,8,128]{2,1,0:T(8,128)(2,1)S(1)} collective-permute-done((bf16[10,8,128]{2,1,0:T(8,128)(2,1)S(1)}, bf16[10,8,128]{2,1,0:T(8,128)(2,1)S(1)}, u32[]{:S(2)}, u32[]{:S(2)}) %collective-permute-start.5) | collective-permute-done | bytes 20512 | tf_op jit(solution)/shard_map/ppermute | solution.py:378
  22.2 0.0 collective-permute-done.6.refs_2_
  22.2 1.2 %place.1 = (f32[13,512]{1,0:T(8,128)}, bf16[13,65536]{1,0:T(8,128)(2,1)}) custom-call(s32[256]{0:T(256)S(4)} %get-tuple-element.21.blocks_ref, bf16[10,8,128]{2,1,0:T(8,128)(2,1)S(1)} %collective-permute-done.4.refs_0_, bf16[10,8,128]{2,1,0:T(8,128)(2,1)S(1)} %collective-permute-done.5.refs_1_, ...), custom_call_target="tpu_custom_call", output_to_operand_aliasing={{1}: (8, {})} | custom-call | tf_op jit(solution)/shard_map/place/pallas_call | solution.py:379
  (1 shorter events, 0.0 us)
Async XLA Ops:
  4.1 5.9 %collective-permute-start.2 = (bf16[9,8,128]{2,1,0:T(8,128)(2,1)S(1)}, bf16[9,8,128]{2,1,0:T(8,128)(2,1)S(1)}, u32[]{:S(2)}, u32[]{:S(2)}) collective-permute-start(bf16[9,8,128]{2,1,0:T(8,128)(2,1)S(1)} %get-tuple-element.26.refs_0_), channel_id=1, source_target_pairs={{0,24},{8,16},{16,8},{24,0},{1,25},{9,17},{17,9},{25,1},{2,26},{10... | collective-permute-start | bytes 55304 | tf_op jit(solution)/shard_map/ppermute | solution.py:328
  8.1 3.8 %collective-permute-start.1 = (bf16[9,8,128]{2,1,0:T(8,128)(2,1)S(1)}, bf16[9,8,128]{2,1,0:T(8,128)(2,1)S(1)}, u32[]{:S(2)}, u32[]{:S(2)}) collective-permute-start(bf16[9,8,128]{2,1,0:T(8,128)(2,1)S(1)} %get-tuple-element.26.refs_0_), channel_id=1, source_target_pairs={{0,16},{8,24},{16,0},{24,8},{1,17},{9,25},{17,1},{25,9},{2,18},{10... | collective-permute-start | bytes 55304 | tf_op jit(solution)/shard_map/ppermute | solution.py:328
  8.6 3.8 %collective-permute-start = (bf16[9,8,128]{2,1,0:T(8,128)(2,1)S(1)}, bf16[9,8,128]{2,1,0:T(8,128)(2,1)S(1)}, u32[]{:S(2)}, u32[]{:S(2)}) collective-permute-start(bf16[9,8,128]{2,1,0:T(8,128)(2,1)S(1)} %get-tuple-element.26.refs_0_), channel_id=1, source_target_pairs={{0,8},{8,0},{16,24},{24,16},{1,9},{9,1},{17,25},{25,17},{2,10},{10... | collective-permute-start | bytes 55304 | tf_op jit(solution)/shard_map/ppermute | solution.py:328
  12.4 1.3 %collective-permute-start.3 = (bf16[4,9,8,128]{3,2,1,0:T(8,128)(2,1)S(1)}, bf16[4,9,8,128]{3,2,1,0:T(8,128)(2,1)S(1)}, u32[]{:S(2)}, u32[]{:S(2)}) collective-permute-start(bf16[4,9,8,128]{3,2,1,0:T(8,128)(2,1)S(1)} %stack.1.mine_ref), channel_id=1, source_target_pairs={{0,1},{1,0},{2,3},{3,2},{4,5},{5,4},{6,7},{7,6},{8,9},{9,8},{10,11... | collective-permute-start | bytes 221192 | tf_op jit(solution)/shard_map/ppermute | solution.py:359
  13.9 5.7 %collective-permute-start.4 = (bf16[10,8,128]{2,1,0:T(8,128)(2,1)S(1)}, bf16[10,8,128]{2,1,0:T(8,128)(2,1)S(1)}, u32[]{:S(2)}, u32[]{:S(2)}) collective-permute-start(bf16[10,8,128]{2,1,0:T(8,128)(2,1)S(1)} %get-tuple-element.35), channel_id=1, source_target_pairs={{0,6},{1,7},{2,4},{3,5},{4,2},{5,3},{6,0},{7,1},{8,14},{9,15},{10,... | collective-permute-start | bytes 61448 | tf_op jit(solution)/shard_map/ppermute | solution.py:378
  17.5 4.7 %collective-permute-start.5 = (bf16[10,8,128]{2,1,0:T(8,128)(2,1)S(1)}, bf16[10,8,128]{2,1,0:T(8,128)(2,1)S(1)}, u32[]{:S(2)}, u32[]{:S(2)}) collective-permute-start(bf16[10,8,128]{2,1,0:T(8,128)(2,1)S(1)} %get-tuple-element.36), channel_id=1, source_target_pairs={{0,4},{1,5},{2,6},{3,7},{4,0},{5,1},{6,2},{7,3},{8,12},{9,13},{10,... | collective-permute-start | bytes 61448 | tf_op jit(solution)/shard_map/ppermute | solution.py:378
  17.5 4.7 %collective-permute-start.6 = (bf16[10,8,128]{2,1,0:T(8,128)(2,1)S(1)}, bf16[10,8,128]{2,1,0:T(8,128)(2,1)S(1)}, u32[]{:S(2)}, u32[]{:S(2)}) collective-permute-start(bf16[10,8,128]{2,1,0:T(8,128)(2,1)S(1)} %get-tuple-element.37), channel_id=1, source_target_pairs={{0,2},{1,3},{2,0},{3,1},{4,6},{5,7},{6,4},{7,5},{8,10},{9,11},{10,... | collective-permute-start | bytes 61448 | tf_op jit(solution)/shard_map/ppermute | solution.py:378

commit v11 on v10

--- a/solution.py
+++ b/solution.py
@@ -248,7 +248,6 @@
                 edge_ref.at[:, lanes], fluctuation_hbm.at[:, points], sems.at[end]
             )
         )
-        copies[-1].start()
 
     tiles, columns = [], []
     sums = jnp.zeros((8, AVG), F32)
@@ -271,8 +270,9 @@
         lanes = slice(pair * AVG, (pair + 1) * AVG)
         table_ref[:8, lanes] = jnp.where(half, first, pltpu.roll(second, blk, 1))
         table_ref[8:, lanes] = jnp.where(half, pltpu.roll(first, blk, 1), second)[: COUNT - 8]
-    copies.append(pltpu.make_async_copy(table_ref, table_hbm, sems.at[2]))
-    copies[-1].start()
+    copies.insert(0, pltpu.make_async_copy(table_ref, table_hbm, sems.at[2]))
+    for copy in copies:
+        copy.start()
     for copy in copies:
         copy.wait()
 

time: 23.5 us -> 23.5 us (level)
  no operation moved by 1% of the time
where the time goes in v11:
time: 23.5 us; the launch traced here: 23.4 us
  starting transfers between devices  9.15 us (39%)
  Pallas kernels  7.33 us (31%)
  waiting for transfers between devices  6.21 us (26%)
  between operations  0.69 us (3%)
    ppermute x3, starting transfers between devices, local(): held.append(lax.ppermute(table, 'grp', moves))  4.63 us
    ppermute x3, starting transfers between devices, local(): got.insert(1, lax.ppermute(sent[offset], 'slab', moves))  4.45 us
    pallas_call x1, Pallas kernels, local(): pl.pallas_call(functools.partial(sum_kernel, cuts=cuts, blk=blk), out_sha...  3.5 us
    ppermute x3, waiting for transfers between devices, local(): got.insert(1, lax.ppermute(sent[offset], 'slab', moves))  2.61 us
    pallas_call x2, Pallas kernels, look_up(): pl.pallas_call(functools.partial(fluctuation_kernel, begin=begin, end=end...  2.54 us
    ppermute x3, waiting for transfers between devices, local(): held.append(lax.ppermute(table, 'grp', moves))  2.34 us
    ppermute x1, waiting for transfers between devices, local(): other = lax.ppermute(mine, 'slab', [(s, s ^ 1) for s in range(slabs)])  1.25 us
    pallas_call x1, Pallas kernels, local(): pl.pallas_call(functools.partial(place_kernel, groups=groups, chips=chips...  1.17 us
  transfers between devices with their start and end apart: 7, of which 4 were waited for; matrix products, arithmetic and copies ran while one was open for 0% of the time, Pallas kernels for 11%

profile of v11, /device:TPU:0, one launch (start us, length us, event | category | flops | bytes accessed | tf_op | source)
XLA Modules:
  0.0 23.4 jit_solution(17480621767510914426)
XLA Ops:
  0.6 3.5 %sums.1 = (bf16[9,8,128]{2,1,0:T(8,128)(2,1)S(1)}, f32[8,16,128]{2,1,0:T(8,128)S(1)}, f32[16,65536]{1,0:T(8,128)S(1)}, s32[256]{0:T(256)S(4)}, s32[512,128]{1,0:T(8,128)S(1)}) custom-call(s32[512,128]{1,0:T(8,128)} %bitcast.7, f32[2048,128]{1,0:T(8,128)} %bitcast.6, f32[9,65536]{1,0:T(8,128)} %s_hbm.1, s32[256]{0:T(256)} %blocks_hbm.1), custom_call_target="tpu_custom_call" | custom-call | flops 67108864 | bytes 4194304 | tf_op jit(solution)/shard_map/sums/pallas_call | solution.py:299
  4.1 4.0 %collective-permute-start.2 = (bf16[9,8,128]{2,1,0:T(8,128)(2,1)S(1)}, bf16[9,8,128]{2,1,0:T(8,128)(2,1)S(1)}, u32[]{:S(2)}, u32[]{:S(2)}) collective-permute-start(bf16[9,8,128]{2,1,0:T(8,128)(2,1)S(1)} %get-tuple-element.26.refs_0_), channel_id=1, source_target_pairs={{0,24},{8,16},{16,8},{24,0},{1,25},{9,17},{17,9},{25,1},{2,26},{10... | collective-permute-start | bytes 55304 | tf_op jit(solution)/shard_map/ppermute | solution.py:328
  8.1 0.5 %collective-permute-start.1 = (bf16[9,8,128]{2,1,0:T(8,128)(2,1)S(1)}, bf16[9,8,128]{2,1,0:T(8,128)(2,1)S(1)}, u32[]{:S(2)}, u32[]{:S(2)}) collective-permute-start(bf16[9,8,128]{2,1,0:T(8,128)(2,1)S(1)} %get-tuple-element.26.refs_0_), channel_id=1, source_target_pairs={{0,16},{8,24},{16,0},{24,8},{1,17},{9,25},{17,1},{25,9},{2,18},{10... | collective-permute-start | bytes 55304 | tf_op jit(solution)/shard_map/ppermute | solution.py:328
  8.6 0.1 collective-permute-start
  8.8 1.3 %fluctuation.2.refs_0_ = bf16[13,65536]{1,0:T(8,128)(2,1)} custom-call(s32[512,128]{1,0:T(8,128)S(1)} %get-tuple-element.23.ids_ref.refs_4_, f32[16,65536]{1,0:T(8,128)S(1)} %get-tuple-element.24.point_ref.refs_5_, f32[8,16,128]{2,1,0:T(8,128)S(1)} %get-tuple-element.25.window_ref.refs_6_), custom_call_target="tpu_custom_call" | custom-call | flops 33554432 | bytes 3145728 | tf_op jit(solution)/shard_map/fluctuation/pallas_call | solution.py:335
  10.0 0.0 collective-permute-done.2.refs_3_
  10.1 1.8 %collective-permute-done.1.refs_2_ = bf16[9,8,128]{2,1,0:T(8,128)(2,1)S(1)} collective-permute-done((bf16[9,8,128]{2,1,0:T(8,128)(2,1)S(1)}, bf16[9,8,128]{2,1,0:T(8,128)(2,1)S(1)}, u32[]{:S(2)}, u32[]{:S(2)}) %collective-permute-start.1) | collective-permute-done | bytes 18464 | tf_op jit(solution)/shard_map/ppermute | solution.py:328
  11.9 0.5 %collective-permute-done.refs_1_ = bf16[9,8,128]{2,1,0:T(8,128)(2,1)S(1)} collective-permute-done((bf16[9,8,128]{2,1,0:T(8,128)(2,1)S(1)}, bf16[9,8,128]{2,1,0:T(8,128)(2,1)S(1)}, u32[]{:S(2)}, u32[]{:S(2)}) %collective-permute-start) | collective-permute-done | bytes 18464 | tf_op jit(solution)/shard_map/ppermute | solution.py:328
  12.4 0.1 collective-permute-start.3
  12.5 1.3 %collective-permute-done.3.other_ref = bf16[4,9,8,128]{3,2,1,0:T(8,128)(2,1)S(1)} collective-permute-done((bf16[4,9,8,128]{3,2,1,0:T(8,128)(2,1)S(1)}, bf16[4,9,8,128]{3,2,1,0:T(8,128)(2,1)S(1)}, u32[]{:S(2)}, u32[]{:S(2)}) %collective-permute-start.3) | collective-permute-done | bytes 73760 | tf_op jit(solution)/shard_map/ppermute | solution.py:359
  13.7 0.1 route.1
  13.9 3.7 %collective-permute-start.4 = (bf16[10,8,128]{2,1,0:T(8,128)(2,1)S(1)}, bf16[10,8,128]{2,1,0:T(8,128)(2,1)S(1)}, u32[]{:S(2)}, u32[]{:S(2)}) collective-permute-start(bf16[10,8,128]{2,1,0:T(8,128)(2,1)S(1)} %get-tuple-element.35), channel_id=1, source_target_pairs={{0,6},{1,7},{2,4},{3,5},{4,2},{5,3},{6,0},{7,1},{8,14},{9,15},{10,... | collective-permute-start | bytes 61448 | tf_op jit(solution)/shard_map/ppermute | solution.py:378
  17.5 0.0 collective-permute-start.5
  17.5 0.8 %collective-permute-start.6 = (bf16[10,8,128]{2,1,0:T(8,128)(2,1)S(1)}, bf16[10,8,128]{2,1,0:T(8,128)(2,1)S(1)}, u32[]{:S(2)}, u32[]{:S(2)}) collective-permute-start(bf16[10,8,128]{2,1,0:T(8,128)(2,1)S(1)} %get-tuple-element.37), channel_id=1, source_target_pairs={{0,2},{1,3},{2,0},{3,1},{4,6},{5,7},{6,4},{7,5},{8,10},{9,11},{10,... | collective-permute-start | bytes 61448 | tf_op jit(solution)/shard_map/ppermute | solution.py:378
  18.3 1.3 %fluctuation.3.refs_7_ = bf16[13,65536]{1,0:T(8,128)(2,1)} custom-call(s32[512,128]{1,0:T(8,128)S(1)} %get-tuple-element.23.ids_ref.refs_4_, f32[16,65536]{1,0:T(8,128)S(1)} %get-tuple-element.24.point_ref.refs_5_, f32[8,16,128]{2,1,0:T(8,128)S(1)} %get-tuple-element.25.window_ref.refs_6_, ...), custom_call_target="tpu_custom_call", output_to_operand_aliasing={{}: (3, {})} | custom-call | flops 33554432 | bytes 3145728 | tf_op jit(solution)/shard_map/fluctuation/pallas_call | solution.py:335
  19.6 0.0 collective-permute-done.4.refs_0_
  19.6 2.6 %collective-permute-done.5.refs_1_ = bf16[10,8,128]{2,1,0:T(8,128)(2,1)S(1)} collective-permute-done((bf16[10,8,128]{2,1,0:T(8,128)(2,1)S(1)}, bf16[10,8,128]{2,1,0:T(8,128)(2,1)S(1)}, u32[]{:S(2)}, u32[]{:S(2)}) %collective-permute-start.5) | collective-permute-done | bytes 20512 | tf_op jit(solution)/shard_map/ppermute | solution.py:378
  22.2 0.0 collective-permute-done.6.refs_2_
  22.2 1.2 %place.1 = (f32[13,512]{1,0:T(8,128)}, bf16[13,65536]{1,0:T(8,128)(2,1)}) custom-call(s32[256]{0:T(256)S(4)} %get-tuple-element.21.blocks_ref, bf16[10,8,128]{2,1,0:T(8,128)(2,1)S(1)} %collective-permute-done.4.refs_0_, bf16[10,8,128]{2,1,0:T(8,128)(2,1)S(1)} %collective-permute-done.5.refs_1_, ...), custom_call_target="tpu_custom_call", output_to_operand_aliasing={{1}: (8, {})} | custom-call | tf_op jit(solution)/shard_map/place/pallas_call | solution.py:379
  (1 shorter events, 0.0 us)
Async XLA Ops:
  4.1 5.9 %collective-permute-start.2 = (bf16[9,8,128]{2,1,0:T(8,128)(2,1)S(1)}, bf16[9,8,128]{2,1,0:T(8,128)(2,1)S(1)}, u32[]{:S(2)}, u32[]{:S(2)}) collective-permute-start(bf16[9,8,128]{2,1,0:T(8,128)(2,1)S(1)} %get-tuple-element.26.refs_0_), channel_id=1, source_target_pairs={{0,24},{8,16},{16,8},{24,0},{1,25},{9,17},{17,9},{25,1},{2,26},{10... | collective-permute-start | bytes 55304 | tf_op jit(solution)/shard_map/ppermute | solution.py:328
  8.1 3.8 %collective-permute-start.1 = (bf16[9,8,128]{2,1,0:T(8,128)(2,1)S(1)}, bf16[9,8,128]{2,1,0:T(8,128)(2,1)S(1)}, u32[]{:S(2)}, u32[]{:S(2)}) collective-permute-start(bf16[9,8,128]{2,1,0:T(8,128)(2,1)S(1)} %get-tuple-element.26.refs_0_), channel_id=1, source_target_pairs={{0,16},{8,24},{16,0},{24,8},{1,17},{9,25},{17,1},{25,9},{2,18},{10... | collective-permute-start | bytes 55304 | tf_op jit(solution)/shard_map/ppermute | solution.py:328
  8.6 3.8 %collective-permute-start = (bf16[9,8,128]{2,1,0:T(8,128)(2,1)S(1)}, bf16[9,8,128]{2,1,0:T(8,128)(2,1)S(1)}, u32[]{:S(2)}, u32[]{:S(2)}) collective-permute-start(bf16[9,8,128]{2,1,0:T(8,128)(2,1)S(1)} %get-tuple-element.26.refs_0_), channel_id=1, source_target_pairs={{0,8},{8,0},{16,24},{24,16},{1,9},{9,1},{17,25},{25,17},{2,10},{10... | collective-permute-start | bytes 55304 | tf_op jit(solution)/shard_map/ppermute | solution.py:328
  12.4 1.3 %collective-permute-start.3 = (bf16[4,9,8,128]{3,2,1,0:T(8,128)(2,1)S(1)}, bf16[4,9,8,128]{3,2,1,0:T(8,128)(2,1)S(1)}, u32[]{:S(2)}, u32[]{:S(2)}) collective-permute-start(bf16[4,9,8,128]{3,2,1,0:T(8,128)(2,1)S(1)} %stack.1.mine_ref), channel_id=1, source_target_pairs={{0,1},{1,0},{2,3},{3,2},{4,5},{5,4},{6,7},{7,6},{8,9},{9,8},{10,11... | collective-permute-start | bytes 221192 | tf_op jit(solution)/shard_map/ppermute | solution.py:359
  13.9 5.7 %collective-permute-start.4 = (bf16[10,8,128]{2,1,0:T(8,128)(2,1)S(1)}, bf16[10,8,128]{2,1,0:T(8,128)(2,1)S(1)}, u32[]{:S(2)}, u32[]{:S(2)}) collective-permute-start(bf16[10,8,128]{2,1,0:T(8,128)(2,1)S(1)} %get-tuple-element.35), channel_id=1, source_target_pairs={{0,6},{1,7},{2,4},{3,5},{4,2},{5,3},{6,0},{7,1},{8,14},{9,15},{10,... | collective-permute-start | bytes 61448 | tf_op jit(solution)/shard_map/ppermute | solution.py:378
  17.5 4.7 %collective-permute-start.5 = (bf16[10,8,128]{2,1,0:T(8,128)(2,1)S(1)}, bf16[10,8,128]{2,1,0:T(8,128)(2,1)S(1)}, u32[]{:S(2)}, u32[]{:S(2)}) collective-permute-start(bf16[10,8,128]{2,1,0:T(8,128)(2,1)S(1)} %get-tuple-element.36), channel_id=1, source_target_pairs={{0,4},{1,5},{2,6},{3,7},{4,0},{5,1},{6,2},{7,3},{8,12},{9,13},{10,... | collective-permute-start | bytes 61448 | tf_op jit(solution)/shard_map/ppermute | solution.py:378
  17.5 4.7 %collective-permute-start.6 = (bf16[10,8,128]{2,1,0:T(8,128)(2,1)S(1)}, bf16[10,8,128]{2,1,0:T(8,128)(2,1)S(1)}, u32[]{:S(2)}, u32[]{:S(2)}) collective-permute-start(bf16[10,8,128]{2,1,0:T(8,128)(2,1)S(1)} %get-tuple-element.37), channel_id=1, source_target_pairs={{0,2},{1,3},{2,0},{3,1},{4,6},{5,7},{6,4},{7,5},{8,10},{9,11},{10,... | collective-permute-start | bytes 61448 | tf_op jit(solution)/shard_map/ppermute | solution.py:378

commit v12 on v11

--- a/solution.py
+++ b/solution.py
@@ -160,28 +160,27 @@
     return (me + offset) % count
 
 
-def stack_kernel(*refs):
-    *held_refs, out_ref = refs
-    for offset, ref in enumerate(held_refs):
-        out_ref[source(lax.axis_index("grp"), offset, len(held_refs))] = ref[...]
-
-
-def route_kernel(blocks_ref, mine_ref, other_ref, *refs):
-    *out_refs, held_ref = refs
+def pair_kernel(mine_ref, other_ref, out_ref):
+    core = div_rem(lax.axis_index("slab"), CORES)[1]
+    out_ref[core] = mine_ref[...]
+    out_ref[1 - core] = other_ref[...]
+
+
+def route_kernel(blocks_ref, *refs, groups):
+    pair_refs, (*out_refs, held_ref) = refs[:groups], refs[groups:]
     chips = len(out_refs)
-    groups, slots = mine_ref.shape[:2]
-    per_device = slots - 1
+    per_device = held_ref.shape[2] - 1
     slabs = chips * CORES
     group = lax.axis_index("grp")
     chip, core = div_rem(lax.axis_index("slab"), CORES)
-    held_ref[core] = mine_ref[...]
-    held_ref[1 - core] = other_ref[...]
+    for offset, ref in enumerate(pair_refs):
+        held_ref[source(group, offset, groups)] = ref[...]
     step = AVG // 2 // groups
     lane = lax.broadcasted_iota(jnp.int32, (8, AVG), 1) & (AVG // 2 - 1)
     for owner_core in range(CORES):
-        ends = held_ref[owner_core, 0, per_device].astype(F32)
+        ends = held_ref[0, owner_core, per_device].astype(F32)
         for owner_group in range(1, groups):
-            rolled = pltpu.roll(held_ref[owner_core, owner_group, per_device].astype(F32), owner_group * step, 1)
+            rolled = pltpu.roll(held_ref[owner_group, owner_core, per_device].astype(F32), owner_group * step, 1)
             ends = jnp.where(lane >= owner_group * step, rolled, ends)
         for out_ref in out_refs:
             out_ref[per_device + owner_core] = ends.astype(BF16)
@@ -190,7 +189,7 @@
         for slot in range(per_device):
             owner, index = div_rem(blocks_ref[wanted + slot], per_device)
             owner_group, owner_slab = div_rem(owner, slabs)
-            out_ref[slot] = held_ref[div_rem(owner_slab, CORES)[1], owner_group, index]
+            out_ref[slot] = held_ref[owner_group, div_rem(owner_slab, CORES)[1], index]
 
 
 def place_kernel(blocks_ref, *refs, groups, chips, blk):
@@ -322,10 +321,19 @@
     )(*in_hbm)
     blocks = pltpu.with_memory_space_constraint(blocks, pltpu.SMEM)
 
-    held = [table]
+    other = lax.ppermute(table, "slab", [(s, s ^ 1) for s in range(slabs)])
+    pair = pl.pallas_call(
+        pair_kernel,
+        out_shape=jax.ShapeDtypeStruct((CORES, slots, 8, AVG), BF16),
+        in_specs=[vmem, vmem],
+        out_specs=vmem,
+        compiler_params=params,
+        name="pair",
+    )(table, other)
+    held = [pair]
     for offset in range(1, groups):
         moves = [(g, int(target(g, offset, groups))) for g in range(groups)]
-        held.append(lax.ppermute(table, "grp", moves))
+        held.append(lax.ppermute(pair, "grp", moves))
 
     on_chip = (on_chip_ids, point, windows)
     count = tiles // blk
@@ -348,24 +356,15 @@
 
     fluctuation = look_up(0, count // 2, [])
     held, fluctuation = lax.optimization_barrier((held, fluctuation))
-    mine = pl.pallas_call(
-        stack_kernel,
-        out_shape=jax.ShapeDtypeStruct((groups, slots, 8, AVG), BF16),
-        in_specs=[vmem] * groups,
-        out_specs=vmem,
-        compiler_params=params,
-        name="stack",
-    )(*held)
-    other = lax.ppermute(mine, "slab", [(s, s ^ 1) for s in range(slabs)])
     sent = pl.pallas_call(
-        route_kernel,
+        functools.partial(route_kernel, groups=groups),
         out_shape=[jax.ShapeDtypeStruct((per_device + CORES, 8, AVG), BF16)] * chips,
-        in_specs=[smem, vmem, vmem],
+        in_specs=[smem] + [vmem] * groups,
         out_specs=[vmem] * chips,
-        scratch_shapes=[pltpu.VMEM((CORES, groups, slots, 8, AVG), BF16)],
+        scratch_shapes=[pltpu.VMEM((groups, CORES, slots, 8, AVG), BF16)],
         compiler_params=params,
         name="route",
-    )(blocks, mine, other)
+    )(blocks, *held)
     sent, fluctuation = lax.optimization_barrier((sent, fluctuation))
     fluctuation = look_up(count // 2, count, [fluctuation])
     got = [sent[0]]

time: 23.5 us -> 23.6 us (level)
  starting transfers between devices: 9.15 us -> 9.42 us
    ppermute x4, starting transfers between devices: 4.7 us -> 4.97 us  [the longest x3 4.41 us: local(): held.append(lax.ppermute(pair, 'grp', moves))]
where the time goes in v12:
time: 23.6 us; the launch traced here: 23.4 us
  starting transfers between devices  9.42 us (40%)
  Pallas kernels  7.33 us (31%)
  waiting for transfers between devices  6.01 us (25%)
  between operations  0.67 us (3%)
    ppermute x3, starting transfers between devices, local(): got.insert(1, lax.ppermute(sent[offset], 'slab', moves))  4.45 us
    ppermute x3, starting transfers between devices, local(): held.append(lax.ppermute(pair, 'grp', moves))  4.41 us
    pallas_call x1, Pallas kernels, local(): pl.pallas_call(functools.partial(sum_kernel, cuts=cuts, blk=blk), out_sha...  3.5 us
    ppermute x3, waiting for transfers between devices, local(): got.insert(1, lax.ppermute(sent[offset], 'slab', moves))  2.62 us
    ppermute x3, waiting for transfers between devices, local(): held.append(lax.ppermute(pair, 'grp', moves))  2.55 us
    pallas_call x2, Pallas kernels, look_up(): pl.pallas_call(functools.partial(fluctuation_kernel, begin=begin, end=end...  2.54 us
    pallas_call x1, Pallas kernels, local(): pl.pallas_call(functools.partial(place_kernel, groups=groups, chips=chips...  1.17 us
    ppermute x1, waiting for transfers between devices, local(): other = lax.ppermute(table, 'slab', [(s, s ^ 1) for s in range(slabs)])  0.84 us
  transfers between devices with their start and end apart: 7, of which 4 were waited for; matrix products, arithmetic and copies ran while one was open for 0% of the time, Pallas kernels for 11%

profile of v12, /device:TPU:0, one launch (start us, length us, event | category | flops | bytes accessed | tf_op | source)
XLA Modules:
  0.0 23.4 jit_solution(11224906605496505423)
XLA Ops:
  0.6 3.5 %sums.1 = (bf16[9,8,128]{2,1,0:T(8,128)(2,1)S(1)}, f32[8,16,128]{2,1,0:T(8,128)S(1)}, f32[16,65536]{1,0:T(8,128)S(1)}, s32[256]{0:T(256)S(4)}, s32[512,128]{1,0:T(8,128)S(1)}) custom-call(s32[512,128]{1,0:T(8,128)} %bitcast.7, f32[2048,128]{1,0:T(8,128)} %bitcast.6, f32[9,65536]{1,0:T(8,128)} %s_hbm.1, s32[256]{0:T(256)} %blocks_hbm.1), custom_call_target="tpu_custom_call" | custom-call | flops 67108864 | bytes 4194304 | tf_op jit(solution)/shard_map/sums/pallas_call | solution.py:298
  4.1 0.6 %collective-permute-start = (bf16[9,8,128]{2,1,0:T(8,128)(2,1)S(1)}, bf16[9,8,128]{2,1,0:T(8,128)(2,1)S(1)}, u32[]{:S(2)}, u32[]{:S(2)}) collective-permute-start(bf16[9,8,128]{2,1,0:T(8,128)(2,1)S(1)} %get-tuple-element.22.mine_ref), channel_id=1, source_target_pairs={{0,1},{1,0},{2,3},{3,2},{4,5},{5,4},{6,7},{7,6},{8,9},{9,8},{10,11... | collective-permute-start | bytes 55304 | tf_op jit(solution)/shard_map/ppermute | solution.py:324
  4.7 0.8 %collective-permute-done.other_ref = bf16[9,8,128]{2,1,0:T(8,128)(2,1)S(1)} collective-permute-done((bf16[9,8,128]{2,1,0:T(8,128)(2,1)S(1)}, bf16[9,8,128]{2,1,0:T(8,128)(2,1)S(1)}, u32[]{:S(2)}, u32[]{:S(2)}) %collective-permute-start) | collective-permute-done | bytes 18464 | tf_op jit(solution)/shard_map/ppermute | solution.py:324
  5.5 3.8 %collective-permute-start.3 = (bf16[2,9,8,128]{3,2,1,0:T(8,128)(2,1)S(1)}, bf16[2,9,8,128]{3,2,1,0:T(8,128)(2,1)S(1)}, u32[]{:S(2)}, u32[]{:S(2)}) collective-permute-start(bf16[2,9,8,128]{3,2,1,0:T(8,128)(2,1)S(1)} %pair.1.refs_0_), channel_id=1, source_target_pairs={{0,24},{8,16},{16,8},{24,0},{1,25},{9,17},{17,9},{25,1},{2,26},{10... | collective-permute-start | bytes 110600 | tf_op jit(solution)/shard_map/ppermute | solution.py:336
  9.3 0.5 %collective-permute-start.2 = (bf16[2,9,8,128]{3,2,1,0:T(8,128)(2,1)S(1)}, bf16[2,9,8,128]{3,2,1,0:T(8,128)(2,1)S(1)}, u32[]{:S(2)}, u32[]{:S(2)}) collective-permute-start(bf16[2,9,8,128]{3,2,1,0:T(8,128)(2,1)S(1)} %pair.1.refs_0_), channel_id=1, source_target_pairs={{0,16},{8,24},{16,0},{24,8},{1,17},{9,25},{17,1},{25,9},{2,18},{10... | collective-permute-start | bytes 110600 | tf_op jit(solution)/shard_map/ppermute | solution.py:336
  9.8 0.1 collective-permute-start.1
  10.0 1.3 %fluctuation.2.refs_0_ = bf16[13,65536]{1,0:T(8,128)(2,1)} custom-call(s32[512,128]{1,0:T(8,128)S(1)} %get-tuple-element.23.ids_ref.refs_4_, f32[16,65536]{1,0:T(8,128)S(1)} %get-tuple-element.24.point_ref.refs_5_, f32[8,16,128]{2,1,0:T(8,128)S(1)} %get-tuple-element.25.window_ref.refs_6_), custom_call_target="tpu_custom_call" | custom-call | flops 33554432 | bytes 3145728 | tf_op jit(solution)/shard_map/fluctuation/pallas_call | solution.py:343
  11.2 0.0 collective-permute-done.3.refs_3_
  11.3 2.0 %collective-permute-done.2.refs_2_ = bf16[2,9,8,128]{3,2,1,0:T(8,128)(2,1)S(1)} collective-permute-done((bf16[2,9,8,128]{3,2,1,0:T(8,128)(2,1)S(1)}, bf16[2,9,8,128]{3,2,1,0:T(8,128)(2,1)S(1)}, u32[]{:S(2)}, u32[]{:S(2)}) %collective-permute-start.2) | collective-permute-done | bytes 36896 | tf_op jit(solution)/shard_map/ppermute | solution.py:336
  13.3 0.5 %collective-permute-done.1.refs_1_ = bf16[2,9,8,128]{3,2,1,0:T(8,128)(2,1)S(1)} collective-permute-done((bf16[2,9,8,128]{3,2,1,0:T(8,128)(2,1)S(1)}, bf16[2,9,8,128]{3,2,1,0:T(8,128)(2,1)S(1)}, u32[]{:S(2)}, u32[]{:S(2)}) %collective-permute-start.1) | collective-permute-done | bytes 36896 | tf_op jit(solution)/shard_map/ppermute | solution.py:336
  13.8 0.1 route.1
  13.9 3.7 %collective-permute-start.4 = (bf16[10,8,128]{2,1,0:T(8,128)(2,1)S(1)}, bf16[10,8,128]{2,1,0:T(8,128)(2,1)S(1)}, u32[]{:S(2)}, u32[]{:S(2)}) collective-permute-start(bf16[10,8,128]{2,1,0:T(8,128)(2,1)S(1)} %get-tuple-element.35), channel_id=1, source_target_pairs={{0,6},{1,7},{2,4},{3,5},{4,2},{5,3},{6,0},{7,1},{8,14},{9,15},{10,... | collective-permute-start | bytes 61448 | tf_op jit(solution)/shard_map/ppermute | solution.py:377
  17.6 0.0 collective-permute-start.5
  17.6 0.8 %collective-permute-start.6 = (bf16[10,8,128]{2,1,0:T(8,128)(2,1)S(1)}, bf16[10,8,128]{2,1,0:T(8,128)(2,1)S(1)}, u32[]{:S(2)}, u32[]{:S(2)}) collective-permute-start(bf16[10,8,128]{2,1,0:T(8,128)(2,1)S(1)} %get-tuple-element.37), channel_id=1, source_target_pairs={{0,2},{1,3},{2,0},{3,1},{4,6},{5,7},{6,4},{7,5},{8,10},{9,11},{10,... | collective-permute-start | bytes 61448 | tf_op jit(solution)/shard_map/ppermute | solution.py:377
  18.4 1.3 %fluctuation.3.refs_7_ = bf16[13,65536]{1,0:T(8,128)(2,1)} custom-call(s32[512,128]{1,0:T(8,128)S(1)} %get-tuple-element.23.ids_ref.refs_4_, f32[16,65536]{1,0:T(8,128)S(1)} %get-tuple-element.24.point_ref.refs_5_, f32[8,16,128]{2,1,0:T(8,128)S(1)} %get-tuple-element.25.window_ref.refs_6_, ...), custom_call_target="tpu_custom_call", output_to_operand_aliasing={{}: (3, {})} | custom-call | flops 33554432 | bytes 3145728 | tf_op jit(solution)/shard_map/fluctuation/pallas_call | solution.py:343
  19.6 0.0 collective-permute-done.4.refs_0_
  19.7 2.6 %collective-permute-done.5.refs_1_ = bf16[10,8,128]{2,1,0:T(8,128)(2,1)S(1)} collective-permute-done((bf16[10,8,128]{2,1,0:T(8,128)(2,1)S(1)}, bf16[10,8,128]{2,1,0:T(8,128)(2,1)S(1)}, u32[]{:S(2)}, u32[]{:S(2)}) %collective-permute-start.5) | collective-permute-done | bytes 20512 | tf_op jit(solution)/shard_map/ppermute | solution.py:377
  22.3 0.0 collective-permute-done.6.refs_2_
  22.3 1.2 %place.1 = (f32[13,512]{1,0:T(8,128)}, bf16[13,65536]{1,0:T(8,128)(2,1)}) custom-call(s32[256]{0:T(256)S(4)} %get-tuple-element.21.blocks_ref, bf16[10,8,128]{2,1,0:T(8,128)(2,1)S(1)} %collective-permute-done.4.refs_0_, bf16[10,8,128]{2,1,0:T(8,128)(2,1)S(1)} %collective-permute-done.5.refs_1_, ...), custom_call_target="tpu_custom_call", output_to_operand_aliasing={{1}: (8, {})} | custom-call | tf_op jit(solution)/shard_map/place/pallas_call | solution.py:378
  (1 shorter events, 0.0 us)
Async XLA Ops:
  4.1 1.4 %collective-permute-start = (bf16[9,8,128]{2,1,0:T(8,128)(2,1)S(1)}, bf16[9,8,128]{2,1,0:T(8,128)(2,1)S(1)}, u32[]{:S(2)}, u32[]{:S(2)}) collective-permute-start(bf16[9,8,128]{2,1,0:T(8,128)(2,1)S(1)} %get-tuple-element.22.mine_ref), channel_id=1, source_target_pairs={{0,1},{1,0},{2,3},{3,2},{4,5},{5,4},{6,7},{7,6},{8,9},{9,8},{10,11... | collective-permute-start | bytes 55304 | tf_op jit(solution)/shard_map/ppermute | solution.py:324
  5.5 5.7 %collective-permute-start.3 = (bf16[2,9,8,128]{3,2,1,0:T(8,128)(2,1)S(1)}, bf16[2,9,8,128]{3,2,1,0:T(8,128)(2,1)S(1)}, u32[]{:S(2)}, u32[]{:S(2)}) collective-permute-start(bf16[2,9,8,128]{3,2,1,0:T(8,128)(2,1)S(1)} %pair.1.refs_0_), channel_id=1, source_target_pairs={{0,24},{8,16},{16,8},{24,0},{1,25},{9,17},{17,9},{25,1},{2,26},{10... | collective-permute-start | bytes 110600 | tf_op jit(solution)/shard_map/ppermute | solution.py:336
  9.3 4.0 %collective-permute-start.2 = (bf16[2,9,8,128]{3,2,1,0:T(8,128)(2,1)S(1)}, bf16[2,9,8,128]{3,2,1,0:T(8,128)(2,1)S(1)}, u32[]{:S(2)}, u32[]{:S(2)}) collective-permute-start(bf16[2,9,8,128]{3,2,1,0:T(8,128)(2,1)S(1)} %pair.1.refs_0_), channel_id=1, source_target_pairs={{0,16},{8,24},{16,0},{24,8},{1,17},{9,25},{17,1},{25,9},{2,18},{10... | collective-permute-start | bytes 110600 | tf_op jit(solution)/shard_map/ppermute | solution.py:336
  9.8 4.0 %collective-permute-start.1 = (bf16[2,9,8,128]{3,2,1,0:T(8,128)(2,1)S(1)}, bf16[2,9,8,128]{3,2,1,0:T(8,128)(2,1)S(1)}, u32[]{:S(2)}, u32[]{:S(2)}) collective-permute-start(bf16[2,9,8,128]{3,2,1,0:T(8,128)(2,1)S(1)} %pair.1.refs_0_), channel_id=1, source_target_pairs={{0,8},{8,0},{16,24},{24,16},{1,9},{9,1},{17,25},{25,17},{2,10},{10... | collective-permute-start | bytes 110600 | tf_op jit(solution)/shard_map/ppermute | solution.py:336
  13.9 5.7 %collective-permute-start.4 = (bf16[10,8,128]{2,1,0:T(8,128)(2,1)S(1)}, bf16[10,8,128]{2,1,0:T(8,128)(2,1)S(1)}, u32[]{:S(2)}, u32[]{:S(2)}) collective-permute-start(bf16[10,8,128]{2,1,0:T(8,128)(2,1)S(1)} %get-tuple-element.35), channel_id=1, source_target_pairs={{0,6},{1,7},{2,4},{3,5},{4,2},{5,3},{6,0},{7,1},{8,14},{9,15},{10,... | collective-permute-start | bytes 61448 | tf_op jit(solution)/shard_map/ppermute | solution.py:377
  17.6 4.7 %collective-permute-start.5 = (bf16[10,8,128]{2,1,0:T(8,128)(2,1)S(1)}, bf16[10,8,128]{2,1,0:T(8,128)(2,1)S(1)}, u32[]{:S(2)}, u32[]{:S(2)}) collective-permute-start(bf16[10,8,128]{2,1,0:T(8,128)(2,1)S(1)} %get-tuple-element.36), channel_id=1, source_target_pairs={{0,4},{1,5},{2,6},{3,7},{4,0},{5,1},{6,2},{7,3},{8,12},{9,13},{10,... | collective-permute-start | bytes 61448 | tf_op jit(solution)/shard_map/ppermute | solution.py:377
  17.6 4.7 %collective-permute-start.6 = (bf16[10,8,128]{2,1,0:T(8,128)(2,1)S(1)}, bf16[10,8,128]{2,1,0:T(8,128)(2,1)S(1)}, u32[]{:S(2)}, u32[]{:S(2)}) collective-permute-start(bf16[10,8,128]{2,1,0:T(8,128)(2,1)S(1)} %get-tuple-element.37), channel_id=1, source_target_pairs={{0,2},{1,3},{2,0},{3,1},{4,6},{5,7},{6,4},{7,5},{8,10},{9,11},{10,... | collective-permute-start | bytes 61448 | tf_op jit(solution)/shard_map/ppermute | solution.py:377

commit v13 on v12

--- a/solution.py
+++ b/solution.py
@@ -338,24 +338,21 @@
     on_chip = (on_chip_ids, point, windows)
     count = tiles // blk
 
-    def look_up(begin, end, earlier):
+    def look_up(begin, end, on_chip):
         share = (end - begin) * points // count
         return pl.pallas_call(
             functools.partial(fluctuation_kernel, begin=begin, end=end),
             out_shape=jax.ShapeDtypeStruct((COUNT, points), BF16),
-            in_specs=[vmem] * 3 + [hbm] * len(earlier),
+            in_specs=[vmem] * 3,
             out_specs=hbm,
             scratch_shapes=[pltpu.VMEM((COUNT, share), BF16), pltpu.SemaphoreType.DMA((end - begin,))],
-            input_output_aliases={3: 0} if earlier else {},
             compiler_params=params,
             cost_estimate=pl.CostEstimate(
                 flops=64 * share * ROWS, bytes_accessed=6 * share * ROWS, transcendentals=0
             ),
             name="fluctuation",
-        )(*on_chip, *earlier)
-
-    fluctuation = look_up(0, count // 2, [])
-    held, fluctuation = lax.optimization_barrier((held, fluctuation))
+        )(*on_chip)
+
     sent = pl.pallas_call(
         functools.partial(route_kernel, groups=groups),
         out_shape=[jax.ShapeDtypeStruct((per_device + CORES, 8, AVG), BF16)] * chips,
@@ -365,8 +362,8 @@
         compiler_params=params,
         name="route",
     )(blocks, *held)
-    sent, fluctuation = lax.optimization_barrier((sent, fluctuation))
-    fluctuation = look_up(count // 2, count, [fluctuation])
+    on_chip, sent = lax.optimization_barrier((on_chip, sent))
+    fluctuation = look_up(0, count, on_chip)
     got = [sent[0]]
     for offset in reversed(range(1, chips)):
         moves = [

time: 23.6 us -> 23.6 us (level)
  Pallas kernels: 7.33 us -> 6.45 us
  waiting for transfers between devices: 6.01 us -> 6.89 us
    ppermute x3, waiting for transfers between devices: 2.55 us -> 3.83 us  [local(): held.append(lax.ppermute(pair, 'grp', moves))]
    pallas_call x2 -> x1, Pallas kernels: 2.54 us -> 1.66 us  [look_up(): pl.pallas_call(functools.partial(fluctuation_kernel, begin=begin, end=end...]
    ppermute x3, waiting for transfers between devices: 2.62 us -> 2.22 us  [local(): got.insert(1, lax.ppermute(sent[offset], 'slab', moves))]
  transfers between devices with their start and end apart: 7 -> 7, of which waited for: 4 -> 5; matrix products, arithmetic and copies ran while one was open for 0% -> 0% of each run, Pallas kernels for 11% -> 7%
where the time goes in v13:
time: 23.6 us; the launch traced here: 23.4 us
  starting transfers between devices  9.42 us (40%)
  waiting for transfers between devices  6.89 us (29%)
  Pallas kernels  6.45 us (27%)
  between operations  0.67 us (3%)
    ppermute x3, starting transfers between devices, local(): got.insert(1, lax.ppermute(sent[offset], 'slab', moves))  4.45 us
    ppermute x3, starting transfers between devices, local(): held.append(lax.ppermute(pair, 'grp', moves))  4.41 us
    ppermute x3, waiting for transfers between devices, local(): held.append(lax.ppermute(pair, 'grp', moves))  3.83 us
    pallas_call x1, Pallas kernels, local(): pl.pallas_call(functools.partial(sum_kernel, cuts=cuts, blk=blk), out_sha...  3.5 us
    ppermute x3, waiting for transfers between devices, local(): got.insert(1, lax.ppermute(sent[offset], 'slab', moves))  2.22 us
    pallas_call x1, Pallas kernels, look_up(): pl.pallas_call(functools.partial(fluctuation_kernel, begin=begin, end=end...  1.66 us
    pallas_call x1, Pallas kernels, local(): pl.pallas_call(functools.partial(place_kernel, groups=groups, chips=chips...  1.17 us
    ppermute x1, waiting for transfers between devices, local(): other = lax.ppermute(table, 'slab', [(s, s ^ 1) for s in range(slabs)])  0.84 us
  transfers between devices with their start and end apart: 7, of which 5 were waited for; matrix products, arithmetic and copies ran while one was open for 0% of the time, Pallas kernels for 7%

profile of v13, /device:TPU:0, one launch (start us, length us, event | category | flops | bytes accessed | tf_op | source)
XLA Modules:
  0.0 23.4 jit_solution(14412278146436905941)
XLA Ops:
  0.6 3.5 %sums.1 = (bf16[9,8,128]{2,1,0:T(8,128)(2,1)S(1)}, f32[8,16,128]{2,1,0:T(8,128)S(1)}, f32[16,65536]{1,0:T(8,128)S(1)}, s32[256]{0:T(256)S(4)}, s32[512,128]{1,0:T(8,128)S(1)}) custom-call(s32[512,128]{1,0:T(8,128)} %bitcast.7, f32[2048,128]{1,0:T(8,128)} %bitcast.6, f32[9,65536]{1,0:T(8,128)} %s_hbm.1, s32[256]{0:T(256)} %blocks_hbm.1), custom_call_target="tpu_custom_call" | custom-call | flops 67108864 | bytes 4194304 | tf_op jit(solution)/shard_map/sums/pallas_call | solution.py:298
  4.1 0.6 %collective-permute-start = (bf16[9,8,128]{2,1,0:T(8,128)(2,1)S(1)}, bf16[9,8,128]{2,1,0:T(8,128)(2,1)S(1)}, u32[]{:S(2)}, u32[]{:S(2)}) collective-permute-start(bf16[9,8,128]{2,1,0:T(8,128)(2,1)S(1)} %get-tuple-element.22.mine_ref), channel_id=1, source_target_pairs={{0,1},{1,0},{2,3},{3,2},{4,5},{5,4},{6,7},{7,6},{8,9},{9,8},{10,11... | collective-permute-start | bytes 55304 | tf_op jit(solution)/shard_map/ppermute | solution.py:324
  4.7 0.8 %collective-permute-done.other_ref = bf16[9,8,128]{2,1,0:T(8,128)(2,1)S(1)} collective-permute-done((bf16[9,8,128]{2,1,0:T(8,128)(2,1)S(1)}, bf16[9,8,128]{2,1,0:T(8,128)(2,1)S(1)}, u32[]{:S(2)}, u32[]{:S(2)}) %collective-permute-start) | collective-permute-done | bytes 18464 | tf_op jit(solution)/shard_map/ppermute | solution.py:324
  5.5 3.8 %collective-permute-start.3 = (bf16[2,9,8,128]{3,2,1,0:T(8,128)(2,1)S(1)}, bf16[2,9,8,128]{3,2,1,0:T(8,128)(2,1)S(1)}, u32[]{:S(2)}, u32[]{:S(2)}) collective-permute-start(bf16[2,9,8,128]{3,2,1,0:T(8,128)(2,1)S(1)} %pair.1.refs_0_), channel_id=1, source_target_pairs={{0,24},{8,16},{16,8},{24,0},{1,25},{9,17},{17,9},{25,1},{2,26},{10... | collective-permute-start | bytes 110600 | tf_op jit(solution)/shard_map/ppermute | solution.py:336
  9.3 0.5 %collective-permute-start.2 = (bf16[2,9,8,128]{3,2,1,0:T(8,128)(2,1)S(1)}, bf16[2,9,8,128]{3,2,1,0:T(8,128)(2,1)S(1)}, u32[]{:S(2)}, u32[]{:S(2)}) collective-permute-start(bf16[2,9,8,128]{3,2,1,0:T(8,128)(2,1)S(1)} %pair.1.refs_0_), channel_id=1, source_target_pairs={{0,16},{8,24},{16,0},{24,8},{1,17},{9,25},{17,1},{25,9},{2,18},{10... | collective-permute-start | bytes 110600 | tf_op jit(solution)/shard_map/ppermute | solution.py:336
  9.8 0.1 collective-permute-start.1
  10.0 1.3 %collective-permute-done.3.refs_3_ = bf16[2,9,8,128]{3,2,1,0:T(8,128)(2,1)S(1)} collective-permute-done((bf16[2,9,8,128]{3,2,1,0:T(8,128)(2,1)S(1)}, bf16[2,9,8,128]{3,2,1,0:T(8,128)(2,1)S(1)}, u32[]{:S(2)}, u32[]{:S(2)}) %collective-permute-start.3) | collective-permute-done | bytes 36896 | tf_op jit(solution)/shard_map/ppermute | solution.py:336
  11.3 2.0 %collective-permute-done.2.refs_2_ = bf16[2,9,8,128]{3,2,1,0:T(8,128)(2,1)S(1)} collective-permute-done((bf16[2,9,8,128]{3,2,1,0:T(8,128)(2,1)S(1)}, bf16[2,9,8,128]{3,2,1,0:T(8,128)(2,1)S(1)}, u32[]{:S(2)}, u32[]{:S(2)}) %collective-permute-start.2) | collective-permute-done | bytes 36896 | tf_op jit(solution)/shard_map/ppermute | solution.py:336
  13.3 0.5 %collective-permute-done.1.refs_1_ = bf16[2,9,8,128]{3,2,1,0:T(8,128)(2,1)S(1)} collective-permute-done((bf16[2,9,8,128]{3,2,1,0:T(8,128)(2,1)S(1)}, bf16[2,9,8,128]{3,2,1,0:T(8,128)(2,1)S(1)}, u32[]{:S(2)}, u32[]{:S(2)}) %collective-permute-start.1) | collective-permute-done | bytes 36896 | tf_op jit(solution)/shard_map/ppermute | solution.py:336
  13.8 0.1 route.1
  13.9 3.7 %collective-permute-start.4 = (bf16[10,8,128]{2,1,0:T(8,128)(2,1)S(1)}, bf16[10,8,128]{2,1,0:T(8,128)(2,1)S(1)}, u32[]{:S(2)}, u32[]{:S(2)}) collective-permute-start(bf16[10,8,128]{2,1,0:T(8,128)(2,1)S(1)} %get-tuple-element.27), channel_id=1, source_target_pairs={{0,6},{1,7},{2,4},{3,5},{4,2},{5,3},{6,0},{7,1},{8,14},{9,15},{10,... | collective-permute-start | bytes 61448 | tf_op jit(solution)/shard_map/ppermute | solution.py:374
  17.6 0.0 collective-permute-start.5
  17.6 0.8 %collective-permute-start.6 = (bf16[10,8,128]{2,1,0:T(8,128)(2,1)S(1)}, bf16[10,8,128]{2,1,0:T(8,128)(2,1)S(1)}, u32[]{:S(2)}, u32[]{:S(2)}) collective-permute-start(bf16[10,8,128]{2,1,0:T(8,128)(2,1)S(1)} %get-tuple-element.29), channel_id=1, source_target_pairs={{0,2},{1,3},{2,0},{3,1},{4,6},{5,7},{6,4},{7,5},{8,10},{9,11},{10,... | collective-permute-start | bytes 61448 | tf_op jit(solution)/shard_map/ppermute | solution.py:374
  18.4 1.7 %fluctuation.1.refs_7_ = bf16[13,65536]{1,0:T(8,128)(2,1)} custom-call(s32[512,128]{1,0:T(8,128)S(1)} %get-tuple-element.31.ids_ref.refs_4_, f32[16,65536]{1,0:T(8,128)S(1)} %get-tuple-element.32.point_ref.refs_5_, f32[8,16,128]{2,1,0:T(8,128)S(1)} %get-tuple-element.33.window_ref.refs_6_), custom_call_target="tpu_custom_call" | custom-call | flops 67108864 | bytes 6291456 | tf_op jit(solution)/shard_map/fluctuation/pallas_call | solution.py:343
  20.0 0.0 collective-permute-done.4.refs_0_
  20.0 2.2 %collective-permute-done.5.refs_1_ = bf16[10,8,128]{2,1,0:T(8,128)(2,1)S(1)} collective-permute-done((bf16[10,8,128]{2,1,0:T(8,128)(2,1)S(1)}, bf16[10,8,128]{2,1,0:T(8,128)(2,1)S(1)}, u32[]{:S(2)}, u32[]{:S(2)}) %collective-permute-start.5) | collective-permute-done | bytes 20512 | tf_op jit(solution)/shard_map/ppermute | solution.py:374
  22.3 0.0 collective-permute-done.6.refs_2_
  22.3 1.2 %place.1 = (f32[13,512]{1,0:T(8,128)}, bf16[13,65536]{1,0:T(8,128)(2,1)}) custom-call(s32[256]{0:T(256)S(4)} %get-tuple-element.18.blocks_ref, bf16[10,8,128]{2,1,0:T(8,128)(2,1)S(1)} %collective-permute-done.4.refs_0_, bf16[10,8,128]{2,1,0:T(8,128)(2,1)S(1)} %collective-permute-done.5.refs_1_, ...), custom_call_target="tpu_custom_call", output_to_operand_aliasing={{1}: (8, {})} | custom-call | tf_op jit(solution)/shard_map/place/pallas_call | solution.py:375
  (1 shorter events, 0.0 us)
Async XLA Ops:
  4.1 1.4 %collective-permute-start = (bf16[9,8,128]{2,1,0:T(8,128)(2,1)S(1)}, bf16[9,8,128]{2,1,0:T(8,128)(2,1)S(1)}, u32[]{:S(2)}, u32[]{:S(2)}) collective-permute-start(bf16[9,8,128]{2,1,0:T(8,128)(2,1)S(1)} %get-tuple-element.22.mine_ref), channel_id=1, source_target_pairs={{0,1},{1,0},{2,3},{3,2},{4,5},{5,4},{6,7},{7,6},{8,9},{9,8},{10,11... | collective-permute-start | bytes 55304 | tf_op jit(solution)/shard_map/ppermute | solution.py:324
  5.5 5.7 %collective-permute-start.3 = (bf16[2,9,8,128]{3,2,1,0:T(8,128)(2,1)S(1)}, bf16[2,9,8,128]{3,2,1,0:T(8,128)(2,1)S(1)}, u32[]{:S(2)}, u32[]{:S(2)}) collective-permute-start(bf16[2,9,8,128]{3,2,1,0:T(8,128)(2,1)S(1)} %pair.1.refs_0_), channel_id=1, source_target_pairs={{0,24},{8,16},{16,8},{24,0},{1,25},{9,17},{17,9},{25,1},{2,26},{10... | collective-permute-start | bytes 110600 | tf_op jit(solution)/shard_map/ppermute | solution.py:336
  9.3 4.0 %collective-permute-start.2 = (bf16[2,9,8,128]{3,2,1,0:T(8,128)(2,1)S(1)}, bf16[2,9,8,128]{3,2,1,0:T(8,128)(2,1)S(1)}, u32[]{:S(2)}, u32[]{:S(2)}) collective-permute-start(bf16[2,9,8,128]{3,2,1,0:T(8,128)(2,1)S(1)} %pair.1.refs_0_), channel_id=1, source_target_pairs={{0,16},{8,24},{16,0},{24,8},{1,17},{9,25},{17,1},{25,9},{2,18},{10... | collective-permute-start | bytes 110600 | tf_op jit(solution)/shard_map/ppermute | solution.py:336
  9.8 4.0 %collective-permute-start.1 = (bf16[2,9,8,128]{3,2,1,0:T(8,128)(2,1)S(1)}, bf16[2,9,8,128]{3,2,1,0:T(8,128)(2,1)S(1)}, u32[]{:S(2)}, u32[]{:S(2)}) collective-permute-start(bf16[2,9,8,128]{3,2,1,0:T(8,128)(2,1)S(1)} %pair.1.refs_0_), channel_id=1, source_target_pairs={{0,8},{8,0},{16,24},{24,16},{1,9},{9,1},{17,25},{25,17},{2,10},{10... | collective-permute-start | bytes 110600 | tf_op jit(solution)/shard_map/ppermute | solution.py:336
  13.9 6.1 %collective-permute-start.4 = (bf16[10,8,128]{2,1,0:T(8,128)(2,1)S(1)}, bf16[10,8,128]{2,1,0:T(8,128)(2,1)S(1)}, u32[]{:S(2)}, u32[]{:S(2)}) collective-permute-start(bf16[10,8,128]{2,1,0:T(8,128)(2,1)S(1)} %get-tuple-element.27), channel_id=1, source_target_pairs={{0,6},{1,7},{2,4},{3,5},{4,2},{5,3},{6,0},{7,1},{8,14},{9,15},{10,... | collective-permute-start | bytes 61448 | tf_op jit(solution)/shard_map/ppermute | solution.py:374
  17.6 4.7 %collective-permute-start.5 = (bf16[10,8,128]{2,1,0:T(8,128)(2,1)S(1)}, bf16[10,8,128]{2,1,0:T(8,128)(2,1)S(1)}, u32[]{:S(2)}, u32[]{:S(2)}) collective-permute-start(bf16[10,8,128]{2,1,0:T(8,128)(2,1)S(1)} %get-tuple-element.28), channel_id=1, source_target_pairs={{0,4},{1,5},{2,6},{3,7},{4,0},{5,1},{6,2},{7,3},{8,12},{9,13},{10,... | collective-permute-start | bytes 61448 | tf_op jit(solution)/shard_map/ppermute | solution.py:374
  17.6 4.7 %collective-permute-start.6 = (bf16[10,8,128]{2,1,0:T(8,128)(2,1)S(1)}, bf16[10,8,128]{2,1,0:T(8,128)(2,1)S(1)}, u32[]{:S(2)}, u32[]{:S(2)}) collective-permute-start(bf16[10,8,128]{2,1,0:T(8,128)(2,1)S(1)} %get-tuple-element.29), channel_id=1, source_target_pairs={{0,2},{1,3},{2,0},{3,1},{4,6},{5,7},{6,4},{7,5},{8,10},{9,11},{10,... | collective-permute-start | bytes 61448 | tf_op jit(solution)/shard_map/ppermute | solution.py:374

commit v14 on v11

--- a/solution.py
+++ b/solution.py
@@ -193,6 +193,10 @@
             out_ref[slot] = held_ref[div_rem(owner_slab, CORES)[1], owner_group, index]
 
 
+def transfer_order(chips):
+    return [*range(2, chips), *range(1, min(chips, 2)), 0]
+
+
 def place_kernel(blocks_ref, *refs, groups, chips, blk):
     (*got_refs, ids_ref, point_ref, window_ref, _, table_hbm, fluctuation_hbm, held_ref, ends_ref,
      edge_ref, table_ref, sems) = refs
@@ -207,7 +211,7 @@
     lane = lax.broadcasted_iota(jnp.int32, (8, AVG), 1)
     half = lane < blk
 
-    for offset, ref in enumerate(reversed(got_refs)):
+    for offset, ref in zip(transfer_order(chips), got_refs):
         owner_chip = source(chip, offset, chips)
         held_ref[owner_chip] = ref[...]
         for core in range(CORES):
@@ -394,7 +398,7 @@
         input_output_aliases={chips + 4: 1},
         compiler_params=params,
         name="place",
-    )(blocks, *reversed(got), *on_chip, fluctuation)
+    )(blocks, *(got[offset] for offset in transfer_order(chips)), *on_chip, fluctuation)
     return (grain_table, fluctuation)
 
 

time: 23.5 us -> 23.4 us (level)
  no operation moved by 1% of the time
where the time goes in v14:
time: 23.4 us; the launch traced here: 23.3 us
  starting transfers between devices  8.93 us (38%)
  Pallas kernels  7.33 us (31%)
  waiting for transfers between devices  6.31 us (27%)
  between operations  0.69 us (3%)
    ppermute x3, starting transfers between devices, local(): held.append(lax.ppermute(table, 'grp', moves))  4.63 us
    ppermute x3, starting transfers between devices, local(): got.insert(1, lax.ppermute(sent[offset], 'slab', moves))  4.23 us
    pallas_call x1, Pallas kernels, local(): pl.pallas_call(functools.partial(sum_kernel, cuts=cuts, blk=blk), out_sha...  3.5 us
    ppermute x3, waiting for transfers between devices, local(): got.insert(1, lax.ppermute(sent[offset], 'slab', moves))  2.72 us
    pallas_call x2, Pallas kernels, look_up(): pl.pallas_call(functools.partial(fluctuation_kernel, begin=begin, end=end...  2.53 us
    ppermute x3, waiting for transfers between devices, local(): held.append(lax.ppermute(table, 'grp', moves))  2.34 us
    ppermute x1, waiting for transfers between devices, local(): other = lax.ppermute(mine, 'slab', [(s, s ^ 1) for s in range(slabs)])  1.25 us
    pallas_call x1, Pallas kernels, local(): pl.pallas_call(functools.partial(place_kernel, groups=groups, chips=chips...  1.17 us
  transfers between devices with their start and end apart: 7, of which 4 were waited for; matrix products, arithmetic and copies ran while one was open for 0% of the time, Pallas kernels for 11%

profile of v14, /device:TPU:0, one launch (start us, length us, event | category | flops | bytes accessed | tf_op | source)
XLA Modules:
  0.0 23.3 jit_solution(13115013836542013119)
XLA Ops:
  0.6 3.5 %sums.1 = (bf16[9,8,128]{2,1,0:T(8,128)(2,1)S(1)}, f32[8,16,128]{2,1,0:T(8,128)S(1)}, f32[16,65536]{1,0:T(8,128)S(1)}, s32[256]{0:T(256)S(4)}, s32[512,128]{1,0:T(8,128)S(1)}) custom-call(s32[512,128]{1,0:T(8,128)} %bitcast.7, f32[2048,128]{1,0:T(8,128)} %bitcast.6, f32[9,65536]{1,0:T(8,128)} %s_hbm.1, s32[256]{0:T(256)} %blocks_hbm.1), custom_call_target="tpu_custom_call" | custom-call | flops 67108864 | bytes 4194304 | tf_op jit(solution)/shard_map/sums/pallas_call | solution.py:303
  4.1 4.0 %collective-permute-start.2 = (bf16[9,8,128]{2,1,0:T(8,128)(2,1)S(1)}, bf16[9,8,128]{2,1,0:T(8,128)(2,1)S(1)}, u32[]{:S(2)}, u32[]{:S(2)}) collective-permute-start(bf16[9,8,128]{2,1,0:T(8,128)(2,1)S(1)} %get-tuple-element.26.refs_0_), channel_id=1, source_target_pairs={{0,24},{8,16},{16,8},{24,0},{1,25},{9,17},{17,9},{25,1},{2,26},{10... | collective-permute-start | bytes 55304 | tf_op jit(solution)/shard_map/ppermute | solution.py:332
  8.1 0.5 %collective-permute-start.1 = (bf16[9,8,128]{2,1,0:T(8,128)(2,1)S(1)}, bf16[9,8,128]{2,1,0:T(8,128)(2,1)S(1)}, u32[]{:S(2)}, u32[]{:S(2)}) collective-permute-start(bf16[9,8,128]{2,1,0:T(8,128)(2,1)S(1)} %get-tuple-element.26.refs_0_), channel_id=1, source_target_pairs={{0,16},{8,24},{16,0},{24,8},{1,17},{9,25},{17,1},{25,9},{2,18},{10... | collective-permute-start | bytes 55304 | tf_op jit(solution)/shard_map/ppermute | solution.py:332
  8.6 0.1 collective-permute-start
  8.8 1.3 %fluctuation.2.refs_0_ = bf16[13,65536]{1,0:T(8,128)(2,1)} custom-call(s32[512,128]{1,0:T(8,128)S(1)} %get-tuple-element.23.ids_ref.refs_4_, f32[16,65536]{1,0:T(8,128)S(1)} %get-tuple-element.24.point_ref.refs_5_, f32[8,16,128]{2,1,0:T(8,128)S(1)} %get-tuple-element.25.window_ref.refs_6_), custom_call_target="tpu_custom_call" | custom-call | flops 33554432 | bytes 3145728 | tf_op jit(solution)/shard_map/fluctuation/pallas_call | solution.py:339
  10.0 0.0 collective-permute-done.2.refs_3_
  10.1 1.8 %collective-permute-done.1.refs_2_ = bf16[9,8,128]{2,1,0:T(8,128)(2,1)S(1)} collective-permute-done((bf16[9,8,128]{2,1,0:T(8,128)(2,1)S(1)}, bf16[9,8,128]{2,1,0:T(8,128)(2,1)S(1)}, u32[]{:S(2)}, u32[]{:S(2)}) %collective-permute-start.1) | collective-permute-done | bytes 18464 | tf_op jit(solution)/shard_map/ppermute | solution.py:332
  11.9 0.5 %collective-permute-done.refs_1_ = bf16[9,8,128]{2,1,0:T(8,128)(2,1)S(1)} collective-permute-done((bf16[9,8,128]{2,1,0:T(8,128)(2,1)S(1)}, bf16[9,8,128]{2,1,0:T(8,128)(2,1)S(1)}, u32[]{:S(2)}, u32[]{:S(2)}) %collective-permute-start) | collective-permute-done | bytes 18464 | tf_op jit(solution)/shard_map/ppermute | solution.py:332
  12.4 0.1 collective-permute-start.3
  12.5 1.3 %collective-permute-done.3.other_ref = bf16[4,9,8,128]{3,2,1,0:T(8,128)(2,1)S(1)} collective-permute-done((bf16[4,9,8,128]{3,2,1,0:T(8,128)(2,1)S(1)}, bf16[4,9,8,128]{3,2,1,0:T(8,128)(2,1)S(1)}, u32[]{:S(2)}, u32[]{:S(2)}) %collective-permute-start.3) | collective-permute-done | bytes 73760 | tf_op jit(solution)/shard_map/ppermute | solution.py:363
  13.7 0.1 route.1
  13.9 2.7 %collective-permute-start.4 = (bf16[10,8,128]{2,1,0:T(8,128)(2,1)S(1)}, bf16[10,8,128]{2,1,0:T(8,128)(2,1)S(1)}, u32[]{:S(2)}, u32[]{:S(2)}) collective-permute-start(bf16[10,8,128]{2,1,0:T(8,128)(2,1)S(1)} %get-tuple-element.35), channel_id=1, source_target_pairs={{0,4},{1,5},{2,6},{3,7},{4,0},{5,1},{6,2},{7,3},{8,12},{9,13},{10,... | collective-permute-start | bytes 61448 | tf_op jit(solution)/shard_map/ppermute | solution.py:382
  16.5 1.3 %collective-permute-start.5 = (bf16[10,8,128]{2,1,0:T(8,128)(2,1)S(1)}, bf16[10,8,128]{2,1,0:T(8,128)(2,1)S(1)}, u32[]{:S(2)}, u32[]{:S(2)}) collective-permute-start(bf16[10,8,128]{2,1,0:T(8,128)(2,1)S(1)} %get-tuple-element.36), channel_id=1, source_target_pairs={{0,6},{1,7},{2,4},{3,5},{4,2},{5,3},{6,0},{7,1},{8,14},{9,15},{10,... | collective-permute-start | bytes 61448 | tf_op jit(solution)/shard_map/ppermute | solution.py:382
  17.9 0.2 collective-permute-start.6
  18.1 1.3 %fluctuation.3.refs_7_ = bf16[13,65536]{1,0:T(8,128)(2,1)} custom-call(s32[512,128]{1,0:T(8,128)S(1)} %get-tuple-element.23.ids_ref.refs_4_, f32[16,65536]{1,0:T(8,128)S(1)} %get-tuple-element.24.point_ref.refs_5_, f32[8,16,128]{2,1,0:T(8,128)S(1)} %get-tuple-element.25.window_ref.refs_6_, ...), custom_call_target="tpu_custom_call", output_to_operand_aliasing={{}: (3, {})} | custom-call | flops 33554432 | bytes 3145728 | tf_op jit(solution)/shard_map/fluctuation/pallas_call | solution.py:339
  19.4 0.0 collective-permute-done.4.refs_0_
  19.4 2.7 %collective-permute-done.5.refs_1_ = bf16[10,8,128]{2,1,0:T(8,128)(2,1)S(1)} collective-permute-done((bf16[10,8,128]{2,1,0:T(8,128)(2,1)S(1)}, bf16[10,8,128]{2,1,0:T(8,128)(2,1)S(1)}, u32[]{:S(2)}, u32[]{:S(2)}) %collective-permute-start.5) | collective-permute-done | bytes 20512 | tf_op jit(solution)/shard_map/ppermute | solution.py:382
  22.1 0.0 collective-permute-done.6.refs_2_
  22.1 1.2 %place.1 = (f32[13,512]{1,0:T(8,128)}, bf16[13,65536]{1,0:T(8,128)(2,1)}) custom-call(s32[256]{0:T(256)S(4)} %get-tuple-element.21.blocks_ref, bf16[10,8,128]{2,1,0:T(8,128)(2,1)S(1)} %collective-permute-done.4.refs_0_, bf16[10,8,128]{2,1,0:T(8,128)(2,1)S(1)} %collective-permute-done.5.refs_1_, ...), custom_call_target="tpu_custom_call", output_to_operand_aliasing={{1}: (8, {})} | custom-call | tf_op jit(solution)/shard_map/place/pallas_call | solution.py:383
  (1 shorter events, 0.0 us)
Async XLA Ops:
  4.1 5.9 %collective-permute-start.2 = (bf16[9,8,128]{2,1,0:T(8,128)(2,1)S(1)}, bf16[9,8,128]{2,1,0:T(8,128)(2,1)S(1)}, u32[]{:S(2)}, u32[]{:S(2)}) collective-permute-start(bf16[9,8,128]{2,1,0:T(8,128)(2,1)S(1)} %get-tuple-element.26.refs_0_), channel_id=1, source_target_pairs={{0,24},{8,16},{16,8},{24,0},{1,25},{9,17},{17,9},{25,1},{2,26},{10... | collective-permute-start | bytes 55304 | tf_op jit(solution)/shard_map/ppermute | solution.py:332
  8.1 3.8 %collective-permute-start.1 = (bf16[9,8,128]{2,1,0:T(8,128)(2,1)S(1)}, bf16[9,8,128]{2,1,0:T(8,128)(2,1)S(1)}, u32[]{:S(2)}, u32[]{:S(2)}) collective-permute-start(bf16[9,8,128]{2,1,0:T(8,128)(2,1)S(1)} %get-tuple-element.26.refs_0_), channel_id=1, source_target_pairs={{0,16},{8,24},{16,0},{24,8},{1,17},{9,25},{17,1},{25,9},{2,18},{10... | collective-permute-start | bytes 55304 | tf_op jit(solution)/shard_map/ppermute | solution.py:332
  8.6 3.8 %collective-permute-start = (bf16[9,8,128]{2,1,0:T(8,128)(2,1)S(1)}, bf16[9,8,128]{2,1,0:T(8,128)(2,1)S(1)}, u32[]{:S(2)}, u32[]{:S(2)}) collective-permute-start(bf16[9,8,128]{2,1,0:T(8,128)(2,1)S(1)} %get-tuple-element.26.refs_0_), channel_id=1, source_target_pairs={{0,8},{8,0},{16,24},{24,16},{1,9},{9,1},{17,25},{25,17},{2,10},{10... | collective-permute-start | bytes 55304 | tf_op jit(solution)/shard_map/ppermute | solution.py:332
  12.4 1.3 %collective-permute-start.3 = (bf16[4,9,8,128]{3,2,1,0:T(8,128)(2,1)S(1)}, bf16[4,9,8,128]{3,2,1,0:T(8,128)(2,1)S(1)}, u32[]{:S(2)}, u32[]{:S(2)}) collective-permute-start(bf16[4,9,8,128]{3,2,1,0:T(8,128)(2,1)S(1)} %stack.1.mine_ref), channel_id=1, source_target_pairs={{0,1},{1,0},{2,3},{3,2},{4,5},{5,4},{6,7},{7,6},{8,9},{9,8},{10,11... | collective-permute-start | bytes 221192 | tf_op jit(solution)/shard_map/ppermute | solution.py:363
  13.9 5.5 %collective-permute-start.4 = (bf16[10,8,128]{2,1,0:T(8,128)(2,1)S(1)}, bf16[10,8,128]{2,1,0:T(8,128)(2,1)S(1)}, u32[]{:S(2)}, u32[]{:S(2)}) collective-permute-start(bf16[10,8,128]{2,1,0:T(8,128)(2,1)S(1)} %get-tuple-element.35), channel_id=1, source_target_pairs={{0,4},{1,5},{2,6},{3,7},{4,0},{5,1},{6,2},{7,3},{8,12},{9,13},{10,... | collective-permute-start | bytes 61448 | tf_op jit(solution)/shard_map/ppermute | solution.py:382
  16.5 5.6 %collective-permute-start.5 = (bf16[10,8,128]{2,1,0:T(8,128)(2,1)S(1)}, bf16[10,8,128]{2,1,0:T(8,128)(2,1)S(1)}, u32[]{:S(2)}, u32[]{:S(2)}) collective-permute-start(bf16[10,8,128]{2,1,0:T(8,128)(2,1)S(1)} %get-tuple-element.36), channel_id=1, source_target_pairs={{0,6},{1,7},{2,4},{3,5},{4,2},{5,3},{6,0},{7,1},{8,14},{9,15},{10,... | collective-permute-start | bytes 61448 | tf_op jit(solution)/shard_map/ppermute | solution.py:382
  17.9 4.2 %collective-permute-start.6 = (bf16[10,8,128]{2,1,0:T(8,128)(2,1)S(1)}, bf16[10,8,128]{2,1,0:T(8,128)(2,1)S(1)}, u32[]{:S(2)}, u32[]{:S(2)}) collective-permute-start(bf16[10,8,128]{2,1,0:T(8,128)(2,1)S(1)} %get-tuple-element.37), channel_id=1, source_target_pairs={{0,2},{1,3},{2,0},{3,1},{4,6},{5,7},{6,4},{7,5},{8,10},{9,11},{10,... | collective-permute-start | bytes 61448 | tf_op jit(solution)/shard_map/ppermute | solution.py:382
